TPU v7x, 32 devices: a whole 2x2x4 slice. The times are simulated.
32 devices in a mesh: scen: 2 (over x), node: 16 (over z, y, core).
Axes of the slice: x: 2, y: 2, z: 4, core: 2. Of those that a mesh axis runs over, the one named last changes fastest.
Arguments:
- hidden_state: bfloat16 [65536, 128], P(('scen', 'node')), parts along dimension 0, may hold values from -6 to 6
- conv_cache: bfloat16 [3, 65536, 128], P(None, ('scen', 'node')), parts along dimension 1, may hold values from -6 to 6
- conv_weight: bfloat16 [3, 256, 512], replicated, may hold values from -0.375 to 0.375
- conv_bias: float32 [3, 512], replicated, may hold values from -3 to 3
- mix_weight: bfloat16 [3, 768, 128], replicated, may hold values from -0.21875 to 0.21875
- skip_weight: bfloat16 [3, 256, 256], replicated, may hold values from -0.375 to 0.375
- block_values: bfloat16 [752, 128, 128], P('node'), may hold values from -0.3125 to 0.3125
- block_target: int32 [752], P('node'), may hold values from 0 to 15, as said below
- block_owner: int32 [752], P('node'), may hold values from 0 to 15, as said below
- block_slot: int32 [752], P('node'), may hold values from 0 to 15, as said below
- send_tiles: int32 [16, 16, 2], P('node'), may hold values from 0 to 15
- send_count: int32 [16, 16], P('node'), may hold values from 0 to 2, as said below
Outputs:
- next_state: bfloat16 [65536, 128], P(('scen', 'node')), parts along dimension 0
- skip_total: bfloat16 [65536, 256], P(('scen', 'node')), parts along dimension 0
There are 2 independent parts, one for each index of `scen`. A program takes and returns all parts, laid end to end along the dimension named above; an argument that names none is the same for every part. Nothing has to cross between parts.
Inputs may be any that keep to these rules, and one draw needn't show every extreme that they name: `block_target`: each device's blocks target its own tiles; every tile has one block whose source is itself and one whose source is another tile of the same device. `block_owner`: each device has 32 blocks owned by itself and 15 owned by other devices. `block_slot`: for a remote owner o, the slot is below send_count[o, device], and each such slot is used by exactly one block of the device. `send_count`: zero from a device to itself; the counts into one device sum to 15; some pair reaches 2 in every draw.
All inputs are finite; a program needn't handle non-finite values.
Results may differ from a plain program's by a relative error of at most 0.01.
Values may be sent and summed in bfloat16 or wider, within the bound.
No kernel may reach another device: no remote copies, remote signals or barrier semaphores. Data moves between devices by JAX's collectives and lax.ppermute only.
A program may use at most 128 MiB of HBM per device.

v0:
```python
import jax
import jax.numpy as jnp
from jax import lax
from jax.sharding import PartitionSpec as P

TILE = 128
CAP = 2
LAYERS = 3


def gating(preact, gate_width):
    return (jnp.tanh(preact[..., :gate_width]) * jax.nn.sigmoid(preact[..., gate_width:])).astype(
        jnp.bfloat16
    )


def local(
    hidden_state,
    conv_cache,
    conv_weight,
    conv_bias,
    mix_weight,
    skip_weight,
    block_values,
    block_target,
    block_owner,
    block_slot,
    send_tiles,
    send_count,
):
    row_count, res_width = hidden_state.shape
    gate_width = skip_weight.shape[1]
    tile_count = row_count // TILE
    position = lax.axis_index("node")
    peer_count = lax.axis_size("node")
    source = jnp.where(
        block_owner == position, block_slot, tile_count + block_owner * CAP + block_slot
    )
    routing = send_tiles[0]
    live_slots = send_count[0][:, None] > jnp.arange(CAP, dtype=jnp.int32)[None, :]

    def outbound(local_tiles):
        return jnp.where(
            live_slots[:, :, None, None], local_tiles[routing], jnp.zeros((), local_tiles.dtype)
        )

    def propagate(lookup):
        picked = lookup[source]
        blockwise = jnp.einsum(
            "bij,bjc->bic", block_values, picked, preferred_element_type=jnp.float32
        )
        summed = (
            jnp.zeros((tile_count, TILE, lookup.shape[2]), jnp.float32)
            .at[block_target]
            .add(blockwise)
        )
        return summed.astype(jnp.bfloat16)

    current = hidden_state
    skip_sum = jnp.zeros((row_count, skip_weight.shape[2]), jnp.float32)
    for layer_index in range(LAYERS):
        weight_past = conv_weight[layer_index, :res_width]
        weight_now = conv_weight[layer_index, res_width:]
        preact = jnp.dot(conv_cache[layer_index], weight_past, preferred_element_type=jnp.float32)
        preact = preact + jnp.dot(current, weight_now, preferred_element_type=jnp.float32)
        preact = preact + conv_bias[layer_index]
        gated_out = gating(preact, gate_width)
        local_gated = gated_out.reshape(tile_count, TILE, gate_width)
        far_gated = lax.all_to_all(
            outbound(local_gated), "node", split_axis=0, concat_axis=0, tiled=True
        )
        far_gated = far_gated.reshape(peer_count * CAP, TILE, gate_width)
        hop_one = propagate(jnp.concatenate([local_gated, far_gated], axis=0))
        far_first = lax.all_to_all(
            outbound(hop_one), "node", split_axis=0, concat_axis=0, tiled=True
        )
        far_first = far_first.reshape(peer_count * CAP, TILE, gate_width)
        hop_two = propagate(jnp.concatenate([hop_one, far_first], axis=0))
        mixing = mix_weight[layer_index]
        mixed = jnp.dot(gated_out, mixing[:gate_width], preferred_element_type=jnp.float32)
        mixed = mixed + jnp.dot(
            hop_one.reshape(row_count, gate_width),
            mixing[gate_width : 2 * gate_width],
            preferred_element_type=jnp.float32,
        )
        mixed = mixed + jnp.dot(
            hop_two.reshape(row_count, gate_width),
            mixing[2 * gate_width :],
            preferred_element_type=jnp.float32,
        )
        skip_sum = skip_sum + jnp.dot(
            gated_out, skip_weight[layer_index], preferred_element_type=jnp.float32
        )
        current = (current.astype(jnp.float32) + mixed).astype(jnp.bfloat16)
    return (current, skip_sum.astype(jnp.bfloat16))


def solution(mesh):
    placed = (
        P(("scen", "node"), None),
        P(None, ("scen", "node"), None),
        P(),
        P(),
        P(),
        P(),
        P("node", None, None),
        P("node"),
        P("node"),
        P("node"),
        P("node", None, None),
        P("node", None),
    )
    return jax.shard_map(
        local,
        mesh=mesh,
        in_specs=placed,
        out_specs=(P(("scen", "node"), None), P(("scen", "node"), None)),
        check_vma=False,
    )
```

profile of v0, /device:TPU:9, one launch (start us, length us, event | category | flops | bytes accessed | tf_op | source)
XLA Modules:
  0.0 593.8 jit_solution(4098193076599236234)
XLA Ops:
  11.2 6.7 %all-to-all-start = ((bf16[16,2,128,256]{3,2,1,0:T(8,128)(2,1)}), bf16[16,2,128,256]{3,2,1,0:T(8,128)(2,1)}, u32[]{:S(2)}, u32[]{:S(2)}) async-start(bf16[16,2,128,256]{3,2,1,0:T(8,128)(2,1)} %broadcast_select_fusion.5), calls=%async_computation | async-start | bytes 4194304 | tf_op jit(solution)/shard_map/all_to_all | solution.py:69
  18.0 46.0 %all-to-all-done = bf16[16,2,128,256]{3,2,1,0:T(8,128)(2,1)} async-done(((bf16[16,2,128,256]{3,2,1,0:T(8,128)(2,1)}), bf16[16,2,128,256]{3,2,1,0:T(8,128)(2,1)}, u32[]{:S(2)}, u32[]{:S(2)}) %all-to-all-start) | async-done | bytes 2097184 | tf_op jit(solution)/shard_map/all_to_all | solution.py:69
  67.5 4.4 gather_fusion.1
  71.9 5.5 convolution_bitcast_fusion.5
  77.4 6.5 %copy.23 = f32[47,128,256]{2,1,0:T(8,128)} copy(f32[47,128,256]{1,2,0:T(8,128)} %convolution_bitcast_fusion.5) | data formatting | bytes 12320768 | tf_op jit(solution)/shard_map/bij,bjc->bic/dot_general | solution.py:49
  85.5 14.1 %scatter_fusion = f32[16,128,256]{2,1,0:T(8,128)} fusion(f32[16,128,256]{2,1,0:T(8,128)} %broadcast.49.clone, s32[47]{0:T(128)S(1)} %compare_select_fusion.2, f32[47,128,256]{2,1,0:T(8,128)} %copy.23), kind=kCustom, calls=%fused_computation.12 | custom fusion | flops 1540096 | bytes 18481340 | tf_op jit(solution)/shard_map/scatter-add | solution.py:55
  108.7 6.6 %all-to-all-start.1 = ((bf16[16,2,128,256]{3,2,1,0:T(8,128)(2,1)}), bf16[16,2,128,256]{3,2,1,0:T(8,128)(2,1)}, u32[]{:S(2)}, u32[]{:S(2)}) async-start(bf16[16,2,128,256]{3,2,1,0:T(8,128)(2,1)} %broadcast_select_fusion.4), calls=%async_computation.1 | async-start | bytes 4194304 | tf_op jit(solution)/shard_map/all_to_all | solution.py:74
  122.5 38.8 %all-to-all-done.1 = bf16[16,2,128,256]{3,2,1,0:T(8,128)(2,1)} async-done(((bf16[16,2,128,256]{3,2,1,0:T(8,128)(2,1)}), bf16[16,2,128,256]{3,2,1,0:T(8,128)(2,1)}, u32[]{:S(2)}, u32[]{:S(2)}) %all-to-all-start.1) | async-done | bytes 2097184 | tf_op jit(solution)/shard_map/all_to_all | solution.py:74
  165.1 4.4 gather_fusion.3
  169.4 5.5 convolution_bitcast_fusion.4
  174.9 6.5 %copy.25 = f32[47,128,256]{2,1,0:T(8,128)} copy(f32[47,128,256]{1,2,0:T(8,128)} %convolution_bitcast_fusion.4) | data formatting | bytes 12320768 | tf_op jit(solution)/shard_map/bij,bjc->bic/dot_general | solution.py:49
  183.0 14.1 %scatter_fusion.1 = f32[16,128,256]{2,1,0:T(8,128)} fusion(f32[16,128,256]{2,1,0:T(8,128)} %broadcast.49.clone.1, s32[47]{0:T(128)S(1)} %compare_select_fusion.2, f32[47,128,256]{2,1,0:T(8,128)} %copy.25), kind=kCustom, calls=%fused_computation.13 | custom fusion | flops 1540096 | bytes 18481340 | tf_op jit(solution)/shard_map/scatter-add | solution.py:55
  209.4 54.4 %all_to_all.30 = bf16[16,2,128,256]{3,2,1,0:T(8,128)(2,1)S(1)} all-to-all(bf16[16,2,128,256]{3,2,1,0:T(8,128)(2,1)S(1)} %broadcast_select_fusion.3), channel_id=1, replica_groups=mesh['scen'=2,'node'=16] {'node'}, dimensions={0} | all-to-all | bytes 4194304 | tf_op jit(solution)/shard_map/all_to_all | solution.py:69
  265.7 4.4 gather_fusion.5
  270.1 5.5 convolution_bitcast_fusion.3
  275.6 6.5 %copy.27 = f32[47,128,256]{2,1,0:T(8,128)} copy(f32[47,128,256]{1,2,0:T(8,128)} %convolution_bitcast_fusion.3) | data formatting | bytes 12320768 | tf_op jit(solution)/shard_map/bij,bjc->bic/dot_general | solution.py:49
  283.7 14.1 %scatter_fusion.2 = f32[16,128,256]{2,1,0:T(8,128)} fusion(f32[16,128,256]{2,1,0:T(8,128)} %broadcast.49.clone.2, s32[47]{0:T(128)S(1)} %compare_select_fusion.2, f32[47,128,256]{2,1,0:T(8,128)} %copy.27), kind=kCustom, calls=%fused_computation.14 | custom fusion | flops 1540096 | bytes 18481340 | tf_op jit(solution)/shard_map/scatter-add | solution.py:55
  306.8 4.8 all-to-all-start.3
  319.1 38.7 %all-to-all-done.3 = bf16[16,2,128,256]{3,2,1,0:T(8,128)(2,1)} async-done(((bf16[16,2,128,256]{3,2,1,0:T(8,128)(2,1)}), bf16[16,2,128,256]{3,2,1,0:T(8,128)(2,1)}, u32[]{:S(2)}, u32[]{:S(2)}) %all-to-all-start.3) | async-done | bytes 2097184 | tf_op jit(solution)/shard_map/all_to_all | solution.py:74
  361.5 4.4 gather_fusion.7
  365.9 5.5 convolution_bitcast_fusion.2
  371.4 6.5 %copy.29 = f32[47,128,256]{2,1,0:T(8,128)} copy(f32[47,128,256]{1,2,0:T(8,128)} %convolution_bitcast_fusion.2) | data formatting | bytes 12320768 | tf_op jit(solution)/shard_map/bij,bjc->bic/dot_general | solution.py:49
  379.5 14.1 %scatter_fusion.3 = f32[16,128,256]{2,1,0:T(8,128)} fusion(f32[16,128,256]{2,1,0:T(8,128)} %broadcast.49.clone.3, s32[47]{0:T(128)S(1)} %compare_select_fusion.2, f32[47,128,256]{2,1,0:T(8,128)} %copy.29), kind=kCustom, calls=%fused_computation.15 | custom fusion | flops 1540096 | bytes 18481340 | tf_op jit(solution)/shard_map/scatter-add | solution.py:55
  405.8 54.4 %all_to_all.31 = bf16[16,2,128,256]{3,2,1,0:T(8,128)(2,1)S(1)} all-to-all(bf16[16,2,128,256]{3,2,1,0:T(8,128)(2,1)S(1)} %broadcast_select_fusion.1), channel_id=1, replica_groups=mesh['scen'=2,'node'=16] {'node'}, dimensions={0} | all-to-all | bytes 4194304 | tf_op jit(solution)/shard_map/all_to_all | solution.py:69
  466.5 5.5 convolution_bitcast_fusion.1
  472.0 6.5 %copy.31 = f32[47,128,256]{2,1,0:T(8,128)} copy(f32[47,128,256]{1,2,0:T(8,128)} %convolution_bitcast_fusion.1) | data formatting | bytes 12320768 | tf_op jit(solution)/shard_map/bij,bjc->bic/dot_general | solution.py:49
  480.1 14.1 %scatter_fusion.4 = f32[16,128,256]{2,1,0:T(8,128)} fusion(f32[16,128,256]{2,1,0:T(8,128)} %broadcast.49.clone.4, s32[47]{0:T(128)S(1)} %compare_select_fusion.2, f32[47,128,256]{2,1,0:T(8,128)} %copy.31), kind=kCustom, calls=%fused_computation.16 | custom fusion | flops 1540096 | bytes 18481340 | tf_op jit(solution)/shard_map/scatter-add | solution.py:55
  503.3 4.9 all-to-all-start.5
  515.7 38.7 %all-to-all-done.5 = bf16[16,2,128,256]{3,2,1,0:T(8,128)(2,1)} async-done(((bf16[16,2,128,256]{3,2,1,0:T(8,128)(2,1)}), bf16[16,2,128,256]{3,2,1,0:T(8,128)(2,1)}, u32[]{:S(2)}, u32[]{:S(2)}) %all-to-all-start.5) | async-done | bytes 2097184 | tf_op jit(solution)/shard_map/all_to_all | solution.py:74
  562.2 5.5 convolution_bitcast_fusion
  567.7 6.5 %copy.33 = f32[47,128,256]{2,1,0:T(8,128)} copy(f32[47,128,256]{1,2,0:T(8,128)} %convolution_bitcast_fusion) | data formatting | bytes 12320768 | tf_op jit(solution)/shard_map/bij,bjc->bic/dot_general | solution.py:49
  575.8 14.1 %scatter_fusion.5 = f32[16,128,256]{2,1,0:T(8,128)} fusion(f32[16,128,256]{2,1,0:T(8,128)} %broadcast.49, s32[47]{0:T(128)S(1)} %compare_select_fusion.2, f32[47,128,256]{2,1,0:T(8,128)} %copy.33), kind=kCustom, calls=%fused_computation.17 | custom fusion | flops 1540096 | bytes 18481340 | tf_op jit(solution)/shard_map/scatter-add | solution.py:55
  (102 shorter events, 124.6 us)
Async XLA Ops:
  0.6 71.3 %copy-start = (bf16[47,128,128]{2,1,0:T(8,128)(2,1)S(1)}, bf16[47,128,128]{2,1,0:T(8,128)(2,1)}, u32[]{:S(2)}) copy-start(bf16[47,128,128]{2,1,0:T(8,128)(2,1)} %param.18) | copy-start | bytes 4620292
  1.5 1.8 copy-start.13
  4.9 0.9 copy-start.15
  4.9 1.1 copy-start.16
  11.2 6.8 %copy-start.17 = (s32[47]{0:T(128)S(1)}, s32[47]{0:T(128)}, u32[]{:S(2)}) copy-start(s32[47]{0:T(128)} %param.21) | copy-start | bytes 568
  11.2 6.8 %copy-start.18 = (s32[47]{0:T(128)S(1)}, s32[47]{0:T(128)}, u32[]{:S(2)}) copy-start(s32[47]{0:T(128)} %param.20) | copy-start | bytes 568
  11.2 6.8 %copy-start.19 = (s32[47]{0:T(128)S(1)}, s32[47]{0:T(128)}, u32[]{:S(2)}) copy-start(s32[47]{0:T(128)} %param.19) | copy-start | bytes 568
  11.2 52.8 %all-to-all-start = ((bf16[16,2,128,256]{3,2,1,0:T(8,128)(2,1)}), bf16[16,2,128,256]{3,2,1,0:T(8,128)(2,1)}, u32[]{:S(2)}, u32[]{:S(2)}) async-start(bf16[16,2,128,256]{3,2,1,0:T(8,128)(2,1)} %broadcast_select_fusion.5), calls=%async_computation | async-start | bytes 4194304 | tf_op jit(solution)/shard_map/all_to_all | solution.py:69
  108.7 52.7 %all-to-all-start.1 = ((bf16[16,2,128,256]{3,2,1,0:T(8,128)(2,1)}), bf16[16,2,128,256]{3,2,1,0:T(8,128)(2,1)}, u32[]{:S(2)}, u32[]{:S(2)}) async-start(bf16[16,2,128,256]{3,2,1,0:T(8,128)(2,1)} %broadcast_select_fusion.4), calls=%async_computation.1 | async-start | bytes 4194304 | tf_op jit(solution)/shard_map/all_to_all | solution.py:74
  116.5 3.8 copy-start.7
  197.2 3.6 copy-start.10
  200.8 1.8 copy-start.11
  209.4 54.4 %copy-start.1 = (bf16[2048,256]{1,0:T(8,128)(2,1)S(1)}, bf16[2048,256]{1,0:T(8,128)(2,1)}, u32[]{:S(2)}) copy-start(bf16[2048,256]{1,0:T(8,128)(2,1)} %fusion.20) | copy-start | bytes 3145732
  306.8 50.9 %all-to-all-start.3 = ((bf16[16,2,128,256]{3,2,1,0:T(8,128)(2,1)}), bf16[16,2,128,256]{3,2,1,0:T(8,128)(2,1)}, u32[]{:S(2)}, u32[]{:S(2)}) async-start(bf16[16,2,128,256]{3,2,1,0:T(8,128)(2,1)} %broadcast_select_fusion.2), calls=%async_computation.3 | async-start | bytes 4194304 | tf_op jit(solution)/shard_map/all_to_all | solution.py:74
  311.6 3.8 copy-start.2
  315.5 1.4 copy-start.8
  393.6 3.7 copy-start.9
  405.8 54.4 %copy-start.4 = (bf16[2048,256]{1,0:T(8,128)(2,1)S(1)}, bf16[2048,256]{1,0:T(8,128)(2,1)}, u32[]{:S(2)}) copy-start(bf16[2048,256]{1,0:T(8,128)(2,1)} %fusion.21) | copy-start | bytes 3145732
  503.3 4.9 copy-start.14
  503.3 51.0 %all-to-all-start.5 = ((bf16[16,2,128,256]{3,2,1,0:T(8,128)(2,1)}), bf16[16,2,128,256]{3,2,1,0:T(8,128)(2,1)}, u32[]{:S(2)}, u32[]{:S(2)}) async-start(bf16[16,2,128,256]{3,2,1,0:T(8,128)(2,1)} %broadcast_select_fusion), calls=%async_computation.5 | async-start | bytes 4194304 | tf_op jit(solution)/shard_map/all_to_all | solution.py:74
  508.2 1.2 copy-start.3
  509.5 1.2 copy-start.5
  512.0 1.4 copy-start.6
  589.9 1.9 copy-start.12
where the time goes:
time: 598 us; the launch traced here: 594 us
  waiting for transfers between devices  162 us (27%)
  other arithmetic  137 us (23%)
  blocking collectives  109 us (18%)
  local copies, waits for them, and re-layouts  95.6 us (16%)
  matrix products  65.9 us (11%)
  starting transfers between devices  23 us (4%)
    all_to_all x3, waiting for transfers between devices, local(): lax.all_to_all(outbound(hop_one), 'node', split_axis=0, concat_axis=0, ti...  116 us
    all_to_all x2, blocking collectives, local(): lax.all_to_all(outbound(local_gated), 'node', split_axis=0, concat_axis=0...  109 us
    scatter-add x6, other arithmetic, propagate(): summed = jnp.zeros((tile_count, TILE, lookup.shape[2]), jnp.float32).at[b...  84.7 us
    all_to_all x1, waiting for transfers between devices, local(): lax.all_to_all(outbound(local_gated), 'node', split_axis=0, concat_axis=0...  46 us
    dot_general x6, local copies, waits for them, and re-layouts, propagate(): jnp.einsum('bij,bjc->bic', block_values, picked, preferred_element_type=j...  39.2 us
    dot_general x6, matrix products, propagate(): jnp.einsum('bij,bjc->bic', block_values, picked, preferred_element_type=j...  33 us
    gather x6, local copies, waits for them, and re-layouts, propagate(): picked = lookup[source]  26.3 us
    gather x6, local copies, waits for them, and re-layouts, outbound(): local_tiles[routing]  18.1 us
  transfers between devices with their start and end apart: 4, of which 4 were waited for; matrix products, arithmetic and copies ran while one was open for 3% of the time, Pallas kernels for 0%

commit v1 on v0

v1 whole, which is shorter than its diff:
```python
import functools

import jax
import jax.numpy as jnp
from jax import lax
from jax.experimental import pallas as pl
from jax.experimental.pallas import tpu as pltpu
from jax.sharding import PartitionSpec as P

TILE = 128
CAP = 2
F32 = jnp.float32
BF16 = jnp.bfloat16
VMEM = pl.BlockSpec(memory_space=pltpu.VMEM)
SMEM = pl.BlockSpec(memory_space=pltpu.SMEM)
LIMIT = 48 << 20


def dot(a, b):
    return jnp.dot(a, b, preferred_element_type=F32)


def call(kernel, name, ins, outs, in_specs, out_specs, flops, scratch=(), alias=None):
    moved = sum(x.size * x.dtype.itemsize for x in ins) + sum(
        o.size * o.dtype.itemsize for o in outs
    )
    return pl.pallas_call(
        kernel,
        name=name,
        out_shape=tuple(outs),
        in_specs=in_specs,
        out_specs=tuple(out_specs),
        scratch_shapes=scratch,
        input_output_aliases=alias or {},
        compiler_params=pltpu.CompilerParams(vmem_limit_bytes=LIMIT),
        cost_estimate=pl.CostEstimate(flops=flops, bytes_accessed=moved, transcendentals=0),
    )(*ins)


def shape(dims, dtype):
    return jax.ShapeDtypeStruct(dims, dtype)


def fill_send(routing, field, send):
    for place in range(send.shape[0]):
        tile = routing[place]
        send[place] = field[pl.ds(pl.multiple_of(tile * TILE, TILE), TILE), :]


def add_remote(table, blocks, far, total):
    remote = blocks.shape[0]
    for j in range(remote):
        rows = pl.ds(pl.multiple_of(table[0, j] * TILE, TILE), TILE)
        total[rows, :] += dot(blocks[j], far[table[1, j]])


def convolve(past, state, weight, bias, mix, gated, second, gate):
    rows = state.shape[0]
    chunk = 512
    part = 128

    def body(i, carry):
        for k in range(chunk // part):
            at = pl.ds(pl.multiple_of(i * chunk + k * part, part), part)
            both = jnp.concatenate([past[at, :], state[at, :]], axis=1)
            pre = dot(both, weight[...]) + bias[...]
            value = jnp.tanh(pre[:, :gate]) * (0.5 * jnp.tanh(0.5 * pre[:, gate:]) + 0.5)
            value = value.astype(BF16)
            gated[at, :] = value
            second[at, :] = dot(value, mix[...]).astype(BF16)
        return carry

    lax.fori_loop(0, rows // chunk, body, 0)


def first_kernel(routing, state, past, weight, bias, mix, gated, second, send, *, gate):
    convolve(past, state, weight, bias, mix, gated, second, gate)
    fill_send(routing, second, send)


def next_kernel(
    routing, table, blocks, far, total_in, past, weight, bias, mix,
    state, gated, second, send, total, *, gate,
):
    total[...] = total_in[...]
    add_remote(table, blocks, far, total)
    state[...] = total[...].astype(BF16)
    convolve(past, state, weight, bias, mix, gated, second, gate)
    fill_send(routing, second, send)


def hop_kernel(routing, table, blocks, far, total_in, field, send, total):
    total[...] = total_in[...]
    add_remote(table, blocks, far, total)
    field[...] = total[...].astype(BF16)
    fill_send(routing, field, send)


def last_kernel(table, blocks, far, total_in, state, total):
    total[...] = total_in[...]
    add_remote(table, blocks, far, total)
    state[...] = total[...].astype(BF16)


def build_kernel(place, target, owner, slot, values, table, local, remote_blocks, *, tiles):
    me = place[0]

    def body(b, seen):
        t, o, s = target[b], owner[b], slot[b]
        mine = o == me

        @pl.when(mine)
        def _():
            row = jnp.where(s == t, 0, 1)
            local[row, t] = b
            local[row + 2, t] = s

        @pl.when(jnp.logical_not(mine))
        def _():
            table[0, seen] = t
            table[1, seen] = o * CAP + s
            remote_blocks[seen] = values[b]

        return seen + jnp.where(mine, 0, 1)

    lax.fori_loop(0, target.shape[0], body, jnp.int32(0))


def local_sum(local, values, field, t):
    other = field[pl.ds(pl.multiple_of(local[3, t] * TILE, TILE), TILE), :]
    own = field[pl.ds(t * TILE, TILE), :]
    block = jnp.concatenate([values[local[0, t]], values[local[1, t]]], axis=1)
    return dot(block, jnp.concatenate([own, other], axis=0))


def under_first_kernel(
    local, values, gated, second, wide, skip_in, total, base, skip, *, res
):
    for t in range(gated.shape[0] // TILE):
        at = pl.ds(t * TILE, TILE)
        out = dot(gated[at, :], wide[...])
        total[at, :] = out[:, :res] + local_sum(local, values, second, t)
        base[at, :] = out[:, res : 2 * res]
        if skip_in is None:
            skip[at, :] = out[:, 2 * res :].astype(skip.dtype)
        else:
            skip[at, :] = (skip_in[at, :] + out[:, 2 * res :]).astype(skip.dtype)


def under_second_kernel(local, values, field, base, state, total):
    for t in range(field.shape[0] // TILE):
        at = pl.ds(t * TILE, TILE)
        total[at, :] = (
            state[at, :].astype(F32) + base[at, :] + local_sum(local, values, field, t)
        )


def local(
    hidden_state,
    conv_cache,
    conv_weight,
    conv_bias,
    mix_weight,
    skip_weight,
    block_values,
    block_target,
    block_owner,
    block_slot,
    send_tiles,
    send_count,
):
    rows, res = hidden_state.shape
    layers = conv_cache.shape[0]
    gate, skips = skip_weight.shape[1:]
    tiles = rows // TILE
    peers = send_tiles.shape[1]
    slots = peers * CAP
    blocks = block_values.shape[0]
    remote = blocks - 2 * tiles
    place = lax.axis_index("node").astype(jnp.int32)[None]
    routing = send_tiles.reshape(slots)

    table, local_table, remote_blocks = call(
        functools.partial(build_kernel, tiles=tiles),
        "sort_blocks",
        (place, block_target, block_owner, block_slot, block_values),
        (
            shape((2, remote), jnp.int32),
            shape((4, tiles), jnp.int32),
            shape((remote, TILE, TILE), BF16),
        ),
        [SMEM] * 4 + [VMEM],
        [SMEM, SMEM, VMEM],
        blocks * 1000,
    )

    def exchange(send):
        got = lax.all_to_all(
            send.reshape(peers, CAP, TILE, res), "node", split_axis=0, concat_axis=0, tiled=True
        )
        return got.reshape(slots, TILE, res)

    conv_flops = 2 * rows * (2 * res * 2 * gate + gate * res)
    hop_flops = 2 * remote * TILE * TILE * res
    conv_outs = (
        shape((rows, gate), BF16),
        shape((rows, res), BF16),
        shape((slots, TILE, res), BF16),
    )
    state = hidden_state
    skip = None
    total = far = None
    for layer in range(layers):
        mixing = mix_weight[layer]
        weight, bias = conv_weight[layer], conv_bias[layer][None, :]
        wide = jnp.concatenate(
            [mixing[gate : 2 * gate], mixing[:gate], skip_weight[layer]], axis=1
        )
        deep = mixing[2 * gate :]
        if layer == 0:
            gated, second, send = call(
                functools.partial(first_kernel, gate=gate),
                "conv_first",
                (routing, state, conv_cache[layer], weight, bias, deep),
                conv_outs,
                [SMEM] + [VMEM] * 5,
                [VMEM] * 3,
                conv_flops,
            )
        else:
            state, gated, second, send = call(
                functools.partial(next_kernel, gate=gate),
                "conv_next",
                (routing, table, remote_blocks, far, total, conv_cache[layer], weight, bias, deep),
                (shape((rows, res), BF16),) + conv_outs,
                [SMEM] * 2 + [VMEM] * 7,
                [VMEM] * 4,
                conv_flops + hop_flops,
                [pltpu.VMEM((rows, res), F32)],
            )
        far = exchange(send)
        last = layer == layers - 1
        first_ins = (local_table, block_values, gated, second, wide)
        kernel = functools.partial(under_first_kernel, res=res)
        if layer == 0:
            ins = first_ins

            def body(l, v, g, s, w, t, b, k):
                under_first_kernel(l, v, g, s, w, None, t, b, k, res=res)

        else:
            ins = first_ins + (skip,)
            body = kernel
        total, base, skip = call(
            body,
            "under_first",
            ins,
            (
                shape((rows, res), F32),
                shape((rows, res), F32),
                shape((rows, skips), BF16 if last else F32),
            ),
            [SMEM] + [VMEM] * (len(ins) - 1),
            [VMEM] * 3,
            2 * rows * gate * (2 * res + skips) + 4 * rows * TILE * res,
        )
        field, send = call(
            hop_kernel,
            "hop",
            (routing, table, remote_blocks, far, total),
            (shape((rows, res), BF16), shape((slots, TILE, res), BF16)),
            [SMEM] * 2 + [VMEM] * 3,
            [VMEM] * 2,
            hop_flops,
            [pltpu.VMEM((rows, res), F32)],
        )
        far = exchange(send)
        (total,) = call(
            under_second_kernel,
            "under_second",
            (local_table, block_values, field, base, state),
            (shape((rows, res), F32),),
            [SMEM] + [VMEM] * 4,
            [VMEM],
            4 * rows * TILE * res,
        )
    (state,) = call(
        last_kernel,
        "last",
        (table, remote_blocks, far, total),
        (shape((rows, res), BF16),),
        [SMEM] + [VMEM] * 3,
        [VMEM],
        hop_flops,
        [pltpu.VMEM((rows, res), F32)],
    )
    return state, skip


def solution(mesh):
    placed = (
        P(("scen", "node"), None),
        P(None, ("scen", "node"), None),
        P(),
        P(),
        P(),
        P(),
        P("node", None, None),
        P("node"),
        P("node"),
        P("node"),
        P("node", None, None),
        P("node", None),
    )
    return jax.shard_map(
        local,
        mesh=mesh,
        in_specs=placed,
        out_specs=(P(("scen", "node"), None), P(("scen", "node"), None)),
        check_vma=False,
    )
```

time: 598 us -> 231 us (0.39)
  other arithmetic: 137 us -> 1.7 us
  blocking collectives: 109 us -> 0 us
  matrix products: 65.9 us -> 0 us
  waiting for transfers between devices: 162 us -> 106 us
  local copies, waits for them, and re-layouts: 95.6 us -> 54.4 us
  Pallas kernels: 0 us -> 34 us
  starting transfers between devices: 23 us -> 31.7 us
    all_to_all x2 -> x0, blocking collectives: 109 us -> none  [local(): lax.all_to_all(outbound(local_gated), 'node', split_axis=0, concat_axis=0...]
    scatter-add x6 -> x0, other arithmetic: 84.7 us -> none  [propagate(): summed = jnp.zeros((tile_count, TILE, lookup.shape[2]), jnp.float32).at[b...]
    dot_general x24 -> x0, matrix products: 65.9 us -> none  [the longest x6 33 us: propagate(): jnp.einsum('bij,bjc->bic', block_values, picked, preferred_element_type=j...]
    all_to_all x4 -> x6, waiting for transfers between devices: 162 us -> 106 us  [exchange(): lax.all_to_all(send.reshape(peers, CAP, TILE, res), 'node', split_axis=0,...]
    unnamed x40 -> x119, local copies, waits for them, and re-layouts: 1.7 us -> 48 us
    gather x12 -> x0, local copies, waits for them, and re-layouts: 44.4 us -> none  [the longest x6 26.3 us: propagate(): picked = lookup[source]]
    dot_general x6 -> x0, local copies, waits for them, and re-layouts: 39.2 us -> none  [propagate(): jnp.einsum('bij,bjc->bic', block_values, picked, preferred_element_type=j...]
    pallas_call x0 -> x14, Pallas kernels: none -> 34 us  [call(): pl.pallas_call(kernel, name=name, out_shape=tuple(outs), in_specs=in_spec...]
  transfers between devices with their start and end apart: 4 -> 6, of which waited for: 4 -> 6; matrix products, arithmetic and copies ran while one was open for 3% -> 1% of each run, Pallas kernels for 0% -> 7%
where the time goes in v1:
time: 231 us; the launch traced here: 229 us
  waiting for transfers between devices  106 us (46%)
  local copies, waits for them, and re-layouts  54.4 us (24%)
  Pallas kernels  34 us (15%)
  starting transfers between devices  31.7 us (14%)
    all_to_all x6, waiting for transfers between devices, exchange(): lax.all_to_all(send.reshape(peers, CAP, TILE, res), 'node', split_axis=0,...  106 us
    unnamed x119, local copies, waits for them, and re-layouts  48 us
    pallas_call x14, Pallas kernels, call(): pl.pallas_call(kernel, name=name, out_shape=tuple(outs), in_specs=in_spec...  34 us
    all_to_all x6, starting transfers between devices, exchange(): lax.all_to_all(send.reshape(peers, CAP, TILE, res), 'node', split_axis=0,...  31.7 us
  transfers between devices with their start and end apart: 6, of which 6 were waited for; matrix products, arithmetic and copies ran while one was open for 1% of the time, Pallas kernels for 7%

profile of v1, /device:TPU:9, one launch (start us, length us, event | category | flops | bytes accessed | tf_op | source)
XLA Modules:
  0.0 228.7 jit_solution(14658243974637872323)
XLA Ops:
  2.3 2.0 slice_bitcast_fusion.10
  6.2 3.9 %conv_first.1 = (bf16[2048,256]{1,0:T(8,128)(2,1)S(1)}, bf16[2048,128]{1,0:T(8,128)(2,1)S(1)}, bf16[32,128,128]{2,1,0:T(8,128)(2,1)S(1)}) custom-call(s32[32]{0:T(128)S(1)} %reshape.52.routing, bf16[2048,128]{1,0:T(8,128)(2,1)S(1)} %copy-done.33, bf16[2048,128]{1,0:T(8,128)(2,1)S(1)} %get-tuple-element.61.past, ...), custom_call_target="tpu_custom_call" | custom-call | flops 671088640 | bytes 3999872 | tf_op jit(solution)/shard_map/conv_first/pallas_call | solution.py:27
  12.8 6.8 %all-to-all-start = ((bf16[16,2,128,128]{3,2,1,0:T(8,128)(2,1)}), bf16[16,2,128,128]{3,2,1,0:T(8,128)(2,1)S(1)}, u32[]{:S(2)}, u32[]{:S(2)}) async-start(bf16[16,2,128,128]{3,2,1,0:T(8,128)(2,1)} %bitcast.55), calls=%async_computation | async-start | bytes 2097152 | tf_op jit(solution)/shard_map/all_to_all | solution.py:198
  19.6 2.0 sort_blocks.1
  21.7 1.7 slice_bitcast_fusion.6
  23.4 1.7 pad_maximum_fusion
  25.1 2.9 %under_first.3 = (f32[2048,128]{1,0:T(8,128)S(1)}, f32[2048,128]{1,0:T(8,128)S(1)}, f32[2048,256]{1,0:T(8,128)}) custom-call(s32[4,16]{1,0:T(4,128)S(1)} %get-tuple-element.34.l.local, bf16[47,128,128]{2,1,0:T(8,128)(2,1)S(1)} %copy-done, bf16[2048,256]{1,0:T(8,128)(2,1)S(1)} %copy-done.8, bf16[2048,128]{1,0:T(8,128)(2,1)S(1)} %copy-done.50, ...), custom_call_target="tpu_custom_call" | custom-call | flops 671088640 | bytes 7569664 | tf_op jit(solution)/shard_map/under_first/pallas_call | solution.py:27
  29.9 14.6 %all-to-all-done = bf16[16,2,128,128]{3,2,1,0:T(8,128)(2,1)S(1)} async-done(((bf16[16,2,128,128]{3,2,1,0:T(8,128)(2,1)}), bf16[16,2,128,128]{3,2,1,0:T(8,128)(2,1)S(1)}, u32[]{:S(2)}, u32[]{:S(2)}) %all-to-all-start) | async-done | bytes 1048608 | tf_op jit(solution)/shard_map/all_to_all | solution.py:198
  44.4 1.2 copy-done.19
  48.5 5.0 %all-to-all-start.1 = ((bf16[16,2,128,128]{3,2,1,0:T(8,128)(2,1)}), bf16[16,2,128,128]{3,2,1,0:T(8,128)(2,1)S(1)}, u32[]{:S(2)}, u32[]{:S(2)}) async-start(bf16[16,2,128,128]{3,2,1,0:T(8,128)(2,1)} %bitcast.60), calls=%async_computation.1 | async-start | bytes 2097152 | tf_op jit(solution)/shard_map/all_to_all | solution.py:198
  53.4 1.2 copy-done.32
  58.7 19.5 %all-to-all-done.1 = bf16[16,2,128,128]{3,2,1,0:T(8,128)(2,1)S(1)} async-done(((bf16[16,2,128,128]{3,2,1,0:T(8,128)(2,1)}), bf16[16,2,128,128]{3,2,1,0:T(8,128)(2,1)S(1)}, u32[]{:S(2)}, u32[]{:S(2)}) %all-to-all-start.1) | async-done | bytes 1048608 | tf_op jit(solution)/shard_map/all_to_all | solution.py:198
  80.3 5.0 %conv_next.2 = (bf16[2048,128]{1,0:T(8,128)(2,1)S(1)}, bf16[2048,256]{1,0:T(8,128)(2,1)S(1)}, bf16[2048,128]{1,0:T(8,128)(2,1)S(1)}, bf16[32,128,128]{2,1,0:T(8,128)(2,1)S(1)}) custom-call(s32[32]{0:T(128)S(1)} %reshape.52.routing, s32[2,15]{1,0:T(2,128)S(1)} %get-tuple-element.31.table, bf16[15,128,128]{2,1,0:T(8,128)(2,1)S(1)} %get-tuple-element.32.blocks, ...), custom_call_target="tpu_custom_call" | custom-call | flops 734003200 | bytes 6588664 | tf_op jit(solution)/shard_map/conv_next/pallas_call | solution.py:27
  88.8 5.0 %all-to-all-start.2 = ((bf16[16,2,128,128]{3,2,1,0:T(8,128)(2,1)}), bf16[16,2,128,128]{3,2,1,0:T(8,128)(2,1)S(1)}, u32[]{:S(2)}, u32[]{:S(2)}) async-start(bf16[16,2,128,128]{3,2,1,0:T(8,128)(2,1)} %bitcast.57), calls=%async_computation.2 | async-start | bytes 2097152 | tf_op jit(solution)/shard_map/all_to_all | solution.py:198
  93.8 1.2 copy-done.12
  97.0 3.9 %under_first.4 = (f32[2048,128]{1,0:T(8,128)S(1)}, f32[2048,128]{1,0:T(8,128)S(1)}, f32[2048,256]{1,0:T(8,128)}) custom-call(s32[4,16]{1,0:T(4,128)S(1)} %get-tuple-element.34.l.local, bf16[47,128,128]{2,1,0:T(8,128)(2,1)S(1)} %copy-done, bf16[2048,256]{1,0:T(8,128)(2,1)S(1)} %copy-done.12, bf16[2048,128]{1,0:T(8,128)(2,1)S(1)} %copy-done.42, ...), custom_call_target="tpu_custom_call" | custom-call | flops 671088640 | bytes 9666816 | tf_op jit(solution)/shard_map/under_first/pallas_call | solution.py:27
  102.9 15.7 %all-to-all-done.2 = bf16[16,2,128,128]{3,2,1,0:T(8,128)(2,1)S(1)} async-done(((bf16[16,2,128,128]{3,2,1,0:T(8,128)(2,1)}), bf16[16,2,128,128]{3,2,1,0:T(8,128)(2,1)S(1)}, u32[]{:S(2)}, u32[]{:S(2)}) %all-to-all-start.2) | async-done | bytes 1048608 | tf_op jit(solution)/shard_map/all_to_all | solution.py:198
  118.6 1.2 copy-done.21
  122.6 5.0 %all-to-all-start.3 = ((bf16[16,2,128,128]{3,2,1,0:T(8,128)(2,1)}), bf16[16,2,128,128]{3,2,1,0:T(8,128)(2,1)S(1)}, u32[]{:S(2)}, u32[]{:S(2)}) async-start(bf16[16,2,128,128]{3,2,1,0:T(8,128)(2,1)} %bitcast.59), calls=%async_computation.3 | async-start | bytes 2097152 | tf_op jit(solution)/shard_map/all_to_all | solution.py:198
  127.6 1.2 copy-done.30
  132.9 19.5 %all-to-all-done.3 = bf16[16,2,128,128]{3,2,1,0:T(8,128)(2,1)S(1)} async-done(((bf16[16,2,128,128]{3,2,1,0:T(8,128)(2,1)}), bf16[16,2,128,128]{3,2,1,0:T(8,128)(2,1)S(1)}, u32[]{:S(2)}, u32[]{:S(2)}) %all-to-all-start.3) | async-done | bytes 1048608 | tf_op jit(solution)/shard_map/all_to_all | solution.py:198
  153.5 5.0 %conv_next.3 = (bf16[2048,128]{1,0:T(8,128)(2,1)S(1)}, bf16[2048,256]{1,0:T(8,128)(2,1)S(1)}, bf16[2048,128]{1,0:T(8,128)(2,1)S(1)}, bf16[32,128,128]{2,1,0:T(8,128)(2,1)S(1)}) custom-call(s32[32]{0:T(128)S(1)} %reshape.52.routing, s32[2,15]{1,0:T(2,128)S(1)} %get-tuple-element.31.table, bf16[15,128,128]{2,1,0:T(8,128)(2,1)S(1)} %get-tuple-element.32.blocks, ...), custom_call_target="tpu_custom_call" | custom-call | flops 734003200 | bytes 6588664 | tf_op jit(solution)/shard_map/conv_next/pallas_call | solution.py:27
  162.0 5.1 %all-to-all-start.4 = ((bf16[16,2,128,128]{3,2,1,0:T(8,128)(2,1)}), bf16[16,2,128,128]{3,2,1,0:T(8,128)(2,1)S(1)}, u32[]{:S(2)}, u32[]{:S(2)}) async-start(bf16[16,2,128,128]{3,2,1,0:T(8,128)(2,1)} %bitcast.56), calls=%async_computation.4 | async-start | bytes 2097152 | tf_op jit(solution)/shard_map/all_to_all | solution.py:198
  167.2 1.2 copy-done.10
  169.4 3.6 %under_first.5 = (f32[2048,128]{1,0:T(8,128)S(1)}, f32[2048,128]{1,0:T(8,128)S(1)}, bf16[2048,256]{1,0:T(8,128)(2,1)}) custom-call(s32[4,16]{1,0:T(4,128)S(1)} %get-tuple-element.34.l.local, bf16[47,128,128]{2,1,0:T(8,128)(2,1)S(1)} %copy-done, bf16[2048,256]{1,0:T(8,128)(2,1)S(1)} %copy-done.10, bf16[2048,128]{1,0:T(8,128)(2,1)S(1)} %copy-done.40, ...), custom_call_target="tpu_custom_call" | custom-call | flops 671088640 | bytes 8618240 | tf_op jit(solution)/shard_map/under_first/pallas_call | solution.py:27
  174.9 17.0 %all-to-all-done.4 = bf16[16,2,128,128]{3,2,1,0:T(8,128)(2,1)S(1)} async-done(((bf16[16,2,128,128]{3,2,1,0:T(8,128)(2,1)}), bf16[16,2,128,128]{3,2,1,0:T(8,128)(2,1)S(1)}, u32[]{:S(2)}, u32[]{:S(2)}) %all-to-all-start.4) | async-done | bytes 1048608 | tf_op jit(solution)/shard_map/all_to_all | solution.py:198
  191.9 1.2 copy-done.17
  195.9 5.0 %all-to-all-start.5 = ((bf16[16,2,128,128]{3,2,1,0:T(8,128)(2,1)}), bf16[16,2,128,128]{3,2,1,0:T(8,128)(2,1)S(1)}, u32[]{:S(2)}, u32[]{:S(2)}) async-start(bf16[16,2,128,128]{3,2,1,0:T(8,128)(2,1)} %bitcast.58), calls=%async_computation.5 | async-start | bytes 2097152 | tf_op jit(solution)/shard_map/all_to_all | solution.py:198
  200.9 1.2 copy-done.28
  206.2 19.5 %all-to-all-done.5 = bf16[16,2,128,128]{3,2,1,0:T(8,128)(2,1)S(1)} async-done(((bf16[16,2,128,128]{3,2,1,0:T(8,128)(2,1)}), bf16[16,2,128,128]{3,2,1,0:T(8,128)(2,1)S(1)}, u32[]{:S(2)}, u32[]{:S(2)}) %all-to-all-start.5) | async-done | bytes 1048608 | tf_op jit(solution)/shard_map/all_to_all | solution.py:198
  225.8 1.2 copy-done.4
  227.0 1.7 last.1
  (121 shorter events, 45.8 us)
Async XLA Ops:
  0.6 3.7 %copy-start.55 = (bf16[3,256,512]{2,1,0:T(8,128)(2,1)S(1)}, bf16[3,256,512]{2,1,0:T(8,128)(2,1)}, u32[]{:S(2)}) copy-start(bf16[3,256,512]{2,1,0:T(8,128)(2,1)} %param.14) | copy-start | bytes 2359300
  2.3 2.8 %copy-start.54 = (bf16[3,2048,128]{2,1,0:T(8,128)(2,1)S(1)}, bf16[3,2048,128]{2,1,0:T(8,128)(2,1)}, u32[]{:S(2)}) copy-start(bf16[3,2048,128]{2,1,0:T(8,128)(2,1)} %param.13) | copy-start | bytes 4718596
  5.1 1.1 copy-start.33
  12.8 6.8 %copy-start = (bf16[47,128,128]{2,1,0:T(8,128)(2,1)S(1)}, bf16[47,128,128]{2,1,0:T(8,128)(2,1)}, u32[]{:S(2)}) copy-start(bf16[47,128,128]{2,1,0:T(8,128)(2,1)} %values.11) | copy-start | bytes 4620292
  12.8 6.8 %copy-start.51 = (s32[47]{0:T(128)S(1)}, s32[47]{0:T(128)}, u32[]{:S(2)}) copy-start(s32[47]{0:T(128)} %target.1) | copy-start | bytes 568
  12.8 6.8 %copy-start.52 = (s32[47]{0:T(128)S(1)}, s32[47]{0:T(128)}, u32[]{:S(2)}) copy-start(s32[47]{0:T(128)} %owner.1) | copy-start | bytes 568
  12.8 6.8 %copy-start.53 = (s32[47]{0:T(128)S(1)}, s32[47]{0:T(128)}, u32[]{:S(2)}) copy-start(s32[47]{0:T(128)} %slot.1) | copy-start | bytes 568
  12.8 31.6 %all-to-all-start = ((bf16[16,2,128,128]{3,2,1,0:T(8,128)(2,1)}), bf16[16,2,128,128]{3,2,1,0:T(8,128)(2,1)S(1)}, u32[]{:S(2)}, u32[]{:S(2)}) async-start(bf16[16,2,128,128]{3,2,1,0:T(8,128)(2,1)} %bitcast.55), calls=%async_computation | async-start | bytes 2097152 | tf_op jit(solution)/shard_map/all_to_all | solution.py:198
  19.6 5.4 %copy-start.8 = (bf16[2048,256]{1,0:T(8,128)(2,1)S(1)}, bf16[2048,256]{1,0:T(8,128)(2,1)}, u32[]{:S(2)}) copy-start(bf16[2048,256]{1,0:T(8,128)(2,1)} %copy-done.7) | copy-start | bytes 3145732
  19.6 5.4 %copy-start.50 = (bf16[2048,128]{1,0:T(8,128)(2,1)S(1)}, bf16[2048,128]{1,0:T(8,128)(2,1)}, u32[]{:S(2)}) copy-start(bf16[2048,128]{1,0:T(8,128)(2,1)} %copy-done.49) | copy-start | bytes 1572868
  44.4 1.2 copy-start.19
  48.5 29.8 %all-to-all-start.1 = ((bf16[16,2,128,128]{3,2,1,0:T(8,128)(2,1)}), bf16[16,2,128,128]{3,2,1,0:T(8,128)(2,1)S(1)}, u32[]{:S(2)}, u32[]{:S(2)}) async-start(bf16[16,2,128,128]{3,2,1,0:T(8,128)(2,1)} %bitcast.60), calls=%async_computation.1 | async-start | bytes 2097152 | tf_op jit(solution)/shard_map/all_to_all | solution.py:198
  53.4 1.2 copy-start.32
  54.6 1.0 copy-start.34
  55.7 1.0 copy-start.48
  78.3 1.0 copy-start.6
  88.8 29.8 %all-to-all-start.2 = ((bf16[16,2,128,128]{3,2,1,0:T(8,128)(2,1)}), bf16[16,2,128,128]{3,2,1,0:T(8,128)(2,1)S(1)}, u32[]{:S(2)}, u32[]{:S(2)}) async-start(bf16[16,2,128,128]{3,2,1,0:T(8,128)(2,1)} %bitcast.57), calls=%async_computation.2 | async-start | bytes 2097152 | tf_op jit(solution)/shard_map/all_to_all | solution.py:198
  93.8 1.2 copy-start.12
  95.9 1.0 copy-start.42
  118.6 1.2 copy-start.21
  122.6 29.8 %all-to-all-start.3 = ((bf16[16,2,128,128]{3,2,1,0:T(8,128)(2,1)}), bf16[16,2,128,128]{3,2,1,0:T(8,128)(2,1)S(1)}, u32[]{:S(2)}, u32[]{:S(2)}) async-start(bf16[16,2,128,128]{3,2,1,0:T(8,128)(2,1)} %bitcast.59), calls=%async_computation.3 | async-start | bytes 2097152 | tf_op jit(solution)/shard_map/all_to_all | solution.py:198
  127.6 1.2 copy-start.30
  152.4 1.0 copy-start.5
  162.0 5.1 %copy-start.56 = (bf16[256,256]{1,0:T(8,128)(2,1)S(1)}, bf16[256,256]{1,0:T(8,128)(2,1)}, u32[]{:S(2)}) copy-start(bf16[256,256]{1,0:T(8,128)(2,1)} %get-tuple-element.75) | copy-start | bytes 393220
  162.0 5.1 %copy-start.57 = (bf16[256,128]{1,0:T(8,128)(2,1)S(1)}, bf16[256,128]{1,0:T(8,128)(2,1)}, u32[]{:S(2)}) copy-start(bf16[256,128]{1,0:T(8,128)(2,1)} %get-tuple-element.66) | copy-start | bytes 196612
  162.0 5.1 %copy-start.58 = (bf16[256,128]{1,0:T(8,128)(2,1)S(1)}, bf16[256,128]{1,0:T(8,128)(2,1)}, u32[]{:S(2)}) copy-start(bf16[256,128]{1,0:T(8,128)(2,1)} %get-tuple-element.74) | copy-start | bytes 196612
  162.0 29.9 %all-to-all-start.4 = ((bf16[16,2,128,128]{3,2,1,0:T(8,128)(2,1)}), bf16[16,2,128,128]{3,2,1,0:T(8,128)(2,1)S(1)}, u32[]{:S(2)}, u32[]{:S(2)}) async-start(bf16[16,2,128,128]{3,2,1,0:T(8,128)(2,1)} %bitcast.56), calls=%async_computation.4 | async-start | bytes 2097152 | tf_op jit(solution)/shard_map/all_to_all | solution.py:198
  167.1 1.2 copy-start.10
  191.9 1.2 copy-start.17
  195.9 29.8 %all-to-all-start.5 = ((bf16[16,2,128,128]{3,2,1,0:T(8,128)(2,1)}), bf16[16,2,128,128]{3,2,1,0:T(8,128)(2,1)S(1)}, u32[]{:S(2)}, u32[]{:S(2)}) async-start(bf16[16,2,128,128]{3,2,1,0:T(8,128)(2,1)} %bitcast.58), calls=%async_computation.5 | async-start | bytes 2097152 | tf_op jit(solution)/shard_map/all_to_all | solution.py:198
  200.9 1.2 copy-start.28
  225.7 1.2 copy-start.4
  (33 other events, 31.0 us)

commit v2 on v1

--- a/solution.py
+++ b/solution.py
@@ -13,7 +13,8 @@
 BF16 = jnp.bfloat16
 VMEM = pl.BlockSpec(memory_space=pltpu.VMEM)
 SMEM = pl.BlockSpec(memory_space=pltpu.SMEM)
-LIMIT = 48 << 20
+HBM = pl.BlockSpec(memory_space=pltpu.HBM)
+LIMIT = 60 << 20
 
 
 def dot(a, b):
@@ -41,65 +42,102 @@
     return jax.ShapeDtypeStruct(dims, dtype)
 
 
-def fill_send(routing, field, send):
+def start(source, target, sem):
+    copy = pltpu.make_async_copy(source, target, sem)
+    copy.start()
+    return copy
+
+
+def start_send(routing, field, send, sem):
     for place in range(send.shape[0]):
-        tile = routing[place]
-        send[place] = field[pl.ds(pl.multiple_of(tile * TILE, TILE), TILE), :]
+        rows = pl.ds(pl.multiple_of(routing[place] * TILE, TILE), TILE)
+        start(field.at[rows, :], send.at[place], sem)
+    return pltpu.make_async_copy(send, send, sem)
 
 
 def add_remote(table, blocks, far, total):
-    remote = blocks.shape[0]
-    for j in range(remote):
+    for j in range(blocks.shape[0]):
         rows = pl.ds(pl.multiple_of(table[0, j] * TILE, TILE), TILE)
         total[rows, :] += dot(blocks[j], far[table[1, j]])
 
 
-def convolve(past, state, weight, bias, mix, gated, second, gate):
-    rows = state.shape[0]
-    chunk = 512
-    part = 128
-
-    def body(i, carry):
-        for k in range(chunk // part):
-            at = pl.ds(pl.multiple_of(i * chunk + k * part, part), part)
-            both = jnp.concatenate([past[at, :], state[at, :]], axis=1)
-            pre = dot(both, weight[...]) + bias[...]
-            value = jnp.tanh(pre[:, :gate]) * (0.5 * jnp.tanh(0.5 * pre[:, gate:]) + 0.5)
-            value = value.astype(BF16)
-            gated[at, :] = value
-            second[at, :] = dot(value, mix[...]).astype(BF16)
-        return carry
-
-    lax.fori_loop(0, rows // chunk, body, 0)
-
-
-def first_kernel(routing, state, past, weight, bias, mix, gated, second, send, *, gate):
-    convolve(past, state, weight, bias, mix, gated, second, gate)
-    fill_send(routing, second, send)
+def convolve(past, state, weight, bias, gated):
+    gate = gated.shape[1]
+    part = 512
+    for i in range(state.shape[0] // part):
+        at = pl.ds(i * part, part)
+        both = jnp.concatenate([past[at, :], state[at, :]], axis=1)
+        pre = dot(both, weight[...]) + bias[...]
+        value = jnp.tanh(pre[:, :gate]) * (0.5 * jnp.tanh(0.5 * pre[:, gate:]) + 0.5)
+        gated[at, :] = value.astype(BF16)
+
+
+def conv_loads(layer, past_all, weight_all, bias_all, mix_all, past, weight, bias, mix, sems):
+    depth = mix.shape[0]
+    return [
+        start(weight_all.at[layer], weight, sems.at[0]),
+        start(past_all.at[layer], past, sems.at[1]),
+        start(bias_all.at[pl.ds(layer, 1), :], bias, sems.at[2]),
+        start(mix_all.at[layer, pl.ds(2 * depth, depth), :], mix, sems.at[3]),
+    ]
+
+
+def conv_finish(routing, mix, gated, second, gated_out, second_out, send, sems):
+    second[...] = dot(gated[...], mix[...]).astype(BF16)
+    copies = [
+        start_send(routing, second, send, sems.at[4]),
+        start(gated, gated_out, sems.at[5]),
+        start(second, second_out, sems.at[6]),
+    ]
+    for copy in copies:
+        copy.wait()
+
+
+def first_kernel(
+    routing, state_in, past_all, weight_all, bias_all, mix_all,
+    gated_out, second_out, send,
+    past, weight, bias, mix, gated, second, state, sems, *, layer,
+):
+    loads = conv_loads(layer, past_all, weight_all, bias_all, mix_all, past, weight, bias, mix, sems)
+    loads.append(start(state_in, state, sems.at[7]))
+    for copy in loads:
+        copy.wait()
+    convolve(past, state, weight, bias, gated)
+    conv_finish(routing, mix, gated, second, gated_out, second_out, send, sems)
 
 
 def next_kernel(
-    routing, table, blocks, far, total_in, past, weight, bias, mix,
-    state, gated, second, send, total, *, gate,
+    routing, table, blocks, far, total_in, past_all, weight_all, bias_all, mix_all,
+    gated_out, second_out, send, state_out,
+    past, weight, bias, mix, gated, second, state, total, sems, *, layer,
 ):
-    total[...] = total_in[...]
+    first = start(total_in, total, sems.at[7])
+    loads = conv_loads(layer, past_all, weight_all, bias_all, mix_all, past, weight, bias, mix, sems)
+    first.wait()
     add_remote(table, blocks, far, total)
     state[...] = total[...].astype(BF16)
-    convolve(past, state, weight, bias, mix, gated, second, gate)
-    fill_send(routing, second, send)
-
-
-def hop_kernel(routing, table, blocks, far, total_in, field, send, total):
-    total[...] = total_in[...]
+    for copy in loads:
+        copy.wait()
+    convolve(past, state, weight, bias, gated)
+    last = start(state, state_out, sems.at[7])
+    conv_finish(routing, mix, gated, second, gated_out, second_out, send, sems)
+    last.wait()
+
+
+def hop_kernel(routing, table, blocks, far, total_in, field_out, send, field, total, sems):
+    start(total_in, total, sems.at[0]).wait()
     add_remote(table, blocks, far, total)
     field[...] = total[...].astype(BF16)
-    fill_send(routing, field, send)
-
-
-def last_kernel(table, blocks, far, total_in, state, total):
-    total[...] = total_in[...]
+    copies = [start_send(routing, field, send, sems.at[1]), start(field, field_out, sems.at[2])]
+    for copy in copies:
+        copy.wait()
+
+
+def last_kernel(table, blocks, far, total_in, state_out, state, total, sems):
+    start(total_in, total, sems.at[0]).wait()
     add_remote(table, blocks, far, total)
     state[...] = total[...].astype(BF16)
+    start(state, state_out, sems.at[1]).wait()
 
 
 def build_kernel(place, target, owner, slot, values, table, local, remote_blocks, *, tiles):
@@ -134,17 +172,27 @@
 
 
 def under_first_kernel(
-    local, values, gated, second, wide, skip_in, total, base, skip, *, res
+    local, values, gated, second, mix_all, skip_all, *rest, res, layer
 ):
+    skip_in = rest[0] if layer else None
+    total, base, skip, wide, sems = rest[1 if layer else 0 :]
+    gate = gated.shape[1]
+    loads = [
+        start(mix_all.at[layer, pl.ds(gate, gate), :], wide.at[:, pl.ds(0, res)], sems.at[0]),
+        start(mix_all.at[layer, pl.ds(0, gate), :], wide.at[:, pl.ds(res, res)], sems.at[1]),
+        start(skip_all.at[layer], wide.at[:, pl.ds(2 * res, skip.shape[1])], sems.at[2]),
+    ]
+    for copy in loads:
+        copy.wait()
     for t in range(gated.shape[0] // TILE):
         at = pl.ds(t * TILE, TILE)
         out = dot(gated[at, :], wide[...])
         total[at, :] = out[:, :res] + local_sum(local, values, second, t)
         base[at, :] = out[:, res : 2 * res]
-        if skip_in is None:
-            skip[at, :] = out[:, 2 * res :].astype(skip.dtype)
-        else:
-            skip[at, :] = (skip_in[at, :] + out[:, 2 * res :]).astype(skip.dtype)
+        gain = out[:, 2 * res :]
+        if layer:
+            gain = gain + skip_in[at, :]
+        skip[at, :] = gain.astype(skip.dtype)
 
 
 def under_second_kernel(local, values, field, base, state, total):
@@ -207,52 +255,51 @@
         shape((rows, res), BF16),
         shape((slots, TILE, res), BF16),
     )
+    conv_scratch = [
+        pltpu.VMEM((rows, res), BF16),
+        pltpu.VMEM((2 * res, 2 * gate), BF16),
+        pltpu.VMEM((1, 2 * gate), F32),
+        pltpu.VMEM((gate, res), BF16),
+        pltpu.VMEM((rows, gate), BF16),
+        pltpu.VMEM((rows, res), BF16),
+        pltpu.VMEM((rows, res), BF16),
+    ]
+    wide_field = pltpu.VMEM((rows, res), F32)
+    thin_field = pltpu.VMEM((rows, res), BF16)
+    weights = (conv_cache, conv_weight, conv_bias, mix_weight)
     state = hidden_state
     skip = None
     total = far = None
     for layer in range(layers):
-        mixing = mix_weight[layer]
-        weight, bias = conv_weight[layer], conv_bias[layer][None, :]
-        wide = jnp.concatenate(
-            [mixing[gate : 2 * gate], mixing[:gate], skip_weight[layer]], axis=1
-        )
-        deep = mixing[2 * gate :]
         if layer == 0:
             gated, second, send = call(
-                functools.partial(first_kernel, gate=gate),
+                functools.partial(first_kernel, layer=layer),
                 "conv_first",
-                (routing, state, conv_cache[layer], weight, bias, deep),
+                (routing, state) + weights,
                 conv_outs,
-                [SMEM] + [VMEM] * 5,
-                [VMEM] * 3,
+                [SMEM] + [HBM] * 5,
+                [HBM] * 3,
                 conv_flops,
+                conv_scratch + [pltpu.SemaphoreType.DMA((8,))],
             )
         else:
-            state, gated, second, send = call(
-                functools.partial(next_kernel, gate=gate),
+            gated, second, send, state = call(
+                functools.partial(next_kernel, layer=layer),
                 "conv_next",
-                (routing, table, remote_blocks, far, total, conv_cache[layer], weight, bias, deep),
-                (shape((rows, res), BF16),) + conv_outs,
-                [SMEM] * 2 + [VMEM] * 7,
-                [VMEM] * 4,
+                (routing, table, remote_blocks, far, total) + weights,
+                conv_outs + (shape((rows, res), BF16),),
+                [SMEM] * 2 + [VMEM] * 2 + [HBM] * 5,
+                [HBM] * 4,
                 conv_flops + hop_flops,
-                [pltpu.VMEM((rows, res), F32)],
+                conv_scratch + [wide_field, pltpu.SemaphoreType.DMA((8,))],
             )
         far = exchange(send)
         last = layer == layers - 1
-        first_ins = (local_table, block_values, gated, second, wide)
-        kernel = functools.partial(under_first_kernel, res=res)
-        if layer == 0:
-            ins = first_ins
-
-            def body(l, v, g, s, w, t, b, k):
-                under_first_kernel(l, v, g, s, w, None, t, b, k, res=res)
-
-        else:
-            ins = first_ins + (skip,)
-            body = kernel
+        ins = (local_table, block_values, gated, second, mix_weight, skip_weight)
+        if layer:
+            ins += (skip,)
         total, base, skip = call(
-            body,
+            functools.partial(under_first_kernel, res=res, layer=layer),
             "under_first",
             ins,
             (
@@ -260,19 +307,20 @@
                 shape((rows, res), F32),
                 shape((rows, skips), BF16 if last else F32),
             ),
-            [SMEM] + [VMEM] * (len(ins) - 1),
+            [SMEM] + [VMEM] * 3 + [HBM] * 2 + [VMEM] * (len(ins) - 6),
             [VMEM] * 3,
             2 * rows * gate * (2 * res + skips) + 4 * rows * TILE * res,
+            [pltpu.VMEM((gate, 2 * res + skips), BF16), pltpu.SemaphoreType.DMA((3,))],
         )
         field, send = call(
             hop_kernel,
             "hop",
             (routing, table, remote_blocks, far, total),
             (shape((rows, res), BF16), shape((slots, TILE, res), BF16)),
-            [SMEM] * 2 + [VMEM] * 3,
-            [VMEM] * 2,
+            [SMEM] * 2 + [VMEM] * 2 + [HBM],
+            [HBM] * 2,
             hop_flops,
-            [pltpu.VMEM((rows, res), F32)],
+            [thin_field, wide_field, pltpu.SemaphoreType.DMA((3,))],
         )
         far = exchange(send)
         (total,) = call(
@@ -289,10 +337,10 @@
         "last",
         (table, remote_blocks, far, total),
         (shape((rows, res), BF16),),
-        [SMEM] + [VMEM] * 3,
-        [VMEM],
+        [SMEM] + [VMEM] * 2 + [HBM],
+        [HBM],
         hop_flops,
-        [pltpu.VMEM((rows, res), F32)],
+        [thin_field, wide_field, pltpu.SemaphoreType.DMA((2,))],
     )
     return state, skip
 

time: 231 us -> 221 us (0.957)
  local copies, waits for them, and re-layouts: 54.4 us -> 7.2 us
  Pallas kernels: 34 us -> 63.6 us
  waiting for transfers between devices: 106 us -> 117 us
    unnamed x119 -> x13, local copies, waits for them, and re-layouts: 48 us -> 6.59 us
    pallas_call x14, Pallas kernels: 34 us -> 63.6 us  [call(): pl.pallas_call(kernel, name=name, out_shape=tuple(outs), in_specs=in_spec...]
    all_to_all x6, waiting for transfers between devices: 106 us -> 117 us  [exchange(): lax.all_to_all(send.reshape(peers, CAP, TILE, res), 'node', split_axis=0,...]
    squeeze x3 -> x0, local copies, waits for them, and re-layouts: 3.53 us -> none  [the longest x1 1.71 us: local(): skip_weight[layer]]
    slice x2 -> x0, local copies, waits for them, and re-layouts: 2.81 us -> none  [the longest x1 2 us: local(): mixing[gate:2 * gate]]
  transfers between devices with their start and end apart: 6 -> 6, of which waited for: 6 -> 6; matrix products, arithmetic and copies ran while one was open for 1% -> 0% of each run, Pallas kernels for 7% -> 14%
where the time goes in v2:
time: 221 us; the launch traced here: 220 us
  waiting for transfers between devices  117 us (53%)
  Pallas kernels  63.6 us (29%)
  starting transfers between devices  31.5 us (14%)
  local copies, waits for them, and re-layouts  7.2 us (3%)
    all_to_all x6, waiting for transfers between devices, exchange(): lax.all_to_all(send.reshape(peers, CAP, TILE, res), 'node', split_axis=0,...  117 us
    pallas_call x14, Pallas kernels, call(): pl.pallas_call(kernel, name=name, out_shape=tuple(outs), in_specs=in_spec...  63.6 us
    all_to_all x6, starting transfers between devices, exchange(): lax.all_to_all(send.reshape(peers, CAP, TILE, res), 'node', split_axis=0,...  31.5 us
    unnamed x13, local copies, waits for them, and re-layouts  6.59 us
  transfers between devices with their start and end apart: 6, of which 6 were waited for; matrix products, arithmetic and copies ran while one was open for 0% of the time, Pallas kernels for 14%

profile of v2, /device:TPU:9, one launch (start us, length us, event | category | flops | bytes accessed | tf_op | source)
XLA Modules:
  0.0 220.2 jit_solution(15586517724396119962)
XLA Ops:
  2.0 4.5 %conv_first.1 = (bf16[2048,256]{1,0:T(8,128)(2,1)}, bf16[2048,128]{1,0:T(8,128)(2,1)}, bf16[32,128,128]{2,1,0:T(8,128)(2,1)}) custom-call(s32[32]{0:T(128)} %reshape.43.routing, bf16[2048,128]{1,0:T(8,128)(2,1)} %state.1, bf16[3,2048,128]{2,1,0:T(8,128)(2,1)} %past_all.5, bf16[3,256,512]{2,1,0:T(8,128)(2,1)} %weight_all.5, f32[3,512]{1,0:T(4,128)} %bias_all.5, ...), custom_call_target="tpu_custom_call" | custom-call | flops 671088640 | bytes 6101120 | tf_op jit(solution)/shard_map/conv_first/pallas_call | solution.py:28
  6.5 6.6 %all-to-all-start = ((bf16[16,2,128,128]{3,2,1,0:T(8,128)(2,1)}), bf16[16,2,128,128]{3,2,1,0:T(8,128)(2,1)S(1)}, u32[]{:S(2)}, u32[]{:S(2)}) async-start(bf16[16,2,128,128]{3,2,1,0:T(8,128)(2,1)} %bitcast.19), calls=%async_computation | async-start | bytes 2097152 | tf_op jit(solution)/shard_map/all_to_all | solution.py:246
  13.1 3.0 %sort_blocks.1 = (s32[2,15]{1,0:T(2,128)}, s32[4,16]{1,0:T(4,128)}, bf16[15,128,128]{2,1,0:T(8,128)(2,1)}) custom-call(s32[1]{0:T(128)} %bitcast.place, s32[47]{0:T(128)} %target.1, s32[47]{0:T(128)} %owner.1, s32[47]{0:T(128)} %slot.1, bf16[47,128,128]{2,1,0:T(8,128)(2,1)} %values.13), custom_call_target="tpu_custom_call" | custom-call | flops 47000 | bytes 2032560 | tf_op jit(solution)/shard_map/sort_blocks/pallas_call | solution.py:28
  16.2 5.8 %under_first.3 = (f32[2048,128]{1,0:T(8,128)}, f32[2048,128]{1,0:T(8,128)}, f32[2048,256]{1,0:T(8,128)}) custom-call(s32[4,16]{1,0:T(4,128)} %get-tuple-element.34.local, bf16[47,128,128]{2,1,0:T(8,128)(2,1)} %values.13, bf16[2048,256]{1,0:T(8,128)(2,1)} %get-tuple-element.35.gated, bf16[2048,128]{1,0:T(8,128)(2,1)} %get-tuple-element.36.second, ...), custom_call_target="tpu_custom_call" | custom-call | flops 671088640 | bytes 8290560 | tf_op jit(solution)/shard_map/under_first/pallas_call | solution.py:28
  22.0 16.0 %all-to-all-done = bf16[16,2,128,128]{3,2,1,0:T(8,128)(2,1)S(1)} async-done(((bf16[16,2,128,128]{3,2,1,0:T(8,128)(2,1)}), bf16[16,2,128,128]{3,2,1,0:T(8,128)(2,1)S(1)}, u32[]{:S(2)}, u32[]{:S(2)}) %all-to-all-start) | async-done | bytes 1048608 | tf_op jit(solution)/shard_map/all_to_all | solution.py:246
  38.0 1.0 copy-done.2
  39.0 4.1 %hop.3 = (bf16[2048,128]{1,0:T(8,128)(2,1)}, bf16[32,128,128]{2,1,0:T(8,128)(2,1)}) custom-call(s32[32]{0:T(128)} %reshape.43.routing, s32[2,15]{1,0:T(2,128)} %get-tuple-element.31.table, bf16[15,128,128]{2,1,0:T(8,128)(2,1)} %get-tuple-element.32.blocks, bf16[32,128,128]{2,1,0:T(8,128)(2,1)} %bitcast.15, f32[2048,128]{1,0:T(8,128)} %get-tuple-element.37.total_in), custom_call_target="tpu_custom_call" | custom-call | flops 62914560 | bytes 4161784 | tf_op jit(solution)/shard_map/hop/pallas_call | solution.py:28
  43.1 5.0 %all-to-all-start.1 = ((bf16[16,2,128,128]{3,2,1,0:T(8,128)(2,1)}), bf16[16,2,128,128]{3,2,1,0:T(8,128)(2,1)S(1)}, u32[]{:S(2)}, u32[]{:S(2)}) async-start(bf16[16,2,128,128]{3,2,1,0:T(8,128)(2,1)} %bitcast.24), calls=%async_computation.1 | async-start | bytes 2097152 | tf_op jit(solution)/shard_map/all_to_all | solution.py:246
  48.1 3.5 %under_second.3.total_in = f32[2048,128]{1,0:T(8,128)} custom-call(s32[4,16]{1,0:T(4,128)} %get-tuple-element.34.local, bf16[47,128,128]{2,1,0:T(8,128)(2,1)} %values.13, bf16[2048,128]{1,0:T(8,128)(2,1)} %get-tuple-element.39.field, f32[2048,128]{1,0:T(8,128)} %get-tuple-element.40.base, bf16[2048,128]{1,0:T(8,128)(2,1)} %state.1), custom_call_target="tpu_custom_call" | custom-call | flops 134217728 | bytes 4686080 | tf_op jit(solution)/shard_map/under_second/pallas_call | solution.py:28
  51.5 21.4 %all-to-all-done.1 = bf16[16,2,128,128]{3,2,1,0:T(8,128)(2,1)S(1)} async-done(((bf16[16,2,128,128]{3,2,1,0:T(8,128)(2,1)}), bf16[16,2,128,128]{3,2,1,0:T(8,128)(2,1)S(1)}, u32[]{:S(2)}, u32[]{:S(2)}) %all-to-all-start.1) | async-done | bytes 1048608 | tf_op jit(solution)/shard_map/all_to_all | solution.py:246
  72.9 1.0 copy-done.1
  73.9 5.5 %conv_next.2 = (bf16[2048,256]{1,0:T(8,128)(2,1)}, bf16[2048,128]{1,0:T(8,128)(2,1)}, bf16[32,128,128]{2,1,0:T(8,128)(2,1)}, bf16[2048,128]{1,0:T(8,128)(2,1)}) custom-call(s32[32]{0:T(128)} %reshape.43.routing, s32[2,15]{1,0:T(2,128)} %get-tuple-element.31.table, bf16[15,128,128]{2,1,0:T(8,128)(2,1)} %get-tuple-element.32.blocks, ...), custom_call_target="tpu_custom_call" | custom-call | flops 734003200 | bytes 8689912 | tf_op jit(solution)/shard_map/conv_next/pallas_call | solution.py:28
  79.4 5.0 %all-to-all-start.2 = ((bf16[16,2,128,128]{3,2,1,0:T(8,128)(2,1)}), bf16[16,2,128,128]{3,2,1,0:T(8,128)(2,1)S(1)}, u32[]{:S(2)}, u32[]{:S(2)}) async-start(bf16[16,2,128,128]{3,2,1,0:T(8,128)(2,1)} %bitcast.20), calls=%async_computation.2 | async-start | bytes 2097152 | tf_op jit(solution)/shard_map/all_to_all | solution.py:246
  84.4 6.5 %under_first.4 = (f32[2048,128]{1,0:T(8,128)}, f32[2048,128]{1,0:T(8,128)}, f32[2048,256]{1,0:T(8,128)}) custom-call(s32[4,16]{1,0:T(4,128)} %get-tuple-element.34.local, bf16[47,128,128]{2,1,0:T(8,128)(2,1)} %values.13, bf16[2048,256]{1,0:T(8,128)(2,1)} %get-tuple-element.42.gated, bf16[2048,128]{1,0:T(8,128)(2,1)} %get-tuple-element.43.second, ...), custom_call_target="tpu_custom_call" | custom-call | flops 671088640 | bytes 10387712 | tf_op jit(solution)/shard_map/under_first/pallas_call | solution.py:28
  91.0 18.3 %all-to-all-done.2 = bf16[16,2,128,128]{3,2,1,0:T(8,128)(2,1)S(1)} async-done(((bf16[16,2,128,128]{3,2,1,0:T(8,128)(2,1)}), bf16[16,2,128,128]{3,2,1,0:T(8,128)(2,1)S(1)}, u32[]{:S(2)}, u32[]{:S(2)}) %all-to-all-start.2) | async-done | bytes 1048608 | tf_op jit(solution)/shard_map/all_to_all | solution.py:246
  109.3 1.0 copy-done.4
  110.2 4.1 %hop.4 = (bf16[2048,128]{1,0:T(8,128)(2,1)}, bf16[32,128,128]{2,1,0:T(8,128)(2,1)}) custom-call(s32[32]{0:T(128)} %reshape.43.routing, s32[2,15]{1,0:T(2,128)} %get-tuple-element.31.table, bf16[15,128,128]{2,1,0:T(8,128)(2,1)} %get-tuple-element.32.blocks, bf16[32,128,128]{2,1,0:T(8,128)(2,1)} %bitcast.17, f32[2048,128]{1,0:T(8,128)} %get-tuple-element.45.total_in), custom_call_target="tpu_custom_call" | custom-call | flops 62914560 | bytes 4161784 | tf_op jit(solution)/shard_map/hop/pallas_call | solution.py:28
  114.4 5.0 %all-to-all-start.3 = ((bf16[16,2,128,128]{3,2,1,0:T(8,128)(2,1)}), bf16[16,2,128,128]{3,2,1,0:T(8,128)(2,1)S(1)}, u32[]{:S(2)}, u32[]{:S(2)}) async-start(bf16[16,2,128,128]{3,2,1,0:T(8,128)(2,1)} %bitcast.23), calls=%async_computation.3 | async-start | bytes 2097152 | tf_op jit(solution)/shard_map/all_to_all | solution.py:246
  119.3 3.4 %under_second.4.total_in = f32[2048,128]{1,0:T(8,128)} custom-call(s32[4,16]{1,0:T(4,128)} %get-tuple-element.34.local, bf16[47,128,128]{2,1,0:T(8,128)(2,1)} %values.13, bf16[2048,128]{1,0:T(8,128)(2,1)} %get-tuple-element.47.field, f32[2048,128]{1,0:T(8,128)} %get-tuple-element.48.base, bf16[2048,128]{1,0:T(8,128)(2,1)} %get-tuple-element.49.state), custom_call_target="tpu_custom_call" | custom-call | flops 134217728 | bytes 4686080 | tf_op jit(solution)/shard_map/under_second/pallas_call | solution.py:28
  122.8 21.4 %all-to-all-done.3 = bf16[16,2,128,128]{3,2,1,0:T(8,128)(2,1)S(1)} async-done(((bf16[16,2,128,128]{3,2,1,0:T(8,128)(2,1)}), bf16[16,2,128,128]{3,2,1,0:T(8,128)(2,1)S(1)}, u32[]{:S(2)}, u32[]{:S(2)}) %all-to-all-start.3) | async-done | bytes 1048608 | tf_op jit(solution)/shard_map/all_to_all | solution.py:246
  144.2 1.0 copy-done
  145.2 5.5 %conv_next.3 = (bf16[2048,256]{1,0:T(8,128)(2,1)}, bf16[2048,128]{1,0:T(8,128)(2,1)}, bf16[32,128,128]{2,1,0:T(8,128)(2,1)}, bf16[2048,128]{1,0:T(8,128)(2,1)}) custom-call(s32[32]{0:T(128)} %reshape.43.routing, s32[2,15]{1,0:T(2,128)} %get-tuple-element.31.table, bf16[15,128,128]{2,1,0:T(8,128)(2,1)} %get-tuple-element.32.blocks, ...), custom_call_target="tpu_custom_call" | custom-call | flops 734003200 | bytes 8689912 | tf_op jit(solution)/shard_map/conv_next/pallas_call | solution.py:28
  150.7 5.0 %all-to-all-start.4 = ((bf16[16,2,128,128]{3,2,1,0:T(8,128)(2,1)}), bf16[16,2,128,128]{3,2,1,0:T(8,128)(2,1)S(1)}, u32[]{:S(2)}, u32[]{:S(2)}) async-start(bf16[16,2,128,128]{3,2,1,0:T(8,128)(2,1)} %bitcast.21), calls=%async_computation.4 | async-start | bytes 2097152 | tf_op jit(solution)/shard_map/all_to_all | solution.py:246
  155.7 6.2 %under_first.5 = (f32[2048,128]{1,0:T(8,128)}, f32[2048,128]{1,0:T(8,128)}, bf16[2048,256]{1,0:T(8,128)(2,1)}) custom-call(s32[4,16]{1,0:T(4,128)} %get-tuple-element.34.local, bf16[47,128,128]{2,1,0:T(8,128)(2,1)} %values.13, bf16[2048,256]{1,0:T(8,128)(2,1)} %get-tuple-element.51.gated, bf16[2048,128]{1,0:T(8,128)(2,1)} %get-tuple-element.52.second, ...), custom_call_target="tpu_custom_call" | custom-call | flops 671088640 | bytes 9339136 | tf_op jit(solution)/shard_map/under_first/pallas_call | solution.py:28
  161.9 18.7 %all-to-all-done.4 = bf16[16,2,128,128]{3,2,1,0:T(8,128)(2,1)S(1)} async-done(((bf16[16,2,128,128]{3,2,1,0:T(8,128)(2,1)}), bf16[16,2,128,128]{3,2,1,0:T(8,128)(2,1)S(1)}, u32[]{:S(2)}, u32[]{:S(2)}) %all-to-all-start.4) | async-done | bytes 1048608 | tf_op jit(solution)/shard_map/all_to_all | solution.py:246
  180.5 0.9 copy-done.3
  181.5 4.1 %hop.5 = (bf16[2048,128]{1,0:T(8,128)(2,1)}, bf16[32,128,128]{2,1,0:T(8,128)(2,1)}) custom-call(s32[32]{0:T(128)} %reshape.43.routing, s32[2,15]{1,0:T(2,128)} %get-tuple-element.31.table, bf16[15,128,128]{2,1,0:T(8,128)(2,1)} %get-tuple-element.32.blocks, bf16[32,128,128]{2,1,0:T(8,128)(2,1)} %bitcast.16, f32[2048,128]{1,0:T(8,128)} %get-tuple-element.54.total_in), custom_call_target="tpu_custom_call" | custom-call | flops 62914560 | bytes 4161784 | tf_op jit(solution)/shard_map/hop/pallas_call | solution.py:28
  185.6 5.0 %all-to-all-start.5 = ((bf16[16,2,128,128]{3,2,1,0:T(8,128)(2,1)}), bf16[16,2,128,128]{3,2,1,0:T(8,128)(2,1)S(1)}, u32[]{:S(2)}, u32[]{:S(2)}) async-start(bf16[16,2,128,128]{3,2,1,0:T(8,128)(2,1)} %bitcast.22), calls=%async_computation.5 | async-start | bytes 2097152 | tf_op jit(solution)/shard_map/all_to_all | solution.py:246
  190.6 3.4 %under_second.5.total_in = f32[2048,128]{1,0:T(8,128)} custom-call(s32[4,16]{1,0:T(4,128)} %get-tuple-element.34.local, bf16[47,128,128]{2,1,0:T(8,128)(2,1)} %values.13, bf16[2048,128]{1,0:T(8,128)(2,1)} %get-tuple-element.56.field, f32[2048,128]{1,0:T(8,128)} %get-tuple-element.57.base, bf16[2048,128]{1,0:T(8,128)(2,1)} %get-tuple-element.58.state), custom_call_target="tpu_custom_call" | custom-call | flops 134217728 | bytes 4686080 | tf_op jit(solution)/shard_map/under_second/pallas_call | solution.py:28
  194.0 21.5 %all-to-all-done.5 = bf16[16,2,128,128]{3,2,1,0:T(8,128)(2,1)S(1)} async-done(((bf16[16,2,128,128]{3,2,1,0:T(8,128)(2,1)}), bf16[16,2,128,128]{3,2,1,0:T(8,128)(2,1)S(1)}, u32[]{:S(2)}, u32[]{:S(2)}) %all-to-all-start.5) | async-done | bytes 1048608 | tf_op jit(solution)/shard_map/all_to_all | solution.py:246
  215.4 1.0 copy-done.5
  216.4 3.8 %last.1 = bf16[2048,128]{1,0:T(8,128)(2,1)} custom-call(s32[2,15]{1,0:T(2,128)} %get-tuple-element.31.table, bf16[15,128,128]{2,1,0:T(8,128)(2,1)} %get-tuple-element.32.blocks, bf16[32,128,128]{2,1,0:T(8,128)(2,1)} %bitcast.18, f32[2048,128]{1,0:T(8,128)} %under_second.5.total_in), custom_call_target="tpu_custom_call" | custom-call | flops 62914560 | bytes 3113080 | tf_op jit(solution)/shard_map/last/pallas_call | solution.py:28
  (8 shorter events, 1.4 us)
Async XLA Ops:
  6.5 31.5 %all-to-all-start = ((bf16[16,2,128,128]{3,2,1,0:T(8,128)(2,1)}), bf16[16,2,128,128]{3,2,1,0:T(8,128)(2,1)S(1)}, u32[]{:S(2)}, u32[]{:S(2)}) async-start(bf16[16,2,128,128]{3,2,1,0:T(8,128)(2,1)} %bitcast.19), calls=%async_computation | async-start | bytes 2097152 | tf_op jit(solution)/shard_map/all_to_all | solution.py:246
  38.0 1.0 copy-start.2
  43.1 29.8 %all-to-all-start.1 = ((bf16[16,2,128,128]{3,2,1,0:T(8,128)(2,1)}), bf16[16,2,128,128]{3,2,1,0:T(8,128)(2,1)S(1)}, u32[]{:S(2)}, u32[]{:S(2)}) async-start(bf16[16,2,128,128]{3,2,1,0:T(8,128)(2,1)} %bitcast.24), calls=%async_computation.1 | async-start | bytes 2097152 | tf_op jit(solution)/shard_map/all_to_all | solution.py:246
  72.9 1.0 copy-start.1
  79.4 29.8 %all-to-all-start.2 = ((bf16[16,2,128,128]{3,2,1,0:T(8,128)(2,1)}), bf16[16,2,128,128]{3,2,1,0:T(8,128)(2,1)S(1)}, u32[]{:S(2)}, u32[]{:S(2)}) async-start(bf16[16,2,128,128]{3,2,1,0:T(8,128)(2,1)} %bitcast.20), calls=%async_computation.2 | async-start | bytes 2097152 | tf_op jit(solution)/shard_map/all_to_all | solution.py:246
  109.3 1.0 copy-start.4
  114.4 29.8 %all-to-all-start.3 = ((bf16[16,2,128,128]{3,2,1,0:T(8,128)(2,1)}), bf16[16,2,128,128]{3,2,1,0:T(8,128)(2,1)S(1)}, u32[]{:S(2)}, u32[]{:S(2)}) async-start(bf16[16,2,128,128]{3,2,1,0:T(8,128)(2,1)} %bitcast.23), calls=%async_computation.3 | async-start | bytes 2097152 | tf_op jit(solution)/shard_map/all_to_all | solution.py:246
  144.2 1.0 copy-start
  150.7 29.8 %all-to-all-start.4 = ((bf16[16,2,128,128]{3,2,1,0:T(8,128)(2,1)}), bf16[16,2,128,128]{3,2,1,0:T(8,128)(2,1)S(1)}, u32[]{:S(2)}, u32[]{:S(2)}) async-start(bf16[16,2,128,128]{3,2,1,0:T(8,128)(2,1)} %bitcast.21), calls=%async_computation.4 | async-start | bytes 2097152 | tf_op jit(solution)/shard_map/all_to_all | solution.py:246
  180.5 0.9 copy-start.3
  185.6 29.8 %all-to-all-start.5 = ((bf16[16,2,128,128]{3,2,1,0:T(8,128)(2,1)}), bf16[16,2,128,128]{3,2,1,0:T(8,128)(2,1)S(1)}, u32[]{:S(2)}, u32[]{:S(2)}) async-start(bf16[16,2,128,128]{3,2,1,0:T(8,128)(2,1)} %bitcast.22), calls=%async_computation.5 | async-start | bytes 2097152 | tf_op jit(solution)/shard_map/all_to_all | solution.py:246
  215.4 1.0 copy-start.5

commit v3 on v2

--- a/solution.py
+++ b/solution.py
@@ -13,8 +13,9 @@
 BF16 = jnp.bfloat16
 VMEM = pl.BlockSpec(memory_space=pltpu.VMEM)
 SMEM = pl.BlockSpec(memory_space=pltpu.SMEM)
-HBM = pl.BlockSpec(memory_space=pltpu.HBM)
-LIMIT = 60 << 20
+HBM = pl.BlockSpec(memory_space=pl.ANY)
+LIMITS = {"conv_first": 60}
+PART = 512
 
 
 def dot(a, b):
@@ -33,7 +34,7 @@
         out_specs=tuple(out_specs),
         scratch_shapes=scratch,
         input_output_aliases=alias or {},
-        compiler_params=pltpu.CompilerParams(vmem_limit_bytes=LIMIT),
+        compiler_params=pltpu.CompilerParams(vmem_limit_bytes=LIMITS.get(name, 52) << 20),
         cost_estimate=pl.CostEstimate(flops=flops, bytes_accessed=moved, transcendentals=0),
     )(*ins)
 
@@ -55,89 +56,131 @@
     return pltpu.make_async_copy(send, send, sem)
 
 
-def add_remote(table, blocks, far, total):
+def start_parts(source, target, sem, parts):
+    step = source.shape[0] // parts
+    for i in range(parts):
+        at = pl.ds(i * step, step)
+        start(source.at[at, :], target.at[at, :], sem)
+    return pltpu.make_async_copy(source, target, sem)
+
+
+def start_far(table, far, near, sem):
+    for j in range(near.shape[0]):
+        start(far.at[table[1, j]], near.at[j], sem)
+    return pltpu.make_async_copy(near, near, sem)
+
+
+def add_remote(table, blocks, near, total):
     for j in range(blocks.shape[0]):
         rows = pl.ds(pl.multiple_of(table[0, j] * TILE, TILE), TILE)
-        total[rows, :] += dot(blocks[j], far[table[1, j]])
-
-
-def convolve(past, state, weight, bias, gated):
+        total[rows, :] += dot(blocks[j], near[j])
+
+
+def convolve(past, state, weight, bias, gated, gated_out, sem, ready=None):
     gate = gated.shape[1]
-    part = 512
-    for i in range(state.shape[0] // part):
-        at = pl.ds(i * part, part)
+    for i in range(state.shape[0] // PART):
+        at = pl.ds(i * PART, PART)
+        if ready is not None:
+            ready(i)
         both = jnp.concatenate([past[at, :], state[at, :]], axis=1)
         pre = dot(both, weight[...]) + bias[...]
         value = jnp.tanh(pre[:, :gate]) * (0.5 * jnp.tanh(0.5 * pre[:, gate:]) + 0.5)
         gated[at, :] = value.astype(BF16)
-
-
-def conv_loads(layer, past_all, weight_all, bias_all, mix_all, past, weight, bias, mix, sems):
+        start(gated.at[at, :], gated_out.at[at, :], sem)
+    return pltpu.make_async_copy(gated, gated_out, sem)
+
+
+def weight_loads(layer, weight_all, bias_all, mix_all, weight, bias, mix, sems):
     depth = mix.shape[0]
     return [
         start(weight_all.at[layer], weight, sems.at[0]),
-        start(past_all.at[layer], past, sems.at[1]),
-        start(bias_all.at[pl.ds(layer, 1), :], bias, sems.at[2]),
-        start(mix_all.at[layer, pl.ds(2 * depth, depth), :], mix, sems.at[3]),
-    ]
-
-
-def conv_finish(routing, mix, gated, second, gated_out, second_out, send, sems):
-    second[...] = dot(gated[...], mix[...]).astype(BF16)
-    copies = [
-        start_send(routing, second, send, sems.at[4]),
-        start(gated, gated_out, sems.at[5]),
-        start(second, second_out, sems.at[6]),
-    ]
-    for copy in copies:
-        copy.wait()
+        start(bias_all.at[pl.ds(layer, 1), :], bias, sems.at[1]),
+        start(mix_all.at[layer, pl.ds(2 * depth, depth), :], mix, sems.at[2]),
+    ]
 
 
 def first_kernel(
     routing, state_in, past_all, weight_all, bias_all, mix_all,
-    gated_out, second_out, send,
-    past, weight, bias, mix, gated, second, state, sems, *, layer,
+    gated_out, send,
+    past, weight, bias, mix, gated, second, state, sems, parts, *, layer,
 ):
-    loads = conv_loads(layer, past_all, weight_all, bias_all, mix_all, past, weight, bias, mix, sems)
-    loads.append(start(state_in, state, sems.at[7]))
-    for copy in loads:
-        copy.wait()
-    convolve(past, state, weight, bias, gated)
-    conv_finish(routing, mix, gated, second, gated_out, second_out, send, sems)
+    loads = weight_loads(layer, weight_all, bias_all, mix_all, weight, bias, mix, sems)
+    pieces = []
+    for i in range(state.shape[0] // PART):
+        at = pl.ds(i * PART, PART)
+        pieces.append(
+            (
+                start(past_all.at[layer, at, :], past.at[at, :], parts.at[2 * i]),
+                start(state_in.at[at, :], state.at[at, :], parts.at[2 * i + 1]),
+            )
+        )
+
+    def ready(i):
+        if i == 0:
+            for copy in loads:
+                copy.wait()
+        for copy in pieces[i]:
+            copy.wait()
+
+    copies = [convolve(past, state, weight, bias, gated, gated_out, sems.at[3], ready)]
+    second[...] = dot(gated[...], mix[...]).astype(BF16)
+    copies.append(start_send(routing, second, send, sems.at[4]))
+    for copy in copies:
+        copy.wait()
 
 
 def next_kernel(
     routing, table, blocks, far, total_in, past_all, weight_all, bias_all, mix_all,
-    gated_out, second_out, send, state_out,
-    past, weight, bias, mix, gated, second, state, total, sems, *, layer,
+    gated_out, send, state_out,
+    past, weight, bias, mix, gated, second, state, near, total, sems, *, layer,
 ):
-    first = start(total_in, total, sems.at[7])
-    loads = conv_loads(layer, past_all, weight_all, bias_all, mix_all, past, weight, bias, mix, sems)
-    first.wait()
-    add_remote(table, blocks, far, total)
+    inputs = [
+        start_far(table, far, near, sems.at[5]),
+        start_parts(total_in, total, sems.at[6], 4),
+    ]
+    loads = weight_loads(layer, weight_all, bias_all, mix_all, weight, bias, mix, sems)
+    loads.append(start_parts(past_all.at[layer], past, sems.at[7], 2))
+    for copy in inputs:
+        copy.wait()
+    add_remote(table, blocks, near, total)
     state[...] = total[...].astype(BF16)
+    copies = [start_parts(state, state_out, sems.at[8], 2)]
     for copy in loads:
         copy.wait()
-    convolve(past, state, weight, bias, gated)
-    last = start(state, state_out, sems.at[7])
-    conv_finish(routing, mix, gated, second, gated_out, second_out, send, sems)
-    last.wait()
-
-
-def hop_kernel(routing, table, blocks, far, total_in, field_out, send, field, total, sems):
-    start(total_in, total, sems.at[0]).wait()
-    add_remote(table, blocks, far, total)
+    copies.append(convolve(past, state, weight, bias, gated, gated_out, sems.at[3]))
+    second[...] = dot(gated[...], mix[...]).astype(BF16)
+    copies.append(start_send(routing, second, send, sems.at[4]))
+    for copy in copies:
+        copy.wait()
+
+
+def hop_kernel(routing, table, blocks, far, total_in, field_out, send, field, near, total, sems):
+    inputs = [
+        start_far(table, far, near, sems.at[0]),
+        start_parts(total_in, total, sems.at[1], 4),
+    ]
+    for copy in inputs:
+        copy.wait()
+    add_remote(table, blocks, near, total)
     field[...] = total[...].astype(BF16)
-    copies = [start_send(routing, field, send, sems.at[1]), start(field, field_out, sems.at[2])]
+    copies = [
+        start_send(routing, field, send, sems.at[2]),
+        start_parts(field, field_out, sems.at[3], 2),
+    ]
     for copy in copies:
         copy.wait()
 
 
-def last_kernel(table, blocks, far, total_in, state_out, state, total, sems):
-    start(total_in, total, sems.at[0]).wait()
-    add_remote(table, blocks, far, total)
+def last_kernel(table, blocks, far, total_in, state_out, state, near, total, sems):
+    inputs = [
+        start_far(table, far, near, sems.at[0]),
+        start_parts(total_in, total, sems.at[1], 4),
+    ]
+    for copy in inputs:
+        copy.wait()
+    add_remote(table, blocks, near, total)
     state[...] = total[...].astype(BF16)
-    start(state, state_out, sems.at[1]).wait()
+    start_parts(state, state_out, sems.at[2], 4).wait()
 
 
 def build_kernel(place, target, owner, slot, values, table, local, remote_blocks, *, tiles):
@@ -171,19 +214,19 @@
     return dot(block, jnp.concatenate([own, other], axis=0))
 
 
-def under_first_kernel(
-    local, values, gated, second, mix_all, skip_all, *rest, res, layer
-):
+def under_first_kernel(local, values, gated, mix_all, skip_all, *rest, res, layer):
     skip_in = rest[0] if layer else None
-    total, base, skip, wide, sems = rest[1 if layer else 0 :]
+    total, base, skip, wide, deep, second, sems = rest[1 if layer else 0 :]
     gate = gated.shape[1]
     loads = [
+        start(mix_all.at[layer, pl.ds(2 * gate, gate), :], deep, sems.at[3]),
         start(mix_all.at[layer, pl.ds(gate, gate), :], wide.at[:, pl.ds(0, res)], sems.at[0]),
         start(mix_all.at[layer, pl.ds(0, gate), :], wide.at[:, pl.ds(res, res)], sems.at[1]),
         start(skip_all.at[layer], wide.at[:, pl.ds(2 * res, skip.shape[1])], sems.at[2]),
     ]
     for copy in loads:
         copy.wait()
+    second[...] = dot(gated[...], deep[...]).astype(BF16)
     for t in range(gated.shape[0] // TILE):
         at = pl.ds(t * TILE, TILE)
         out = dot(gated[at, :], wide[...])
@@ -250,11 +293,7 @@
 
     conv_flops = 2 * rows * (2 * res * 2 * gate + gate * res)
     hop_flops = 2 * remote * TILE * TILE * res
-    conv_outs = (
-        shape((rows, gate), BF16),
-        shape((rows, res), BF16),
-        shape((slots, TILE, res), BF16),
-    )
+    conv_outs = (shape((rows, gate), BF16), shape((slots, TILE, res), BF16))
     conv_scratch = [
         pltpu.VMEM((rows, res), BF16),
         pltpu.VMEM((2 * res, 2 * gate), BF16),
@@ -264,38 +303,43 @@
         pltpu.VMEM((rows, res), BF16),
         pltpu.VMEM((rows, res), BF16),
     ]
+    near = pltpu.VMEM((remote, TILE, res), BF16)
     wide_field = pltpu.VMEM((rows, res), F32)
     thin_field = pltpu.VMEM((rows, res), BF16)
+
+    def sems(n):
+        return pltpu.SemaphoreType.DMA((n,))
+
     weights = (conv_cache, conv_weight, conv_bias, mix_weight)
     state = hidden_state
     skip = None
     total = far = None
     for layer in range(layers):
         if layer == 0:
-            gated, second, send = call(
+            gated, send = call(
                 functools.partial(first_kernel, layer=layer),
                 "conv_first",
                 (routing, state) + weights,
                 conv_outs,
                 [SMEM] + [HBM] * 5,
-                [HBM] * 3,
+                [HBM] * 2,
                 conv_flops,
-                conv_scratch + [pltpu.SemaphoreType.DMA((8,))],
+                conv_scratch + [sems(5), sems(2 * rows // PART)],
             )
         else:
-            gated, second, send, state = call(
+            gated, send, state = call(
                 functools.partial(next_kernel, layer=layer),
                 "conv_next",
                 (routing, table, remote_blocks, far, total) + weights,
                 conv_outs + (shape((rows, res), BF16),),
-                [SMEM] * 2 + [VMEM] * 2 + [HBM] * 5,
-                [HBM] * 4,
+                [SMEM] * 2 + [VMEM] + [HBM] * 6,
+                [HBM] * 3,
                 conv_flops + hop_flops,
-                conv_scratch + [wide_field, pltpu.SemaphoreType.DMA((8,))],
+                conv_scratch + [near, wide_field, sems(9)],
             )
         far = exchange(send)
         last = layer == layers - 1
-        ins = (local_table, block_values, gated, second, mix_weight, skip_weight)
+        ins = (local_table, block_values, gated, mix_weight, skip_weight)
         if layer:
             ins += (skip,)
         total, base, skip = call(
@@ -307,20 +351,25 @@
                 shape((rows, res), F32),
                 shape((rows, skips), BF16 if last else F32),
             ),
-            [SMEM] + [VMEM] * 3 + [HBM] * 2 + [VMEM] * (len(ins) - 6),
+            [SMEM] + [VMEM] * 2 + [HBM] * 2 + [VMEM] * (len(ins) - 5),
             [VMEM] * 3,
-            2 * rows * gate * (2 * res + skips) + 4 * rows * TILE * res,
-            [pltpu.VMEM((gate, 2 * res + skips), BF16), pltpu.SemaphoreType.DMA((3,))],
+            2 * rows * gate * (3 * res + skips) + 4 * rows * TILE * res,
+            [
+                pltpu.VMEM((gate, 2 * res + skips), BF16),
+                pltpu.VMEM((gate, res), BF16),
+                thin_field,
+                sems(4),
+            ],
         )
         field, send = call(
             hop_kernel,
             "hop",
             (routing, table, remote_blocks, far, total),
             (shape((rows, res), BF16), shape((slots, TILE, res), BF16)),
-            [SMEM] * 2 + [VMEM] * 2 + [HBM],
+            [SMEM] * 2 + [VMEM] + [HBM] * 2,
             [HBM] * 2,
             hop_flops,
-            [thin_field, wide_field, pltpu.SemaphoreType.DMA((3,))],
+            [thin_field, near, wide_field, sems(4)],
         )
         far = exchange(send)
         (total,) = call(
@@ -337,10 +386,10 @@
         "last",
         (table, remote_blocks, far, total),
         (shape((rows, res), BF16),),
-        [SMEM] + [VMEM] * 2 + [HBM],
+        [SMEM] + [VMEM] + [HBM] * 2,
         [HBM],
         hop_flops,
-        [thin_field, wide_field, pltpu.SemaphoreType.DMA((2,))],
+        [thin_field, near, wide_field, sems(3)],
     )
     return state, skip
 

time: 221 us -> 213 us (0.964)
  Pallas kernels: 63.6 us -> 58 us
  local copies, waits for them, and re-layouts: 7.2 us -> 2.39 us
    pallas_call x14, Pallas kernels: 63.6 us -> 58 us  [call(): pl.pallas_call(kernel, name=name, out_shape=tuple(outs), in_specs=in_spec...]
    unnamed x13 -> x19, local copies, waits for them, and re-layouts: 6.59 us -> 1.76 us
where the time goes in v3:
time: 213 us; the launch traced here: 212 us
  waiting for transfers between devices  119 us (56%)
  Pallas kernels  58 us (27%)
  starting transfers between devices  31.7 us (15%)
  local copies, waits for them, and re-layouts  2.39 us (1%)
    all_to_all x6, waiting for transfers between devices, exchange(): lax.all_to_all(send.reshape(peers, CAP, TILE, res), 'node', split_axis=0,...  119 us
    pallas_call x14, Pallas kernels, call(): pl.pallas_call(kernel, name=name, out_shape=tuple(outs), in_specs=in_spec...  58 us
    all_to_all x6, starting transfers between devices, exchange(): lax.all_to_all(send.reshape(peers, CAP, TILE, res), 'node', split_axis=0,...  31.7 us
  transfers between devices with their start and end apart: 6, of which 6 were waited for; matrix products, arithmetic and copies ran while one was open for 0% of the time, Pallas kernels for 14%

profile of v3, /device:TPU:9, one launch (start us, length us, event | category | flops | bytes accessed | tf_op | source)
XLA Modules:
  0.0 211.8 jit_solution(16874788410570275032)
XLA Ops:
  0.6 0.8 copy.14
  1.4 0.6 reshape.43.routing
  2.0 4.7 %conv_first.1 = (bf16[2048,256]{1,0:T(8,128)(2,1)}, bf16[32,128,128]{2,1,0:T(8,128)(2,1)}) custom-call(s32[32]{0:T(128)} %reshape.43.routing, bf16[2048,128]{1,0:T(8,128)(2,1)} %state.1, bf16[3,2048,128]{2,1,0:T(8,128)(2,1)} %past_all.5, bf16[3,256,512]{2,1,0:T(8,128)(2,1)} %weight_all.5, f32[3,512]{1,0:T(4,128)} %bias_all.5, bf16[3,768,128]{2,1,0:T(8,128)(2,1)} %mix_all.11), custom_call_target="tpu_custom_call" | custom-call | flops 671088640 | bytes 5576832 | tf_op jit(solution)/shard_map/conv_first/pallas_call | solution.py:29
  6.7 0.0 copy-start
  6.7 0.0 copy-start.1
  6.7 6.8 %all-to-all-start = ((bf16[16,2,128,128]{3,2,1,0:T(8,128)(2,1)}), bf16[16,2,128,128]{3,2,1,0:T(8,128)(2,1)S(1)}, u32[]{:S(2)}, u32[]{:S(2)}) async-start(bf16[16,2,128,128]{3,2,1,0:T(8,128)(2,1)} %bitcast.15), calls=%async_computation | async-start | bytes 2097152 | tf_op jit(solution)/shard_map/all_to_all | solution.py:289
  13.5 2.9 %sort_blocks.1 = (s32[2,15]{1,0:T(2,128)S(1)}, s32[4,16]{1,0:T(4,128)S(1)}, bf16[15,128,128]{2,1,0:T(8,128)(2,1)S(1)}) custom-call(s32[1]{0:T(128)} %bitcast.place, s32[47]{0:T(128)S(1)} %copy-done.5, s32[47]{0:T(128)S(1)} %copy-done.6, s32[47]{0:T(128)S(1)} %copy-done.7, bf16[47,128,128]{2,1,0:T(8,128)(2,1)} %values.13), custom_call_target="tpu_custom_call" | custom-call | flops 47000 | bytes 2032560 | tf_op jit(solution)/shard_map/sort_blocks/pallas_call | solution.py:29
  16.4 5.7 %under_first.3 = (f32[2048,128]{1,0:T(8,128)}, f32[2048,128]{1,0:T(8,128)}, f32[2048,256]{1,0:T(8,128)}) custom-call(s32[4,16]{1,0:T(4,128)S(1)} %get-tuple-element.31.local, bf16[47,128,128]{2,1,0:T(8,128)(2,1)} %values.13, bf16[2048,256]{1,0:T(8,128)(2,1)} %get-tuple-element.32.gated, bf16[3,768,128]{2,1,0:T(8,128)(2,1)S(1)} %copy-done, ...), custom_call_target="tpu_custom_call" | custom-call | flops 805306368 | bytes 7766272 | tf_op jit(solution)/shard_map/under_first/pallas_call | solution.py:29
  22.2 16.2 %all-to-all-done = bf16[16,2,128,128]{3,2,1,0:T(8,128)(2,1)S(1)} async-done(((bf16[16,2,128,128]{3,2,1,0:T(8,128)(2,1)}), bf16[16,2,128,128]{3,2,1,0:T(8,128)(2,1)S(1)}, u32[]{:S(2)}, u32[]{:S(2)}) %all-to-all-start) | async-done | bytes 1048608 | tf_op jit(solution)/shard_map/all_to_all | solution.py:289
  38.3 1.0 copy-done.8
  39.3 3.4 %hop.3 = (bf16[2048,128]{1,0:T(8,128)(2,1)S(1)}, bf16[32,128,128]{2,1,0:T(8,128)(2,1)}) custom-call(s32[32]{0:T(128)S(1)} %copy-done.4, s32[2,15]{1,0:T(2,128)S(1)} %get-tuple-element.28.table, bf16[15,128,128]{2,1,0:T(8,128)(2,1)S(1)} %get-tuple-element.29.blocks, bf16[32,128,128]{2,1,0:T(8,128)(2,1)} %bitcast.14, f32[2048,128]{1,0:T(8,128)} %get-tuple-element.33.total_in), custom_call_target="tpu_custom_call" | custom-call | flops 62914560 | bytes 4161784 | tf_op jit(solution)/shard_map/hop/pallas_call | solution.py:29
  42.7 5.0 %all-to-all-start.1 = ((bf16[16,2,128,128]{3,2,1,0:T(8,128)(2,1)}), bf16[16,2,128,128]{3,2,1,0:T(8,128)(2,1)}, u32[]{:S(2)}, u32[]{:S(2)}) async-start(bf16[16,2,128,128]{3,2,1,0:T(8,128)(2,1)} %bitcast.20), calls=%async_computation.1 | async-start | bytes 2097152 | tf_op jit(solution)/shard_map/all_to_all | solution.py:289
  47.7 0.0 copy-start.3
  47.7 3.1 %under_second.3.total_in = f32[2048,128]{1,0:T(8,128)} custom-call(s32[4,16]{1,0:T(4,128)S(1)} %get-tuple-element.31.local, bf16[47,128,128]{2,1,0:T(8,128)(2,1)} %values.13, bf16[2048,128]{1,0:T(8,128)(2,1)S(1)} %get-tuple-element.35.field, f32[2048,128]{1,0:T(8,128)} %get-tuple-element.36.base, bf16[2048,128]{1,0:T(8,128)(2,1)S(1)} %copy-done.2), custom_call_target="tpu_custom_call" | custom-call | flops 134217728 | bytes 4686080 | tf_op jit(solution)/shard_map/under_second/pallas_call | solution.py:29
  50.9 21.8 %all-to-all-done.1 = bf16[16,2,128,128]{3,2,1,0:T(8,128)(2,1)} async-done(((bf16[16,2,128,128]{3,2,1,0:T(8,128)(2,1)}), bf16[16,2,128,128]{3,2,1,0:T(8,128)(2,1)}, u32[]{:S(2)}, u32[]{:S(2)}) %all-to-all-start.1) | async-done | bytes 1048608 | tf_op jit(solution)/shard_map/all_to_all | solution.py:289
  72.7 4.6 %conv_next.2 = (bf16[2048,256]{1,0:T(8,128)(2,1)}, bf16[32,128,128]{2,1,0:T(8,128)(2,1)}, bf16[2048,128]{1,0:T(8,128)(2,1)S(1)}) custom-call(s32[32]{0:T(128)S(1)} %copy-done.4, s32[2,15]{1,0:T(2,128)S(1)} %get-tuple-element.28.table, bf16[15,128,128]{2,1,0:T(8,128)(2,1)S(1)} %get-tuple-element.29.blocks, bf16[32,128,128]{2,1,0:T(8,128)(2,1)} %bitcast.4.far, ...), custom_call_target="tpu_custom_call" | custom-call | flops 734003200 | bytes 8165624 | tf_op jit(solution)/shard_map/conv_next/pallas_call | solution.py:29
  77.2 5.0 %all-to-all-start.2 = ((bf16[16,2,128,128]{3,2,1,0:T(8,128)(2,1)}), bf16[16,2,128,128]{3,2,1,0:T(8,128)(2,1)}, u32[]{:S(2)}, u32[]{:S(2)}) async-start(bf16[16,2,128,128]{3,2,1,0:T(8,128)(2,1)} %bitcast.16), calls=%async_computation.2 | async-start | bytes 2097152 | tf_op jit(solution)/shard_map/all_to_all | solution.py:289
  82.2 6.4 %under_first.4 = (f32[2048,128]{1,0:T(8,128)}, f32[2048,128]{1,0:T(8,128)}, f32[2048,256]{1,0:T(8,128)}) custom-call(s32[4,16]{1,0:T(4,128)S(1)} %get-tuple-element.31.local, bf16[47,128,128]{2,1,0:T(8,128)(2,1)} %values.13, bf16[2048,256]{1,0:T(8,128)(2,1)} %get-tuple-element.38.gated, bf16[3,768,128]{2,1,0:T(8,128)(2,1)S(1)} %copy-done, ...), custom_call_target="tpu_custom_call" | custom-call | flops 805306368 | bytes 9863424 | tf_op jit(solution)/shard_map/under_first/pallas_call | solution.py:29
  88.7 18.5 %all-to-all-done.2 = bf16[16,2,128,128]{3,2,1,0:T(8,128)(2,1)} async-done(((bf16[16,2,128,128]{3,2,1,0:T(8,128)(2,1)}), bf16[16,2,128,128]{3,2,1,0:T(8,128)(2,1)}, u32[]{:S(2)}, u32[]{:S(2)}) %all-to-all-start.2) | async-done | bytes 1048608 | tf_op jit(solution)/shard_map/all_to_all | solution.py:289
  107.2 3.4 %hop.4 = (bf16[2048,128]{1,0:T(8,128)(2,1)S(1)}, bf16[32,128,128]{2,1,0:T(8,128)(2,1)}) custom-call(s32[32]{0:T(128)S(1)} %copy-done.4, s32[2,15]{1,0:T(2,128)S(1)} %get-tuple-element.28.table, bf16[15,128,128]{2,1,0:T(8,128)(2,1)S(1)} %get-tuple-element.29.blocks, bf16[32,128,128]{2,1,0:T(8,128)(2,1)} %bitcast.6.far, f32[2048,128]{1,0:T(8,128)} %get-tuple-element.40.total_in), custom_call_target="tpu_custom_call" | custom-call | flops 62914560 | bytes 4161784 | tf_op jit(solution)/shard_map/hop/pallas_call | solution.py:29
  110.5 5.0 %all-to-all-start.3 = ((bf16[16,2,128,128]{3,2,1,0:T(8,128)(2,1)}), bf16[16,2,128,128]{3,2,1,0:T(8,128)(2,1)}, u32[]{:S(2)}, u32[]{:S(2)}) async-start(bf16[16,2,128,128]{3,2,1,0:T(8,128)(2,1)} %bitcast.19), calls=%async_computation.3 | async-start | bytes 2097152 | tf_op jit(solution)/shard_map/all_to_all | solution.py:289
  115.5 3.1 %under_second.4.total_in = f32[2048,128]{1,0:T(8,128)} custom-call(s32[4,16]{1,0:T(4,128)S(1)} %get-tuple-element.31.local, bf16[47,128,128]{2,1,0:T(8,128)(2,1)} %values.13, bf16[2048,128]{1,0:T(8,128)(2,1)S(1)} %get-tuple-element.42.field, f32[2048,128]{1,0:T(8,128)} %get-tuple-element.43.base, bf16[2048,128]{1,0:T(8,128)(2,1)S(1)} %get-tuple-element.44.state), custom_call_target="tpu_custom_call" | custom-call | flops 134217728 | bytes 4686080 | tf_op jit(solution)/shard_map/under_second/pallas_call | solution.py:29
  118.7 21.8 %all-to-all-done.3 = bf16[16,2,128,128]{3,2,1,0:T(8,128)(2,1)} async-done(((bf16[16,2,128,128]{3,2,1,0:T(8,128)(2,1)}), bf16[16,2,128,128]{3,2,1,0:T(8,128)(2,1)}, u32[]{:S(2)}, u32[]{:S(2)}) %all-to-all-start.3) | async-done | bytes 1048608 | tf_op jit(solution)/shard_map/all_to_all | solution.py:289
  140.5 4.5 %conv_next.3 = (bf16[2048,256]{1,0:T(8,128)(2,1)}, bf16[32,128,128]{2,1,0:T(8,128)(2,1)}, bf16[2048,128]{1,0:T(8,128)(2,1)S(1)}) custom-call(s32[32]{0:T(128)S(1)} %copy-done.4, s32[2,15]{1,0:T(2,128)S(1)} %get-tuple-element.28.table, bf16[15,128,128]{2,1,0:T(8,128)(2,1)S(1)} %get-tuple-element.29.blocks, bf16[32,128,128]{2,1,0:T(8,128)(2,1)} %bitcast.8.far, ...), custom_call_target="tpu_custom_call" | custom-call | flops 734003200 | bytes 8165624 | tf_op jit(solution)/shard_map/conv_next/pallas_call | solution.py:29
  144.9 5.0 %all-to-all-start.4 = ((bf16[16,2,128,128]{3,2,1,0:T(8,128)(2,1)}), bf16[16,2,128,128]{3,2,1,0:T(8,128)(2,1)}, u32[]{:S(2)}, u32[]{:S(2)}) async-start(bf16[16,2,128,128]{3,2,1,0:T(8,128)(2,1)} %bitcast.17), calls=%async_computation.4 | async-start | bytes 2097152 | tf_op jit(solution)/shard_map/all_to_all | solution.py:289
  149.9 6.1 %under_first.5 = (f32[2048,128]{1,0:T(8,128)}, f32[2048,128]{1,0:T(8,128)}, bf16[2048,256]{1,0:T(8,128)(2,1)}) custom-call(s32[4,16]{1,0:T(4,128)S(1)} %get-tuple-element.31.local, bf16[47,128,128]{2,1,0:T(8,128)(2,1)} %values.13, bf16[2048,256]{1,0:T(8,128)(2,1)} %get-tuple-element.46.gated, bf16[3,768,128]{2,1,0:T(8,128)(2,1)S(1)} %copy-done, ...), custom_call_target="tpu_custom_call" | custom-call | flops 805306368 | bytes 8814848 | tf_op jit(solution)/shard_map/under_first/pallas_call | solution.py:29
  156.0 18.9 %all-to-all-done.4 = bf16[16,2,128,128]{3,2,1,0:T(8,128)(2,1)} async-done(((bf16[16,2,128,128]{3,2,1,0:T(8,128)(2,1)}), bf16[16,2,128,128]{3,2,1,0:T(8,128)(2,1)}, u32[]{:S(2)}, u32[]{:S(2)}) %all-to-all-start.4) | async-done | bytes 1048608 | tf_op jit(solution)/shard_map/all_to_all | solution.py:289
  174.9 3.4 %hop.5 = (bf16[2048,128]{1,0:T(8,128)(2,1)S(1)}, bf16[32,128,128]{2,1,0:T(8,128)(2,1)}) custom-call(s32[32]{0:T(128)S(1)} %copy-done.4, s32[2,15]{1,0:T(2,128)S(1)} %get-tuple-element.28.table, bf16[15,128,128]{2,1,0:T(8,128)(2,1)S(1)} %get-tuple-element.29.blocks, bf16[32,128,128]{2,1,0:T(8,128)(2,1)} %bitcast.10.far, f32[2048,128]{1,0:T(8,128)} %get-tuple-element.48.total_in), custom_call_target="tpu_custom_call" | custom-call | flops 62914560 | bytes 4161784 | tf_op jit(solution)/shard_map/hop/pallas_call | solution.py:29
  178.3 5.0 %all-to-all-start.5 = ((bf16[16,2,128,128]{3,2,1,0:T(8,128)(2,1)}), bf16[16,2,128,128]{3,2,1,0:T(8,128)(2,1)S(1)}, u32[]{:S(2)}, u32[]{:S(2)}) async-start(bf16[16,2,128,128]{3,2,1,0:T(8,128)(2,1)} %bitcast.18), calls=%async_computation.5 | async-start | bytes 2097152 | tf_op jit(solution)/shard_map/all_to_all | solution.py:289
  183.2 3.1 %under_second.5.total_in = f32[2048,128]{1,0:T(8,128)} custom-call(s32[4,16]{1,0:T(4,128)S(1)} %get-tuple-element.31.local, bf16[47,128,128]{2,1,0:T(8,128)(2,1)} %values.13, bf16[2048,128]{1,0:T(8,128)(2,1)S(1)} %get-tuple-element.50.field, f32[2048,128]{1,0:T(8,128)} %get-tuple-element.51.base, bf16[2048,128]{1,0:T(8,128)(2,1)S(1)} %get-tuple-element.52.state), custom_call_target="tpu_custom_call" | custom-call | flops 134217728 | bytes 4686080 | tf_op jit(solution)/shard_map/under_second/pallas_call | solution.py:29
  186.4 21.7 %all-to-all-done.5 = bf16[16,2,128,128]{3,2,1,0:T(8,128)(2,1)S(1)} async-done(((bf16[16,2,128,128]{3,2,1,0:T(8,128)(2,1)}), bf16[16,2,128,128]{3,2,1,0:T(8,128)(2,1)S(1)}, u32[]{:S(2)}, u32[]{:S(2)}) %all-to-all-start.5) | async-done | bytes 1048608 | tf_op jit(solution)/shard_map/all_to_all | solution.py:289
  208.1 3.6 %last.1 = bf16[2048,128]{1,0:T(8,128)(2,1)} custom-call(s32[2,15]{1,0:T(2,128)S(1)} %get-tuple-element.28.table, bf16[15,128,128]{2,1,0:T(8,128)(2,1)S(1)} %get-tuple-element.29.blocks, bf16[32,128,128]{2,1,0:T(8,128)(2,1)S(1)} %bitcast.13, f32[2048,128]{1,0:T(8,128)} %under_second.5.total_in), custom_call_target="tpu_custom_call" | custom-call | flops 62914560 | bytes 3113080 | tf_op jit(solution)/shard_map/last/pallas_call | solution.py:29
  (14 shorter events, 0.0 us)
Async XLA Ops:
  2.0 11.5 %copy-start.5 = (s32[47]{0:T(128)S(1)}, s32[47]{0:T(128)}, u32[]{:S(2)}) copy-start(s32[47]{0:T(128)} %target.1) | copy-start | bytes 568
  2.0 11.5 %copy-start.6 = (s32[47]{0:T(128)S(1)}, s32[47]{0:T(128)}, u32[]{:S(2)}) copy-start(s32[47]{0:T(128)} %owner.1) | copy-start | bytes 568
  2.0 11.5 %copy-start.7 = (s32[47]{0:T(128)S(1)}, s32[47]{0:T(128)}, u32[]{:S(2)}) copy-start(s32[47]{0:T(128)} %slot.1) | copy-start | bytes 568
  6.7 9.7 %copy-start = (bf16[3,768,128]{2,1,0:T(8,128)(2,1)S(1)}, bf16[3,768,128]{2,1,0:T(8,128)(2,1)}, u32[]{:S(2)}) copy-start(bf16[3,768,128]{2,1,0:T(8,128)(2,1)} %mix_all.11) | copy-start | bytes 1769476
  6.7 9.7 %copy-start.1 = (bf16[3,256,256]{2,1,0:T(8,128)(2,1)S(1)}, bf16[3,256,256]{2,1,0:T(8,128)(2,1)}, u32[]{:S(2)}) copy-start(bf16[3,256,256]{2,1,0:T(8,128)(2,1)} %skip_all.5) | copy-start | bytes 1179652
  6.7 31.6 %all-to-all-start = ((bf16[16,2,128,128]{3,2,1,0:T(8,128)(2,1)}), bf16[16,2,128,128]{3,2,1,0:T(8,128)(2,1)S(1)}, u32[]{:S(2)}, u32[]{:S(2)}) async-start(bf16[16,2,128,128]{3,2,1,0:T(8,128)(2,1)} %bitcast.15), calls=%async_computation | async-start | bytes 2097152 | tf_op jit(solution)/shard_map/all_to_all | solution.py:289
  16.4 22.9 %copy-start.4 = (s32[32]{0:T(128)S(1)}, s32[32]{0:T(128)}, u32[]{:S(2)}) copy-start(s32[32]{0:T(128)} %reshape.43.routing) | copy-start | bytes 388
  38.3 1.0 copy-start.8
  39.3 8.4 %copy-start.2 = (bf16[2048,128]{1,0:T(8,128)(2,1)S(1)}, bf16[2048,128]{1,0:T(8,128)(2,1)}, u32[]{:S(2)}) copy-start(bf16[2048,128]{1,0:T(8,128)(2,1)} %state.1) | copy-start | bytes 1572868
  42.7 29.9 %all-to-all-start.1 = ((bf16[16,2,128,128]{3,2,1,0:T(8,128)(2,1)}), bf16[16,2,128,128]{3,2,1,0:T(8,128)(2,1)}, u32[]{:S(2)}, u32[]{:S(2)}) async-start(bf16[16,2,128,128]{3,2,1,0:T(8,128)(2,1)} %bitcast.20), calls=%async_computation.1 | async-start | bytes 2097152 | tf_op jit(solution)/shard_map/all_to_all | solution.py:289
  47.7 24.9 %copy-start.3 = (f32[3,512]{1,0:T(4,128)S(1)}, f32[3,512]{1,0:T(4,128)}, u32[]{:S(2)}) copy-start(f32[3,512]{1,0:T(4,128)} %bias_all.5) | copy-start | bytes 18436
  77.2 29.9 %all-to-all-start.2 = ((bf16[16,2,128,128]{3,2,1,0:T(8,128)(2,1)}), bf16[16,2,128,128]{3,2,1,0:T(8,128)(2,1)}, u32[]{:S(2)}, u32[]{:S(2)}) async-start(bf16[16,2,128,128]{3,2,1,0:T(8,128)(2,1)} %bitcast.16), calls=%async_computation.2 | async-start | bytes 2097152 | tf_op jit(solution)/shard_map/all_to_all | solution.py:289
  110.5 29.9 %all-to-all-start.3 = ((bf16[16,2,128,128]{3,2,1,0:T(8,128)(2,1)}), bf16[16,2,128,128]{3,2,1,0:T(8,128)(2,1)}, u32[]{:S(2)}, u32[]{:S(2)}) async-start(bf16[16,2,128,128]{3,2,1,0:T(8,128)(2,1)} %bitcast.19), calls=%async_computation.3 | async-start | bytes 2097152 | tf_op jit(solution)/shard_map/all_to_all | solution.py:289
  144.9 29.9 %all-to-all-start.4 = ((bf16[16,2,128,128]{3,2,1,0:T(8,128)(2,1)}), bf16[16,2,128,128]{3,2,1,0:T(8,128)(2,1)}, u32[]{:S(2)}, u32[]{:S(2)}) async-start(bf16[16,2,128,128]{3,2,1,0:T(8,128)(2,1)} %bitcast.17), calls=%async_computation.4 | async-start | bytes 2097152 | tf_op jit(solution)/shard_map/all_to_all | solution.py:289
  178.3 29.8 %all-to-all-start.5 = ((bf16[16,2,128,128]{3,2,1,0:T(8,128)(2,1)}), bf16[16,2,128,128]{3,2,1,0:T(8,128)(2,1)S(1)}, u32[]{:S(2)}, u32[]{:S(2)}) async-start(bf16[16,2,128,128]{3,2,1,0:T(8,128)(2,1)} %bitcast.18), calls=%async_computation.5 | async-start | bytes 2097152 | tf_op jit(solution)/shard_map/all_to_all | solution.py:289

commit v4 on v3

--- a/solution.py
+++ b/solution.py
@@ -16,6 +16,10 @@
 HBM = pl.BlockSpec(memory_space=pl.ANY)
 LIMITS = {"conv_first": 60}
 PART = 512
+SECTION = 128
+TARGET, SOURCE, PLACE, ROUTE, OWN, OTHER, FROM, SPARE = (SECTION * i for i in range(8))
+TABLE = 8 * SECTION
+COUNT = TABLE - 1
 
 
 def dot(a, b):
@@ -49,11 +53,31 @@
     return copy
 
 
-def start_send(routing, field, send, sem):
-    for place in range(send.shape[0]):
-        rows = pl.ds(pl.multiple_of(routing[place] * TILE, TILE), TILE)
-        start(field.at[rows, :], send.at[place], sem)
-    return pltpu.make_async_copy(send, send, sem)
+def tile_copy(field, tile, send, place, sem):
+    rows = pl.ds(pl.multiple_of(tile * TILE, TILE), TILE)
+    return pltpu.make_async_copy(field.at[rows, :], send.at[place], sem)
+
+
+class Sends:
+    def __init__(self, table, field, send, sems):
+        self.count = table[COUNT]
+
+        def copy(i):
+            place = table[PLACE + i]
+            return tile_copy(field, table[ROUTE + i], send, place, sems.at[place])
+
+        self.copy = copy
+        self.each(lambda i: copy(i).start())
+
+    def each(self, action):
+        def body(i, carry):
+            action(i)
+            return carry
+
+        lax.fori_loop(0, self.count, body, 0)
+
+    def wait(self):
+        self.each(lambda i: self.copy(i).wait())
 
 
 def start_parts(source, target, sem, parts):
@@ -66,13 +90,13 @@
 
 def start_far(table, far, near, sem):
     for j in range(near.shape[0]):
-        start(far.at[table[1, j]], near.at[j], sem)
+        start(far.at[table[SOURCE + j]], near.at[j], sem)
     return pltpu.make_async_copy(near, near, sem)
 
 
 def add_remote(table, blocks, near, total):
     for j in range(blocks.shape[0]):
-        rows = pl.ds(pl.multiple_of(table[0, j] * TILE, TILE), TILE)
+        rows = pl.ds(pl.multiple_of(table[TARGET + j] * TILE, TILE), TILE)
         total[rows, :] += dot(blocks[j], near[j])
 
 
@@ -100,9 +124,9 @@
 
 
 def first_kernel(
-    routing, state_in, past_all, weight_all, bias_all, mix_all,
+    tiles_in, state_in, past_all, weight_all, bias_all, mix_all,
     gated_out, send,
-    past, weight, bias, mix, gated, second, state, sems, parts, *, layer,
+    past, weight, bias, mix, gated, second, state, tiles, sems, parts, *, layer,
 ):
     loads = weight_loads(layer, weight_all, bias_all, mix_all, weight, bias, mix, sems)
     pieces = []
@@ -114,6 +138,7 @@
                 start(state_in.at[at, :], state.at[at, :], parts.at[2 * i + 1]),
             )
         )
+    routes = start(tiles_in, tiles, sems.at[4])
 
     def ready(i):
         if i == 0:
@@ -124,66 +149,69 @@
 
     copies = [convolve(past, state, weight, bias, gated, gated_out, sems.at[3], ready)]
     second[...] = dot(gated[...], mix[...]).astype(BF16)
-    copies.append(start_send(routing, second, send, sems.at[4]))
+    routes.wait()
+    for place in range(send.shape[0]):
+        peer, slot = divmod(place, CAP)
+        tile_copy(second, tiles[0, slot, peer], send, place, sems.at[5]).start()
+    copies.append(pltpu.make_async_copy(send, send, sems.at[5]))
     for copy in copies:
         copy.wait()
 
 
+def receive(table_in, far, total_in, table, near, total, sems, more=lambda: None):
+    index = start(table_in, table, sems.at[0])
+    sums = start_parts(total_in, total, sems.at[1], 4)
+    index.wait()
+    tiles = start_far(table, far, near, sems.at[2])
+    result = more()
+    sums.wait()
+    tiles.wait()
+    return result
+
+
 def next_kernel(
-    routing, table, blocks, far, total_in, past_all, weight_all, bias_all, mix_all,
+    table_in, blocks, far, total_in, past_all, weight_all, bias_all, mix_all,
     gated_out, send, state_out,
-    past, weight, bias, mix, gated, second, state, near, total, sems, *, layer,
-):
-    inputs = [
-        start_far(table, far, near, sems.at[5]),
-        start_parts(total_in, total, sems.at[6], 4),
-    ]
-    loads = weight_loads(layer, weight_all, bias_all, mix_all, weight, bias, mix, sems)
-    loads.append(start_parts(past_all.at[layer], past, sems.at[7], 2))
-    for copy in inputs:
-        copy.wait()
+    past, weight, bias, mix, gated, second, state, table, near, total, arrive, sems, send_sems,
+    *, layer,
+):
+    def more():
+        loads = weight_loads(layer, weight_all, bias_all, mix_all, weight, bias, mix, sems)
+        loads.append(start_parts(past_all.at[layer], past, sems.at[4], 2))
+        return loads
+
+    loads = receive(table_in, far, total_in, table, near, total, arrive, more)
     add_remote(table, blocks, near, total)
     state[...] = total[...].astype(BF16)
-    copies = [start_parts(state, state_out, sems.at[8], 2)]
+    copies = [start_parts(state, state_out, sems.at[5], 2)]
     for copy in loads:
         copy.wait()
     copies.append(convolve(past, state, weight, bias, gated, gated_out, sems.at[3]))
     second[...] = dot(gated[...], mix[...]).astype(BF16)
-    copies.append(start_send(routing, second, send, sems.at[4]))
+    copies.append(Sends(table, second, send, send_sems))
     for copy in copies:
         copy.wait()
 
 
-def hop_kernel(routing, table, blocks, far, total_in, field_out, send, field, near, total, sems):
-    inputs = [
-        start_far(table, far, near, sems.at[0]),
-        start_parts(total_in, total, sems.at[1], 4),
-    ]
-    for copy in inputs:
-        copy.wait()
+def hop_kernel(
+    table_in, blocks, far, total_in, send, field, table, near, total, arrive, send_sems
+):
+    receive(table_in, far, total_in, table, near, total, arrive)
     add_remote(table, blocks, near, total)
     field[...] = total[...].astype(BF16)
-    copies = [
-        start_send(routing, field, send, sems.at[2]),
-        start_parts(field, field_out, sems.at[3], 2),
-    ]
-    for copy in copies:
-        copy.wait()
-
-
-def last_kernel(table, blocks, far, total_in, state_out, state, near, total, sems):
-    inputs = [
-        start_far(table, far, near, sems.at[0]),
-        start_parts(total_in, total, sems.at[1], 4),
-    ]
-    for copy in inputs:
-        copy.wait()
+    Sends(table, field, send, send_sems).wait()
+
+
+def last_kernel(
+    table_in, blocks, far, total_in, state_out, state, table, near, total, arrive, sem
+):
+    receive(table_in, far, total_in, table, near, total, arrive)
     add_remote(table, blocks, near, total)
     state[...] = total[...].astype(BF16)
-    start_parts(state, state_out, sems.at[2], 4).wait()
-
-
-def build_kernel(place, target, owner, slot, values, table, local, remote_blocks, *, tiles):
+    start_parts(state, state_out, sem.at[0], 4).wait()
+
+
+def build_kernel(place, target, owner, slot, tiles, count, values, table, remote_blocks):
     me = place[0]
 
     def body(b, seen):
@@ -192,29 +220,35 @@
 
         @pl.when(mine)
         def _():
-            row = jnp.where(s == t, 0, 1)
-            local[row, t] = b
-            local[row + 2, t] = s
+            table[jnp.where(s == t, OWN, OTHER) + t] = b
+            table[jnp.where(s == t, SPARE, FROM) + t] = s
 
         @pl.when(jnp.logical_not(mine))
         def _():
-            table[0, seen] = t
-            table[1, seen] = o * CAP + s
+            table[TARGET + seen] = t
+            table[SOURCE + seen] = o * CAP + s
             remote_blocks[seen] = values[b]
 
         return seen + jnp.where(mine, 0, 1)
 
     lax.fori_loop(0, target.shape[0], body, jnp.int32(0))
-
-
-def local_sum(local, values, field, t):
-    other = field[pl.ds(pl.multiple_of(local[3, t] * TILE, TILE), TILE), :]
+    live = jnp.int32(0)
+    for peer in range(tiles.shape[2]):
+        for s in range(CAP):
+            table[PLACE + live] = peer * CAP + s
+            table[ROUTE + live] = tiles[0, s, peer]
+            live = live + jnp.where(count[0, peer] > s, 1, 0)
+    table[COUNT] = live
+
+
+def local_sum(table, values, field, t):
+    other = field[pl.ds(pl.multiple_of(table[FROM + t] * TILE, TILE), TILE), :]
     own = field[pl.ds(t * TILE, TILE), :]
-    block = jnp.concatenate([values[local[0, t]], values[local[1, t]]], axis=1)
+    block = jnp.concatenate([values[table[OWN + t]], values[table[OTHER + t]]], axis=1)
     return dot(block, jnp.concatenate([own, other], axis=0))
 
 
-def under_first_kernel(local, values, gated, mix_all, skip_all, *rest, res, layer):
+def under_first_kernel(table, values, gated, mix_all, skip_all, *rest, res, layer):
     skip_in = rest[0] if layer else None
     total, base, skip, wide, deep, second, sems = rest[1 if layer else 0 :]
     gate = gated.shape[1]
@@ -230,7 +264,7 @@
     for t in range(gated.shape[0] // TILE):
         at = pl.ds(t * TILE, TILE)
         out = dot(gated[at, :], wide[...])
-        total[at, :] = out[:, :res] + local_sum(local, values, second, t)
+        total[at, :] = out[:, :res] + local_sum(table, values, second, t)
         base[at, :] = out[:, res : 2 * res]
         gain = out[:, 2 * res :]
         if layer:
@@ -238,11 +272,21 @@
         skip[at, :] = gain.astype(skip.dtype)
 
 
-def under_second_kernel(local, values, field, base, state, total):
+def under_second_kernel(
+    table, values, blocks, far, total_in, base, state, total_out, field, near, total, sems
+):
+    loads = [
+        start_far(table, far, near, sems.at[0]),
+        start_parts(total_in, total, sems.at[1], 4),
+    ]
+    for copy in loads:
+        copy.wait()
+    add_remote(table, blocks, near, total)
+    field[...] = total[...].astype(BF16)
     for t in range(field.shape[0] // TILE):
         at = pl.ds(t * TILE, TILE)
-        total[at, :] = (
-            state[at, :].astype(F32) + base[at, :] + local_sum(local, values, field, t)
+        total_out[at, :] = (
+            state[at, :].astype(F32) + base[at, :] + local_sum(table, values, field, t)
         )
 
 
@@ -266,22 +310,19 @@
     tiles = rows // TILE
     peers = send_tiles.shape[1]
     slots = peers * CAP
+    send_tiles = jnp.swapaxes(send_tiles, 1, 2)
     blocks = block_values.shape[0]
     remote = blocks - 2 * tiles
     place = lax.axis_index("node").astype(jnp.int32)[None]
-    routing = send_tiles.reshape(slots)
-
-    table, local_table, remote_blocks = call(
-        functools.partial(build_kernel, tiles=tiles),
+    assert max(slots, remote, tiles) <= SECTION
+
+    table, remote_blocks = call(
+        build_kernel,
         "sort_blocks",
-        (place, block_target, block_owner, block_slot, block_values),
-        (
-            shape((2, remote), jnp.int32),
-            shape((4, tiles), jnp.int32),
-            shape((remote, TILE, TILE), BF16),
-        ),
-        [SMEM] * 4 + [VMEM],
-        [SMEM, SMEM, VMEM],
+        (place, block_target, block_owner, block_slot, send_tiles, send_count, block_values),
+        (shape((TABLE,), jnp.int32), shape((remote, TILE, TILE), BF16)),
+        [SMEM] * 6 + [VMEM],
+        [SMEM, VMEM],
         blocks * 1000,
     )
 
@@ -306,10 +347,12 @@
     near = pltpu.VMEM((remote, TILE, res), BF16)
     wide_field = pltpu.VMEM((rows, res), F32)
     thin_field = pltpu.VMEM((rows, res), BF16)
+    index = pltpu.SMEM((TABLE,), jnp.int32)
 
     def sems(n):
         return pltpu.SemaphoreType.DMA((n,))
 
+    arrival = [index, near, wide_field, sems(3)]
     weights = (conv_cache, conv_weight, conv_bias, mix_weight)
     state = hidden_state
     skip = None
@@ -319,27 +362,32 @@
             gated, send = call(
                 functools.partial(first_kernel, layer=layer),
                 "conv_first",
-                (routing, state) + weights,
+                (send_tiles, state) + weights,
                 conv_outs,
-                [SMEM] + [HBM] * 5,
+                [HBM] * 6,
                 [HBM] * 2,
                 conv_flops,
-                conv_scratch + [sems(5), sems(2 * rows // PART)],
+                conv_scratch
+                + [
+                    pltpu.SMEM(send_tiles.shape, jnp.int32),
+                    sems(6),
+                    sems(2 * rows // PART),
+                ],
             )
         else:
             gated, send, state = call(
                 functools.partial(next_kernel, layer=layer),
                 "conv_next",
-                (routing, table, remote_blocks, far, total) + weights,
+                (table, remote_blocks, far, total) + weights,
                 conv_outs + (shape((rows, res), BF16),),
-                [SMEM] * 2 + [VMEM] + [HBM] * 6,
+                [HBM, VMEM] + [HBM] * 6,
                 [HBM] * 3,
                 conv_flops + hop_flops,
-                conv_scratch + [near, wide_field, sems(9)],
+                conv_scratch + arrival + [sems(6), sems(slots)],
             )
         far = exchange(send)
         last = layer == layers - 1
-        ins = (local_table, block_values, gated, mix_weight, skip_weight)
+        ins = (table, block_values, gated, mix_weight, skip_weight)
         if layer:
             ins += (skip,)
         total, base, skip = call(
@@ -361,35 +409,36 @@
                 sems(4),
             ],
         )
-        field, send = call(
+        (send,) = call(
             hop_kernel,
             "hop",
-            (routing, table, remote_blocks, far, total),
-            (shape((rows, res), BF16), shape((slots, TILE, res), BF16)),
-            [SMEM] * 2 + [VMEM] + [HBM] * 2,
-            [HBM] * 2,
+            (table, remote_blocks, far, total),
+            (shape((slots, TILE, res), BF16),),
+            [HBM, VMEM, HBM, HBM],
+            [HBM],
             hop_flops,
-            [thin_field, near, wide_field, sems(4)],
-        )
-        far = exchange(send)
+            [thin_field] + arrival + [sems(slots)],
+        )
+        near_far, far = far, exchange(send)
         (total,) = call(
             under_second_kernel,
             "under_second",
-            (local_table, block_values, field, base, state),
+            (table, block_values, remote_blocks, near_far, total, base, state),
             (shape((rows, res), F32),),
-            [SMEM] + [VMEM] * 4,
+            [SMEM] + [VMEM] * 2 + [HBM] * 2 + [VMEM] * 2,
             [VMEM],
-            4 * rows * TILE * res,
+            4 * rows * TILE * res + hop_flops,
+            [thin_field, near, wide_field, sems(2)],
         )
     (state,) = call(
         last_kernel,
         "last",
         (table, remote_blocks, far, total),
         (shape((rows, res), BF16),),
-        [SMEM] + [VMEM] + [HBM] * 2,
+        [HBM, VMEM, HBM, HBM],
         [HBM],
         hop_flops,
-        [thin_field, near, wide_field, sems(3)],
+        [thin_field] + arrival + [sems(1)],
     )
     return state, skip
 

time: 213 us -> 208 us (0.977)
  waiting for transfers between devices: 119 us -> 113 us
  Pallas kernels: 58 us -> 60.5 us
    all_to_all x6, waiting for transfers between devices: 119 us -> 113 us  [exchange(): lax.all_to_all(send.reshape(peers, CAP, TILE, res), 'node', split_axis=0,...]
    pallas_call x14, Pallas kernels: 58 us -> 60.5 us  [call(): pl.pallas_call(kernel, name=name, out_shape=tuple(outs), in_specs=in_spec...]
  transfers between devices with their start and end apart: 6 -> 6, of which waited for: 6 -> 6; matrix products, arithmetic and copies ran while one was open for 0% -> 0% of each run, Pallas kernels for 14% -> 17%
where the time goes in v4:
time: 208 us; the launch traced here: 207 us
  waiting for transfers between devices  113 us (54%)
  Pallas kernels  60.5 us (29%)
  starting transfers between devices  31.4 us (15%)
    all_to_all x6, waiting for transfers between devices, exchange(): lax.all_to_all(send.reshape(peers, CAP, TILE, res), 'node', split_axis=0,...  113 us
    pallas_call x14, Pallas kernels, call(): pl.pallas_call(kernel, name=name, out_shape=tuple(outs), in_specs=in_spec...  60.5 us
    all_to_all x6, starting transfers between devices, exchange(): lax.all_to_all(send.reshape(peers, CAP, TILE, res), 'node', split_axis=0,...  31.4 us
  transfers between devices with their start and end apart: 6, of which 6 were waited for; matrix products, arithmetic and copies ran while one was open for 0% of the time, Pallas kernels for 17%

profile of v4, /device:TPU:9, one launch (start us, length us, event | category | flops | bytes accessed | tf_op | source)
XLA Modules:
  0.0 207.1 jit_solution(979139621973052713)
XLA Ops:
  0.6 0.0 copy-start.4
  0.7 3.9 %conv_first.1 = (bf16[2048,256]{1,0:T(8,128)(2,1)}, bf16[32,128,128]{2,1,0:T(8,128)(2,1)}) custom-call(s32[1,2,16]{2,1,0:T(2,128)} %bitcast.15, bf16[2048,128]{1,0:T(8,128)(2,1)} %state.1, bf16[3,2048,128]{2,1,0:T(8,128)(2,1)} %past_all.5, bf16[3,256,512]{2,1,0:T(8,128)(2,1)} %weight_all.5, f32[3,512]{1,0:T(4,128)} %bias_all.5, bf16[3,768,128]{2,1,0:T(8,128)(2,1)} %mix_all.11), custom_call_target="tpu_custom_call" | custom-call | flops 671088640 | bytes 5576832 | tf_op jit(solution)/shard_map/conv_first/pallas_call | solution.py:33
  4.6 0.0 copy-start
  4.6 0.0 copy-start.1
  4.6 6.8 %all-to-all-start = ((bf16[16,2,128,128]{3,2,1,0:T(8,128)(2,1)}), bf16[16,2,128,128]{3,2,1,0:T(8,128)(2,1)S(1)}, u32[]{:S(2)}, u32[]{:S(2)}) async-start(bf16[16,2,128,128]{3,2,1,0:T(8,128)(2,1)} %bitcast.19), calls=%async_computation | async-start | bytes 2097152 | tf_op jit(solution)/shard_map/all_to_all | solution.py:330
  11.4 2.9 %sort_blocks.1 = (s32[1024]{0:T(1024)S(1)}, bf16[15,128,128]{2,1,0:T(8,128)(2,1)S(1)}) custom-call(s32[1]{0:T(128)} %bitcast.place, s32[47]{0:T(128)S(1)} %copy-done.5, s32[47]{0:T(128)S(1)} %copy-done.6, s32[47]{0:T(128)S(1)} %copy-done.7, s32[1,2,16]{2,1,0:T(2,128)S(1)} %bitcast.16, s32[1,16]{1,0:T(1,128)S(1)} %copy-done.8, bf16[47,128,128]{2,1,0:T(8,128)(2,1)} %values.13), custom_call_target="tpu_custom_call" | custom-call | flops 47000 | bytes 2036472 | tf_op jit(solution)/shard_map/sort_blocks/pallas_call | solution.py:33
  14.4 5.7 %under_first.3 = (f32[2048,128]{1,0:T(8,128)}, f32[2048,128]{1,0:T(8,128)}, f32[2048,256]{1,0:T(8,128)}) custom-call(s32[1024]{0:T(1024)S(1)} %get-tuple-element.21.table.table_in, bf16[47,128,128]{2,1,0:T(8,128)(2,1)} %values.13, bf16[2048,256]{1,0:T(8,128)(2,1)} %get-tuple-element.24.gated, bf16[3,768,128]{2,1,0:T(8,128)(2,1)S(1)} %copy-done, ...), custom_call_target="tpu_custom_call" | custom-call | flops 805306368 | bytes 7770112 | tf_op jit(solution)/shard_map/under_first/pallas_call | solution.py:33
  20.1 16.1 %all-to-all-done = bf16[16,2,128,128]{3,2,1,0:T(8,128)(2,1)S(1)} async-done(((bf16[16,2,128,128]{3,2,1,0:T(8,128)(2,1)}), bf16[16,2,128,128]{3,2,1,0:T(8,128)(2,1)S(1)}, u32[]{:S(2)}, u32[]{:S(2)}) %all-to-all-start) | async-done | bytes 1048608 | tf_op jit(solution)/shard_map/all_to_all | solution.py:330
  36.2 1.0 copy-done.9
  37.2 3.2 %hop.3 = bf16[32,128,128]{2,1,0:T(8,128)(2,1)} custom-call(s32[1024]{0:T(1024)S(1)} %get-tuple-element.21.table.table_in, bf16[15,128,128]{2,1,0:T(8,128)(2,1)S(1)} %get-tuple-element.22.blocks, bf16[32,128,128]{2,1,0:T(8,128)(2,1)} %bitcast.17, f32[2048,128]{1,0:T(8,128)} %get-tuple-element.25.total_in), custom_call_target="tpu_custom_call" | custom-call | flops 62914560 | bytes 3641344 | tf_op jit(solution)/shard_map/hop/pallas_call | solution.py:33
  40.3 4.9 %all-to-all-start.1 = ((bf16[16,2,128,128]{3,2,1,0:T(8,128)(2,1)}), bf16[16,2,128,128]{3,2,1,0:T(8,128)(2,1)}, u32[]{:S(2)}, u32[]{:S(2)}) async-start(bf16[16,2,128,128]{3,2,1,0:T(8,128)(2,1)} %bitcast.4), calls=%async_computation.1 | async-start | bytes 2097152 | tf_op jit(solution)/shard_map/all_to_all | solution.py:330
  45.3 0.0 copy-start.3
  45.3 5.0 %under_second.3.total_in = f32[2048,128]{1,0:T(8,128)} custom-call(s32[1024]{0:T(1024)S(1)} %get-tuple-element.21.table.table_in, bf16[47,128,128]{2,1,0:T(8,128)(2,1)} %values.13, bf16[15,128,128]{2,1,0:T(8,128)(2,1)S(1)} %get-tuple-element.22.blocks, bf16[32,128,128]{2,1,0:T(8,128)(2,1)} %bitcast.18, f32[2048,128]{1,0:T(8,128)} %get-tuple-element.25.total_in, ...), custom_call_target="tpu_custom_call" | custom-call | flops 197132288 | bytes 6754304 | tf_op jit(solution)/shard_map/under_second/pallas_call | solution.py:33
  50.3 19.9 %all-to-all-done.1 = bf16[16,2,128,128]{3,2,1,0:T(8,128)(2,1)} async-done(((bf16[16,2,128,128]{3,2,1,0:T(8,128)(2,1)}), bf16[16,2,128,128]{3,2,1,0:T(8,128)(2,1)}, u32[]{:S(2)}, u32[]{:S(2)}) %all-to-all-start.1) | async-done | bytes 1048608 | tf_op jit(solution)/shard_map/all_to_all | solution.py:330
  70.2 0.0 copy-done.3
  70.2 4.3 %conv_next.2 = (bf16[2048,256]{1,0:T(8,128)(2,1)}, bf16[32,128,128]{2,1,0:T(8,128)(2,1)}, bf16[2048,128]{1,0:T(8,128)(2,1)S(1)}) custom-call(s32[1024]{0:T(1024)S(1)} %get-tuple-element.21.table.table_in, bf16[15,128,128]{2,1,0:T(8,128)(2,1)S(1)} %get-tuple-element.22.blocks, bf16[32,128,128]{2,1,0:T(8,128)(2,1)} %bitcast.5.far, ...), custom_call_target="tpu_custom_call" | custom-call | flops 734003200 | bytes 8169472 | tf_op jit(solution)/shard_map/conv_next/pallas_call | solution.py:33
  74.5 4.9 %all-to-all-start.2 = ((bf16[16,2,128,128]{3,2,1,0:T(8,128)(2,1)}), bf16[16,2,128,128]{3,2,1,0:T(8,128)(2,1)}, u32[]{:S(2)}, u32[]{:S(2)}) async-start(bf16[16,2,128,128]{3,2,1,0:T(8,128)(2,1)} %bitcast.20), calls=%async_computation.2 | async-start | bytes 2097152 | tf_op jit(solution)/shard_map/all_to_all | solution.py:330
  79.5 6.4 %under_first.4 = (f32[2048,128]{1,0:T(8,128)}, f32[2048,128]{1,0:T(8,128)}, f32[2048,256]{1,0:T(8,128)}) custom-call(s32[1024]{0:T(1024)S(1)} %get-tuple-element.21.table.table_in, bf16[47,128,128]{2,1,0:T(8,128)(2,1)} %values.13, bf16[2048,256]{1,0:T(8,128)(2,1)} %get-tuple-element.28.gated, bf16[3,768,128]{2,1,0:T(8,128)(2,1)S(1)} %copy-done, ...), custom_call_target="tpu_custom_call" | custom-call | flops 805306368 | bytes 9867264 | tf_op jit(solution)/shard_map/under_first/pallas_call | solution.py:33
  85.8 18.6 %all-to-all-done.2 = bf16[16,2,128,128]{3,2,1,0:T(8,128)(2,1)} async-done(((bf16[16,2,128,128]{3,2,1,0:T(8,128)(2,1)}), bf16[16,2,128,128]{3,2,1,0:T(8,128)(2,1)}, u32[]{:S(2)}, u32[]{:S(2)}) %all-to-all-start.2) | async-done | bytes 1048608 | tf_op jit(solution)/shard_map/all_to_all | solution.py:330
  104.4 3.1 %hop.4 = bf16[32,128,128]{2,1,0:T(8,128)(2,1)} custom-call(s32[1024]{0:T(1024)S(1)} %get-tuple-element.21.table.table_in, bf16[15,128,128]{2,1,0:T(8,128)(2,1)S(1)} %get-tuple-element.22.blocks, bf16[32,128,128]{2,1,0:T(8,128)(2,1)} %bitcast.7.far, f32[2048,128]{1,0:T(8,128)} %get-tuple-element.30.total_in), custom_call_target="tpu_custom_call" | custom-call | flops 62914560 | bytes 3641344 | tf_op jit(solution)/shard_map/hop/pallas_call | solution.py:33
  107.5 4.9 %all-to-all-start.3 = ((bf16[16,2,128,128]{3,2,1,0:T(8,128)(2,1)}), bf16[16,2,128,128]{3,2,1,0:T(8,128)(2,1)}, u32[]{:S(2)}, u32[]{:S(2)}) async-start(bf16[16,2,128,128]{3,2,1,0:T(8,128)(2,1)} %bitcast.8), calls=%async_computation.3 | async-start | bytes 2097152 | tf_op jit(solution)/shard_map/all_to_all | solution.py:330
  112.4 5.0 %under_second.4.total_in = f32[2048,128]{1,0:T(8,128)} custom-call(s32[1024]{0:T(1024)S(1)} %get-tuple-element.21.table.table_in, bf16[47,128,128]{2,1,0:T(8,128)(2,1)} %values.13, bf16[15,128,128]{2,1,0:T(8,128)(2,1)S(1)} %get-tuple-element.22.blocks, bf16[32,128,128]{2,1,0:T(8,128)(2,1)} %bitcast.7.far, f32[2048,128]{1,0:T(8,128)} %get-tuple-element.30.total_in, ...), custom_call_target="tpu_custom_call" | custom-call | flops 197132288 | bytes 6754304 | tf_op jit(solution)/shard_map/under_second/pallas_call | solution.py:33
  117.4 19.9 %all-to-all-done.3 = bf16[16,2,128,128]{3,2,1,0:T(8,128)(2,1)} async-done(((bf16[16,2,128,128]{3,2,1,0:T(8,128)(2,1)}), bf16[16,2,128,128]{3,2,1,0:T(8,128)(2,1)}, u32[]{:S(2)}, u32[]{:S(2)}) %all-to-all-start.3) | async-done | bytes 1048608 | tf_op jit(solution)/shard_map/all_to_all | solution.py:330
  137.4 4.3 %conv_next.3 = (bf16[2048,256]{1,0:T(8,128)(2,1)}, bf16[32,128,128]{2,1,0:T(8,128)(2,1)}, bf16[2048,128]{1,0:T(8,128)(2,1)S(1)}) custom-call(s32[1024]{0:T(1024)S(1)} %get-tuple-element.21.table.table_in, bf16[15,128,128]{2,1,0:T(8,128)(2,1)S(1)} %get-tuple-element.22.blocks, bf16[32,128,128]{2,1,0:T(8,128)(2,1)} %bitcast.9.far, ...), custom_call_target="tpu_custom_call" | custom-call | flops 734003200 | bytes 8169472 | tf_op jit(solution)/shard_map/conv_next/pallas_call | solution.py:33
  141.7 4.9 %all-to-all-start.4 = ((bf16[16,2,128,128]{3,2,1,0:T(8,128)(2,1)}), bf16[16,2,128,128]{3,2,1,0:T(8,128)(2,1)}, u32[]{:S(2)}, u32[]{:S(2)}) async-start(bf16[16,2,128,128]{3,2,1,0:T(8,128)(2,1)} %bitcast.21), calls=%async_computation.4 | async-start | bytes 2097152 | tf_op jit(solution)/shard_map/all_to_all | solution.py:330
  146.7 6.1 %under_first.5 = (f32[2048,128]{1,0:T(8,128)}, f32[2048,128]{1,0:T(8,128)}, bf16[2048,256]{1,0:T(8,128)(2,1)}) custom-call(s32[1024]{0:T(1024)S(1)} %get-tuple-element.21.table.table_in, bf16[47,128,128]{2,1,0:T(8,128)(2,1)} %values.13, bf16[2048,256]{1,0:T(8,128)(2,1)} %get-tuple-element.34.gated, bf16[3,768,128]{2,1,0:T(8,128)(2,1)S(1)} %copy-done, ...), custom_call_target="tpu_custom_call" | custom-call | flops 805306368 | bytes 8818688 | tf_op jit(solution)/shard_map/under_first/pallas_call | solution.py:33
  152.8 18.8 %all-to-all-done.4 = bf16[16,2,128,128]{3,2,1,0:T(8,128)(2,1)} async-done(((bf16[16,2,128,128]{3,2,1,0:T(8,128)(2,1)}), bf16[16,2,128,128]{3,2,1,0:T(8,128)(2,1)}, u32[]{:S(2)}, u32[]{:S(2)}) %all-to-all-start.4) | async-done | bytes 1048608 | tf_op jit(solution)/shard_map/all_to_all | solution.py:330
  171.6 3.1 %hop.5 = bf16[32,128,128]{2,1,0:T(8,128)(2,1)} custom-call(s32[1024]{0:T(1024)S(1)} %get-tuple-element.21.table.table_in, bf16[15,128,128]{2,1,0:T(8,128)(2,1)S(1)} %get-tuple-element.22.blocks, bf16[32,128,128]{2,1,0:T(8,128)(2,1)} %bitcast.11.far, f32[2048,128]{1,0:T(8,128)} %get-tuple-element.36.total_in), custom_call_target="tpu_custom_call" | custom-call | flops 62914560 | bytes 3641344 | tf_op jit(solution)/shard_map/hop/pallas_call | solution.py:33
  174.7 4.9 %all-to-all-start.5 = ((bf16[16,2,128,128]{3,2,1,0:T(8,128)(2,1)}), bf16[16,2,128,128]{3,2,1,0:T(8,128)(2,1)S(1)}, u32[]{:S(2)}, u32[]{:S(2)}) async-start(bf16[16,2,128,128]{3,2,1,0:T(8,128)(2,1)} %bitcast.12), calls=%async_computation.5 | async-start | bytes 2097152 | tf_op jit(solution)/shard_map/all_to_all | solution.py:330
  179.7 5.0 %under_second.5.total_in = f32[2048,128]{1,0:T(8,128)} custom-call(s32[1024]{0:T(1024)S(1)} %get-tuple-element.21.table.table_in, bf16[47,128,128]{2,1,0:T(8,128)(2,1)} %values.13, bf16[15,128,128]{2,1,0:T(8,128)(2,1)S(1)} %get-tuple-element.22.blocks, bf16[32,128,128]{2,1,0:T(8,128)(2,1)} %bitcast.11.far, f32[2048,128]{1,0:T(8,128)} %get-tuple-element.36.total_in, ...), custom_call_target="tpu_custom_call" | custom-call | flops 197132288 | bytes 6754304 | tf_op jit(solution)/shard_map/under_second/pallas_call | solution.py:33
  184.7 19.8 %all-to-all-done.5 = bf16[16,2,128,128]{3,2,1,0:T(8,128)(2,1)S(1)} async-done(((bf16[16,2,128,128]{3,2,1,0:T(8,128)(2,1)}), bf16[16,2,128,128]{3,2,1,0:T(8,128)(2,1)S(1)}, u32[]{:S(2)}, u32[]{:S(2)}) %all-to-all-start.5) | async-done | bytes 1048608 | tf_op jit(solution)/shard_map/all_to_all | solution.py:330
  204.5 2.5 %last.1 = bf16[2048,128]{1,0:T(8,128)(2,1)} custom-call(s32[1024]{0:T(1024)S(1)} %get-tuple-element.21.table.table_in, bf16[15,128,128]{2,1,0:T(8,128)(2,1)S(1)} %get-tuple-element.22.blocks, bf16[32,128,128]{2,1,0:T(8,128)(2,1)S(1)} %bitcast.14, f32[2048,128]{1,0:T(8,128)} %under_second.5.total_in), custom_call_target="tpu_custom_call" | custom-call | flops 62914560 | bytes 3117056 | tf_op jit(solution)/shard_map/last/pallas_call | solution.py:33
  (14 shorter events, 0.0 us)
Async XLA Ops:
  0.6 10.7 %copy-start.4 = (s32[1,16,2]{1,2,0:T(2,128)S(1)}, s32[1,16,2]{1,2,0:T(2,128)}, u32[]{:S(2)}) copy-start(s32[1,16,2]{1,2,0:T(2,128)} %param.22) | copy-start | bytes 388
  0.6 10.7 %copy-start.5 = (s32[47]{0:T(128)S(1)}, s32[47]{0:T(128)}, u32[]{:S(2)}) copy-start(s32[47]{0:T(128)} %target.1) | copy-start | bytes 568
  0.7 10.7 %copy-start.6 = (s32[47]{0:T(128)S(1)}, s32[47]{0:T(128)}, u32[]{:S(2)}) copy-start(s32[47]{0:T(128)} %owner.1) | copy-start | bytes 568
  0.7 10.7 %copy-start.7 = (s32[47]{0:T(128)S(1)}, s32[47]{0:T(128)}, u32[]{:S(2)}) copy-start(s32[47]{0:T(128)} %slot.1) | copy-start | bytes 568
  0.7 10.7 %copy-start.8 = (s32[1,16]{1,0:T(1,128)S(1)}, s32[1,16]{1,0:T(1,128)}, u32[]{:S(2)}) copy-start(s32[1,16]{1,0:T(1,128)} %count.1) | copy-start | bytes 196
  4.6 9.8 %copy-start = (bf16[3,768,128]{2,1,0:T(8,128)(2,1)S(1)}, bf16[3,768,128]{2,1,0:T(8,128)(2,1)}, u32[]{:S(2)}) copy-start(bf16[3,768,128]{2,1,0:T(8,128)(2,1)} %mix_all.11) | copy-start | bytes 1769476
  4.6 9.8 %copy-start.1 = (bf16[3,256,256]{2,1,0:T(8,128)(2,1)S(1)}, bf16[3,256,256]{2,1,0:T(8,128)(2,1)}, u32[]{:S(2)}) copy-start(bf16[3,256,256]{2,1,0:T(8,128)(2,1)} %skip_all.5) | copy-start | bytes 1179652
  4.6 31.6 %all-to-all-start = ((bf16[16,2,128,128]{3,2,1,0:T(8,128)(2,1)}), bf16[16,2,128,128]{3,2,1,0:T(8,128)(2,1)S(1)}, u32[]{:S(2)}, u32[]{:S(2)}) async-start(bf16[16,2,128,128]{3,2,1,0:T(8,128)(2,1)} %bitcast.19), calls=%async_computation | async-start | bytes 2097152 | tf_op jit(solution)/shard_map/all_to_all | solution.py:330
  36.2 1.0 copy-start.9
  37.2 8.1 %copy-start.2 = (bf16[2048,128]{1,0:T(8,128)(2,1)S(1)}, bf16[2048,128]{1,0:T(8,128)(2,1)}, u32[]{:S(2)}) copy-start(bf16[2048,128]{1,0:T(8,128)(2,1)} %state.1) | copy-start | bytes 1572868
  40.3 29.9 %all-to-all-start.1 = ((bf16[16,2,128,128]{3,2,1,0:T(8,128)(2,1)}), bf16[16,2,128,128]{3,2,1,0:T(8,128)(2,1)}, u32[]{:S(2)}, u32[]{:S(2)}) async-start(bf16[16,2,128,128]{3,2,1,0:T(8,128)(2,1)} %bitcast.4), calls=%async_computation.1 | async-start | bytes 2097152 | tf_op jit(solution)/shard_map/all_to_all | solution.py:330
  45.3 24.9 %copy-start.3 = (f32[3,512]{1,0:T(4,128)S(1)}, f32[3,512]{1,0:T(4,128)}, u32[]{:S(2)}) copy-start(f32[3,512]{1,0:T(4,128)} %bias_all.5) | copy-start | bytes 18436
  74.5 29.9 %all-to-all-start.2 = ((bf16[16,2,128,128]{3,2,1,0:T(8,128)(2,1)}), bf16[16,2,128,128]{3,2,1,0:T(8,128)(2,1)}, u32[]{:S(2)}, u32[]{:S(2)}) async-start(bf16[16,2,128,128]{3,2,1,0:T(8,128)(2,1)} %bitcast.20), calls=%async_computation.2 | async-start | bytes 2097152 | tf_op jit(solution)/shard_map/all_to_all | solution.py:330
  107.5 29.9 %all-to-all-start.3 = ((bf16[16,2,128,128]{3,2,1,0:T(8,128)(2,1)}), bf16[16,2,128,128]{3,2,1,0:T(8,128)(2,1)}, u32[]{:S(2)}, u32[]{:S(2)}) async-start(bf16[16,2,128,128]{3,2,1,0:T(8,128)(2,1)} %bitcast.8), calls=%async_computation.3 | async-start | bytes 2097152 | tf_op jit(solution)/shard_map/all_to_all | solution.py:330
  141.7 29.9 %all-to-all-start.4 = ((bf16[16,2,128,128]{3,2,1,0:T(8,128)(2,1)}), bf16[16,2,128,128]{3,2,1,0:T(8,128)(2,1)}, u32[]{:S(2)}, u32[]{:S(2)}) async-start(bf16[16,2,128,128]{3,2,1,0:T(8,128)(2,1)} %bitcast.21), calls=%async_computation.4 | async-start | bytes 2097152 | tf_op jit(solution)/shard_map/all_to_all | solution.py:330
  174.7 29.8 %all-to-all-start.5 = ((bf16[16,2,128,128]{3,2,1,0:T(8,128)(2,1)}), bf16[16,2,128,128]{3,2,1,0:T(8,128)(2,1)S(1)}, u32[]{:S(2)}, u32[]{:S(2)}) async-start(bf16[16,2,128,128]{3,2,1,0:T(8,128)(2,1)} %bitcast.12), calls=%async_computation.5 | async-start | bytes 2097152 | tf_op jit(solution)/shard_map/all_to_all | solution.py:330

commit v5 on v4

--- a/solution.py
+++ b/solution.py
@@ -20,6 +20,7 @@
 TARGET, SOURCE, PLACE, ROUTE, OWN, OTHER, FROM, SPARE = (SECTION * i for i in range(8))
 TABLE = 8 * SECTION
 COUNT = TABLE - 1
+GROUP = 4
 
 
 def dot(a, b):
@@ -60,24 +61,28 @@
 
 class Sends:
     def __init__(self, table, field, send, sems):
-        self.count = table[COUNT]
-
-        def copy(i):
-            place = table[PLACE + i]
-            return tile_copy(field, table[ROUTE + i], send, place, sems.at[place])
-
-        self.copy = copy
-        self.each(lambda i: copy(i).start())
-
-    def each(self, action):
-        def body(i, carry):
-            action(i)
-            return carry
-
-        lax.fori_loop(0, self.count, body, 0)
+        self.groups = []
+        count = table[COUNT]
+        for g in range(send.shape[0] // GROUP):
+            live = count > g * GROUP
+
+            @pl.when(live)
+            def _():
+                for i in range(g * GROUP, (g + 1) * GROUP):
+                    tile_copy(field, table[ROUTE + i], send, table[PLACE + i], sems.at[g]).start()
+
+            some = send.at[pl.ds(0, GROUP)]
+            self.groups.append((live, pltpu.make_async_copy(some, some, sems.at[g])))
 
     def wait(self):
-        self.each(lambda i: self.copy(i).wait())
+        for live, copy in self.groups:
+            pl.when(live)(copy.wait)
+
+
+def start_sends(tile_of, field, send, sem):
+    for place in range(send.shape[0]):
+        tile_copy(field, tile_of(place), send, place, sem).start()
+    return pltpu.make_async_copy(send, send, sem)
 
 
 def start_parts(source, target, sem, parts):
@@ -92,6 +97,12 @@
     for j in range(near.shape[0]):
         start(far.at[table[SOURCE + j]], near.at[j], sem)
     return pltpu.make_async_copy(near, near, sem)
+
+
+def add_arrived(table, blocks, far, total):
+    for j in range(blocks.shape[0]):
+        rows = pl.ds(pl.multiple_of(table[TARGET + j] * TILE, TILE), TILE)
+        total[rows, :] += dot(blocks[j], far[table[SOURCE + j]])
 
 
 def add_remote(table, blocks, near, total):
@@ -150,29 +161,35 @@
     copies = [convolve(past, state, weight, bias, gated, gated_out, sems.at[3], ready)]
     second[...] = dot(gated[...], mix[...]).astype(BF16)
     routes.wait()
-    for place in range(send.shape[0]):
+    def tile_of(place):
         peer, slot = divmod(place, CAP)
-        tile_copy(second, tiles[0, slot, peer], send, place, sems.at[5]).start()
-    copies.append(pltpu.make_async_copy(send, send, sems.at[5]))
+        return tiles[0, slot, peer]
+
+    copies.append(start_sends(tile_of, second, send, sems.at[5]))
     for copy in copies:
         copy.wait()
 
 
-def receive(table_in, far, total_in, table, near, total, sems, more=lambda: None):
+def receive(table_in, far, part_in, table, part, total, near, sems, more=lambda: None):
     index = start(table_in, table, sems.at[0])
-    sums = start_parts(total_in, total, sems.at[1], 4)
+    tiles = start_parts(far, near, sems.at[2], 8)
+    sums = start_parts(part_in, part, sems.at[1], 2)
+    total[...] = jnp.zeros_like(total)
+    result = more()
     index.wait()
-    tiles = start_far(table, far, near, sems.at[2])
-    result = more()
     sums.wait()
     tiles.wait()
     return result
 
 
+def joined(part, total):
+    return (part.astype(F32) + total).astype(BF16)
+
+
 def next_kernel(
-    table_in, blocks, far, total_in, past_all, weight_all, bias_all, mix_all,
-    gated_out, send, state_out,
-    past, weight, bias, mix, gated, second, state, table, near, total, arrive, sems, send_sems,
+    table_in, blocks, far, part_in, past_all, weight_all, bias_all, mix_all,
+    gated_out, send,
+    past, weight, bias, mix, gated, second, state, table, part, total, near, arrive, sems, send_sems,
     *, layer,
 ):
     def more():
@@ -180,13 +197,12 @@
         loads.append(start_parts(past_all.at[layer], past, sems.at[4], 2))
         return loads
 
-    loads = receive(table_in, far, total_in, table, near, total, arrive, more)
-    add_remote(table, blocks, near, total)
-    state[...] = total[...].astype(BF16)
-    copies = [start_parts(state, state_out, sems.at[5], 2)]
+    loads = receive(table_in, far, part_in, table, part, total, near, arrive, more)
+    add_arrived(table, blocks, near, total)
+    state[...] = joined(part[...], total[...])
     for copy in loads:
         copy.wait()
-    copies.append(convolve(past, state, weight, bias, gated, gated_out, sems.at[3]))
+    copies = [convolve(past, state, weight, bias, gated, gated_out, sems.at[3])]
     second[...] = dot(gated[...], mix[...]).astype(BF16)
     copies.append(Sends(table, second, send, send_sems))
     for copy in copies:
@@ -194,20 +210,20 @@
 
 
 def hop_kernel(
-    table_in, blocks, far, total_in, send, field, table, near, total, arrive, send_sems
-):
-    receive(table_in, far, total_in, table, near, total, arrive)
-    add_remote(table, blocks, near, total)
-    field[...] = total[...].astype(BF16)
+    table_in, blocks, far, part_in, send, field, table, part, total, near, arrive, send_sems
+):
+    receive(table_in, far, part_in, table, part, total, near, arrive)
+    add_arrived(table, blocks, near, total)
+    field[...] = joined(part[...], total[...])
     Sends(table, field, send, send_sems).wait()
 
 
 def last_kernel(
-    table_in, blocks, far, total_in, state_out, state, table, near, total, arrive, sem
-):
-    receive(table_in, far, total_in, table, near, total, arrive)
-    add_remote(table, blocks, near, total)
-    state[...] = total[...].astype(BF16)
+    table_in, blocks, far, part_in, state_out, state, table, part, total, near, arrive, sem
+):
+    receive(table_in, far, part_in, table, part, total, near, arrive)
+    add_arrived(table, blocks, near, total)
+    state[...] = joined(part[...], total[...])
     start_parts(state, state_out, sem.at[0], 4).wait()
 
 
@@ -232,12 +248,16 @@
         return seen + jnp.where(mine, 0, 1)
 
     lax.fori_loop(0, target.shape[0], body, jnp.int32(0))
-    live = jnp.int32(0)
+    slots = tiles.shape[2] * CAP
+    live = dead = jnp.int32(0)
     for peer in range(tiles.shape[2]):
         for s in range(CAP):
-            table[PLACE + live] = peer * CAP + s
-            table[ROUTE + live] = tiles[0, s, peer]
-            live = live + jnp.where(count[0, peer] > s, 1, 0)
+            used = count[0, peer] > s
+            at = jnp.where(used, live, slots - 1 - dead)
+            table[PLACE + at] = peer * CAP + s
+            table[ROUTE + at] = tiles[0, s, peer]
+            live = live + jnp.where(used, 1, 0)
+            dead = dead + jnp.where(used, 0, 1)
     table[COUNT] = live
 
 
@@ -249,8 +269,11 @@
 
 
 def under_first_kernel(table, values, gated, mix_all, skip_all, *rest, res, layer):
-    skip_in = rest[0] if layer else None
-    total, base, skip, wide, deep, second, sems = rest[1 if layer else 0 :]
+    if layer:
+        skip_in, blocks, far, part_in, *rest = rest
+    else:
+        state, *rest = rest
+    total, base, skip, wide, deep, second, sems = rest[:7]
     gate = gated.shape[1]
     loads = [
         start(mix_all.at[layer, pl.ds(2 * gate, gate), :], deep, sems.at[3]),
@@ -258,14 +281,22 @@
         start(mix_all.at[layer, pl.ds(0, gate), :], wide.at[:, pl.ds(res, res)], sems.at[1]),
         start(skip_all.at[layer], wide.at[:, pl.ds(2 * res, skip.shape[1])], sems.at[2]),
     ]
+    if layer:
+        near, part, sums = rest[7:]
+        loads.append(start_far(table, far, near, sems.at[4]))
+        loads.append(start_parts(part_in, part, sems.at[5], 4))
+        sums[...] = jnp.zeros_like(sums)
     for copy in loads:
         copy.wait()
+    if layer:
+        add_remote(table, blocks, near, sums)
     second[...] = dot(gated[...], deep[...]).astype(BF16)
     for t in range(gated.shape[0] // TILE):
         at = pl.ds(t * TILE, TILE)
         out = dot(gated[at, :], wide[...])
-        total[at, :] = out[:, :res] + local_sum(table, values, second, t)
-        base[at, :] = out[:, res : 2 * res]
+        total[at, :] = (out[:, :res] + local_sum(table, values, second, t)).astype(BF16)
+        now = joined(part[at, :], sums[at, :]) if layer else state[at, :]
+        base[at, :] = now.astype(F32) + out[:, res : 2 * res]
         gain = out[:, 2 * res :]
         if layer:
             gain = gain + skip_in[at, :]
@@ -273,21 +304,20 @@
 
 
 def under_second_kernel(
-    table, values, blocks, far, total_in, base, state, total_out, field, near, total, sems
+    table, values, blocks, far, part_in, base, part_out, field, near, part, total, sems
 ):
     loads = [
         start_far(table, far, near, sems.at[0]),
-        start_parts(total_in, total, sems.at[1], 4),
+        start_parts(part_in, part, sems.at[1], 4),
     ]
+    total[...] = jnp.zeros_like(total)
     for copy in loads:
         copy.wait()
     add_remote(table, blocks, near, total)
-    field[...] = total[...].astype(BF16)
+    field[...] = joined(part[...], total[...])
     for t in range(field.shape[0] // TILE):
         at = pl.ds(t * TILE, TILE)
-        total_out[at, :] = (
-            state[at, :].astype(F32) + base[at, :] + local_sum(table, values, field, t)
-        )
+        part_out[at, :] = (base[at, :] + local_sum(table, values, field, t)).astype(BF16)
 
 
 def local(
@@ -352,7 +382,7 @@
     def sems(n):
         return pltpu.SemaphoreType.DMA((n,))
 
-    arrival = [index, near, wide_field, sems(3)]
+    arrival = [index, thin_field, wide_field, pltpu.VMEM((slots, TILE, res), BF16), sems(3)]
     weights = (conv_cache, conv_weight, conv_bias, mix_weight)
     state = hidden_state
     skip = None
@@ -375,39 +405,39 @@
                 ],
             )
         else:
-            gated, send, state = call(
+            gated, send = call(
                 functools.partial(next_kernel, layer=layer),
                 "conv_next",
                 (table, remote_blocks, far, total) + weights,
-                conv_outs + (shape((rows, res), BF16),),
+                conv_outs,
                 [HBM, VMEM] + [HBM] * 6,
-                [HBM] * 3,
+                [HBM] * 2,
                 conv_flops + hop_flops,
-                conv_scratch + arrival + [sems(6), sems(slots)],
+                conv_scratch + arrival + [sems(6), sems(slots // GROUP)],
             )
-        far = exchange(send)
+        old_far, old_total, far = far, total, exchange(send)
         last = layer == layers - 1
         ins = (table, block_values, gated, mix_weight, skip_weight)
-        if layer:
-            ins += (skip,)
+        ins += (skip, remote_blocks, old_far, old_total) if layer else (hidden_state,)
         total, base, skip = call(
             functools.partial(under_first_kernel, res=res, layer=layer),
             "under_first",
             ins,
             (
-                shape((rows, res), F32),
+                shape((rows, res), BF16),
                 shape((rows, res), F32),
                 shape((rows, skips), BF16 if last else F32),
             ),
-            [SMEM] + [VMEM] * 2 + [HBM] * 2 + [VMEM] * (len(ins) - 5),
+            [SMEM] + [VMEM] * 2 + [HBM] * 2 + ([VMEM] * 2 + [HBM] * 2 if layer else [VMEM]),
             [VMEM] * 3,
             2 * rows * gate * (3 * res + skips) + 4 * rows * TILE * res,
             [
                 pltpu.VMEM((gate, 2 * res + skips), BF16),
                 pltpu.VMEM((gate, res), BF16),
                 thin_field,
-                sems(4),
-            ],
+                sems(6),
+            ]
+            + ([near, thin_field, wide_field] if layer else []),
         )
         (send,) = call(
             hop_kernel,
@@ -417,18 +447,18 @@
             [HBM, VMEM, HBM, HBM],
             [HBM],
             hop_flops,
-            [thin_field] + arrival + [sems(slots)],
+            [thin_field] + arrival + [sems(slots // GROUP)],
         )
         near_far, far = far, exchange(send)
         (total,) = call(
             under_second_kernel,
             "under_second",
-            (table, block_values, remote_blocks, near_far, total, base, state),
-            (shape((rows, res), F32),),
-            [SMEM] + [VMEM] * 2 + [HBM] * 2 + [VMEM] * 2,
+            (table, block_values, remote_blocks, near_far, total, base),
+            (shape((rows, res), BF16),),
+            [SMEM] + [VMEM] * 2 + [HBM] * 2 + [VMEM],
             [VMEM],
             4 * rows * TILE * res + hop_flops,
-            [thin_field, near, wide_field, sems(2)],
+            [thin_field, near, thin_field, wide_field, sems(2)],
         )
     (state,) = call(
         last_kernel,

time: 208 us -> 205 us (0.986)
  Pallas kernels: 60.5 us -> 55.9 us
  waiting for transfers between devices: 113 us -> 116 us
    pallas_call x14, Pallas kernels: 60.5 us -> 55.9 us  [call(): pl.pallas_call(kernel, name=name, out_shape=tuple(outs), in_specs=in_spec...]
    all_to_all x6, waiting for transfers between devices: 113 us -> 116 us  [exchange(): lax.all_to_all(send.reshape(peers, CAP, TILE, res), 'node', split_axis=0,...]
where the time goes in v5:
time: 205 us; the launch traced here: 204 us
  waiting for transfers between devices  116 us (57%)
  Pallas kernels  55.9 us (27%)
  starting transfers between devices  31.6 us (15%)
    all_to_all x6, waiting for transfers between devices, exchange(): lax.all_to_all(send.reshape(peers, CAP, TILE, res), 'node', split_axis=0,...  116 us
    pallas_call x14, Pallas kernels, call(): pl.pallas_call(kernel, name=name, out_shape=tuple(outs), in_specs=in_spec...  55.9 us
    all_to_all x6, starting transfers between devices, exchange(): lax.all_to_all(send.reshape(peers, CAP, TILE, res), 'node', split_axis=0,...  31.6 us
  transfers between devices with their start and end apart: 6, of which 6 were waited for; matrix products, arithmetic and copies ran while one was open for 0% of the time, Pallas kernels for 17%

profile of v5, /device:TPU:9, one launch (start us, length us, event | category | flops | bytes accessed | tf_op | source)
XLA Modules:
  0.0 204.2 jit_solution(15576410342713708183)
XLA Ops:
  0.6 0.0 copy-start.5
  0.6 0.0 copy-start.6
  0.7 0.0 copy-start.7
  0.7 3.9 %conv_first.1 = (bf16[2048,256]{1,0:T(8,128)(2,1)}, bf16[32,128,128]{2,1,0:T(8,128)(2,1)}) custom-call(s32[1,2,16]{2,1,0:T(2,128)} %bitcast.14, bf16[2048,128]{1,0:T(8,128)(2,1)} %rest_0_.1, bf16[3,2048,128]{2,1,0:T(8,128)(2,1)} %past_all.5, bf16[3,256,512]{2,1,0:T(8,128)(2,1)} %weight_all.5, f32[3,512]{1,0:T(4,128)} %bias_all.5, bf16[3,768,128]{2,1,0:T(8,128)(2,1)} %mix_all.11), custom_call_target="tpu_custom_call" | custom-call | flops 671088640 | bytes 5576832 | tf_op jit(solution)/shard_map/conv_first/pallas_call | solution.py:34
  4.6 0.0 copy-start.2
  4.6 0.0 copy-start.3
  4.6 6.8 %all-to-all-start = ((bf16[16,2,128,128]{3,2,1,0:T(8,128)(2,1)}), bf16[16,2,128,128]{3,2,1,0:T(8,128)(2,1)}, u32[]{:S(2)}, u32[]{:S(2)}) async-start(bf16[16,2,128,128]{3,2,1,0:T(8,128)(2,1)} %bitcast.19), calls=%async_computation | async-start | bytes 2097152 | tf_op jit(solution)/shard_map/all_to_all | solution.py:360
  11.4 3.0 %sort_blocks.1 = (s32[1024]{0:T(1024)S(1)}, bf16[15,128,128]{2,1,0:T(8,128)(2,1)S(1)}) custom-call(s32[1]{0:T(128)} %bitcast.place, s32[47]{0:T(128)S(1)} %copy-done.6, s32[47]{0:T(128)S(1)} %copy-done.7, s32[47]{0:T(128)S(1)} %copy-done.8, s32[1,2,16]{2,1,0:T(2,128)S(1)} %bitcast.15, s32[1,16]{1,0:T(1,128)S(1)} %copy-done.9, bf16[47,128,128]{2,1,0:T(8,128)(2,1)} %values.13), custom_call_target="tpu_custom_call" | custom-call | flops 47000 | bytes 2036472 | tf_op jit(solution)/shard_map/sort_blocks/pallas_call | solution.py:34
  14.4 6.1 %under_first.3 = (bf16[2048,128]{1,0:T(8,128)(2,1)S(1)}, f32[2048,128]{1,0:T(8,128)}, f32[2048,256]{1,0:T(8,128)}) custom-call(s32[1024]{0:T(1024)S(1)} %get-tuple-element.19.table.table_in, bf16[47,128,128]{2,1,0:T(8,128)(2,1)} %values.13, bf16[2048,256]{1,0:T(8,128)(2,1)} %get-tuple-element.22.gated, bf16[3,768,128]{2,1,0:T(8,128)(2,1)} %mix_all.11, ...), custom_call_target="tpu_custom_call" | custom-call | flops 805306368 | bytes 7770112 | tf_op jit(solution)/shard_map/under_first/pallas_call | solution.py:34
  20.6 15.7 %all-to-all-done = bf16[16,2,128,128]{3,2,1,0:T(8,128)(2,1)} async-done(((bf16[16,2,128,128]{3,2,1,0:T(8,128)(2,1)}), bf16[16,2,128,128]{3,2,1,0:T(8,128)(2,1)}, u32[]{:S(2)}, u32[]{:S(2)}) %all-to-all-start) | async-done | bytes 1048608 | tf_op jit(solution)/shard_map/all_to_all | solution.py:360
  36.3 2.6 %hop.3 = bf16[32,128,128]{2,1,0:T(8,128)(2,1)} custom-call(s32[1024]{0:T(1024)S(1)} %get-tuple-element.19.table.table_in, bf16[15,128,128]{2,1,0:T(8,128)(2,1)S(1)} %get-tuple-element.20.blocks.rest_1_, bf16[32,128,128]{2,1,0:T(8,128)(2,1)} %bitcast.3.far, bf16[2048,128]{1,0:T(8,128)(2,1)S(1)} %get-tuple-element.23.part_in), custom_call_target="tpu_custom_call" | custom-call | flops 62914560 | bytes 3117056 | tf_op jit(solution)/shard_map/hop/pallas_call | solution.py:34
  38.9 5.0 %all-to-all-start.1 = ((bf16[16,2,128,128]{3,2,1,0:T(8,128)(2,1)}), bf16[16,2,128,128]{3,2,1,0:T(8,128)(2,1)}, u32[]{:S(2)}, u32[]{:S(2)}) async-start(bf16[16,2,128,128]{3,2,1,0:T(8,128)(2,1)} %bitcast.16), calls=%async_computation.1 | async-start | bytes 2097152 | tf_op jit(solution)/shard_map/all_to_all | solution.py:360
  43.9 0.0 copy-start.4
  43.9 3.7 %under_second.3.part_in.rest_3_ = bf16[2048,128]{1,0:T(8,128)(2,1)S(1)} custom-call(s32[1024]{0:T(1024)S(1)} %get-tuple-element.19.table.table_in, bf16[47,128,128]{2,1,0:T(8,128)(2,1)} %values.13, bf16[15,128,128]{2,1,0:T(8,128)(2,1)S(1)} %get-tuple-element.20.blocks.rest_1_, bf16[32,128,128]{2,1,0:T(8,128)(2,1)} %bitcast.3.far, ...), custom_call_target="tpu_custom_call" | custom-call | flops 197132288 | bytes 5181440 | tf_op jit(solution)/shard_map/under_second/pallas_call | solution.py:34
  47.6 21.3 %all-to-all-done.1 = bf16[16,2,128,128]{3,2,1,0:T(8,128)(2,1)} async-done(((bf16[16,2,128,128]{3,2,1,0:T(8,128)(2,1)}), bf16[16,2,128,128]{3,2,1,0:T(8,128)(2,1)}, u32[]{:S(2)}, u32[]{:S(2)}) %all-to-all-start.1) | async-done | bytes 1048608 | tf_op jit(solution)/shard_map/all_to_all | solution.py:360
  68.8 3.8 %conv_next.2 = (bf16[2048,256]{1,0:T(8,128)(2,1)}, bf16[32,128,128]{2,1,0:T(8,128)(2,1)}) custom-call(s32[1024]{0:T(1024)S(1)} %get-tuple-element.19.table.table_in, bf16[15,128,128]{2,1,0:T(8,128)(2,1)S(1)} %get-tuple-element.20.blocks.rest_1_, bf16[32,128,128]{2,1,0:T(8,128)(2,1)} %bitcast.5.far.rest_2_, ...), custom_call_target="tpu_custom_call" | custom-call | flops 734003200 | bytes 7120896 | tf_op jit(solution)/shard_map/conv_next/pallas_call | solution.py:34
  72.6 5.0 %all-to-all-start.2 = ((bf16[16,2,128,128]{3,2,1,0:T(8,128)(2,1)}), bf16[16,2,128,128]{3,2,1,0:T(8,128)(2,1)}, u32[]{:S(2)}, u32[]{:S(2)}) async-start(bf16[16,2,128,128]{3,2,1,0:T(8,128)(2,1)} %bitcast.20), calls=%async_computation.2 | async-start | bytes 2097152 | tf_op jit(solution)/shard_map/all_to_all | solution.py:360
  77.6 7.2 %under_first.4 = (bf16[2048,128]{1,0:T(8,128)(2,1)S(1)}, f32[2048,128]{1,0:T(8,128)}, f32[2048,256]{1,0:T(8,128)}) custom-call(s32[1024]{0:T(1024)S(1)} %get-tuple-element.19.table.table_in, bf16[47,128,128]{2,1,0:T(8,128)(2,1)} %values.13, bf16[2048,256]{1,0:T(8,128)(2,1)} %get-tuple-element.26.gated, bf16[3,768,128]{2,1,0:T(8,128)(2,1)} %mix_all.11, ...), custom_call_target="tpu_custom_call" | custom-call | flops 805306368 | bytes 11407360 | tf_op jit(solution)/shard_map/under_first/pallas_call | solution.py:34
  84.8 17.8 %all-to-all-done.2 = bf16[16,2,128,128]{3,2,1,0:T(8,128)(2,1)} async-done(((bf16[16,2,128,128]{3,2,1,0:T(8,128)(2,1)}), bf16[16,2,128,128]{3,2,1,0:T(8,128)(2,1)}, u32[]{:S(2)}, u32[]{:S(2)}) %all-to-all-start.2) | async-done | bytes 1048608 | tf_op jit(solution)/shard_map/all_to_all | solution.py:360
  102.5 2.6 %hop.4 = bf16[32,128,128]{2,1,0:T(8,128)(2,1)} custom-call(s32[1024]{0:T(1024)S(1)} %get-tuple-element.19.table.table_in, bf16[15,128,128]{2,1,0:T(8,128)(2,1)S(1)} %get-tuple-element.20.blocks.rest_1_, bf16[32,128,128]{2,1,0:T(8,128)(2,1)} %bitcast.7.far, bf16[2048,128]{1,0:T(8,128)(2,1)S(1)} %get-tuple-element.28.part_in), custom_call_target="tpu_custom_call" | custom-call | flops 62914560 | bytes 3117056 | tf_op jit(solution)/shard_map/hop/pallas_call | solution.py:34
  105.1 5.0 %all-to-all-start.3 = ((bf16[16,2,128,128]{3,2,1,0:T(8,128)(2,1)}), bf16[16,2,128,128]{3,2,1,0:T(8,128)(2,1)}, u32[]{:S(2)}, u32[]{:S(2)}) async-start(bf16[16,2,128,128]{3,2,1,0:T(8,128)(2,1)} %bitcast.17), calls=%async_computation.3 | async-start | bytes 2097152 | tf_op jit(solution)/shard_map/all_to_all | solution.py:360
  110.1 3.7 %under_second.4.part_in.rest_3_ = bf16[2048,128]{1,0:T(8,128)(2,1)S(1)} custom-call(s32[1024]{0:T(1024)S(1)} %get-tuple-element.19.table.table_in, bf16[47,128,128]{2,1,0:T(8,128)(2,1)} %values.13, bf16[15,128,128]{2,1,0:T(8,128)(2,1)S(1)} %get-tuple-element.20.blocks.rest_1_, bf16[32,128,128]{2,1,0:T(8,128)(2,1)} %bitcast.7.far, ...), custom_call_target="tpu_custom_call" | custom-call | flops 197132288 | bytes 5181440 | tf_op jit(solution)/shard_map/under_second/pallas_call | solution.py:34
  113.8 21.3 %all-to-all-done.3 = bf16[16,2,128,128]{3,2,1,0:T(8,128)(2,1)} async-done(((bf16[16,2,128,128]{3,2,1,0:T(8,128)(2,1)}), bf16[16,2,128,128]{3,2,1,0:T(8,128)(2,1)}, u32[]{:S(2)}, u32[]{:S(2)}) %all-to-all-start.3) | async-done | bytes 1048608 | tf_op jit(solution)/shard_map/all_to_all | solution.py:360
  135.1 3.9 %conv_next.3 = (bf16[2048,256]{1,0:T(8,128)(2,1)}, bf16[32,128,128]{2,1,0:T(8,128)(2,1)}) custom-call(s32[1024]{0:T(1024)S(1)} %get-tuple-element.19.table.table_in, bf16[15,128,128]{2,1,0:T(8,128)(2,1)S(1)} %get-tuple-element.20.blocks.rest_1_, bf16[32,128,128]{2,1,0:T(8,128)(2,1)} %bitcast.9.far.rest_2_, ...), custom_call_target="tpu_custom_call" | custom-call | flops 734003200 | bytes 7120896 | tf_op jit(solution)/shard_map/conv_next/pallas_call | solution.py:34
  138.9 5.0 %all-to-all-start.4 = ((bf16[16,2,128,128]{3,2,1,0:T(8,128)(2,1)}), bf16[16,2,128,128]{3,2,1,0:T(8,128)(2,1)}, u32[]{:S(2)}, u32[]{:S(2)}) async-start(bf16[16,2,128,128]{3,2,1,0:T(8,128)(2,1)} %bitcast.21), calls=%async_computation.4 | async-start | bytes 2097152 | tf_op jit(solution)/shard_map/all_to_all | solution.py:360
  143.9 6.8 %under_first.5 = (bf16[2048,128]{1,0:T(8,128)(2,1)S(1)}, f32[2048,128]{1,0:T(8,128)}, bf16[2048,256]{1,0:T(8,128)(2,1)}) custom-call(s32[1024]{0:T(1024)S(1)} %get-tuple-element.19.table.table_in, bf16[47,128,128]{2,1,0:T(8,128)(2,1)} %values.13, bf16[2048,256]{1,0:T(8,128)(2,1)} %get-tuple-element.31.gated, bf16[3,768,128]{2,1,0:T(8,128)(2,1)} %mix_all.11, ...), custom_call_target="tpu_custom_call" | custom-call | flops 805306368 | bytes 10358784 | tf_op jit(solution)/shard_map/under_first/pallas_call | solution.py:34
  150.7 18.1 %all-to-all-done.4 = bf16[16,2,128,128]{3,2,1,0:T(8,128)(2,1)} async-done(((bf16[16,2,128,128]{3,2,1,0:T(8,128)(2,1)}), bf16[16,2,128,128]{3,2,1,0:T(8,128)(2,1)}, u32[]{:S(2)}, u32[]{:S(2)}) %all-to-all-start.4) | async-done | bytes 1048608 | tf_op jit(solution)/shard_map/all_to_all | solution.py:360
  168.9 2.7 %hop.5 = bf16[32,128,128]{2,1,0:T(8,128)(2,1)} custom-call(s32[1024]{0:T(1024)S(1)} %get-tuple-element.19.table.table_in, bf16[15,128,128]{2,1,0:T(8,128)(2,1)S(1)} %get-tuple-element.20.blocks.rest_1_, bf16[32,128,128]{2,1,0:T(8,128)(2,1)} %bitcast.11.far, bf16[2048,128]{1,0:T(8,128)(2,1)S(1)} %get-tuple-element.33.part_in), custom_call_target="tpu_custom_call" | custom-call | flops 62914560 | bytes 3117056 | tf_op jit(solution)/shard_map/hop/pallas_call | solution.py:34
  171.5 5.0 %all-to-all-start.5 = ((bf16[16,2,128,128]{3,2,1,0:T(8,128)(2,1)}), bf16[16,2,128,128]{3,2,1,0:T(8,128)(2,1)}, u32[]{:S(2)}, u32[]{:S(2)}) async-start(bf16[16,2,128,128]{3,2,1,0:T(8,128)(2,1)} %bitcast.18), calls=%async_computation.5 | async-start | bytes 2097152 | tf_op jit(solution)/shard_map/all_to_all | solution.py:360
  176.5 3.6 %under_second.5.part_in = bf16[2048,128]{1,0:T(8,128)(2,1)S(1)} custom-call(s32[1024]{0:T(1024)S(1)} %get-tuple-element.19.table.table_in, bf16[47,128,128]{2,1,0:T(8,128)(2,1)} %values.13, bf16[15,128,128]{2,1,0:T(8,128)(2,1)S(1)} %get-tuple-element.20.blocks.rest_1_, bf16[32,128,128]{2,1,0:T(8,128)(2,1)} %bitcast.11.far, ...), custom_call_target="tpu_custom_call" | custom-call | flops 197132288 | bytes 5181440 | tf_op jit(solution)/shard_map/under_second/pallas_call | solution.py:34
  180.1 21.3 %all-to-all-done.5 = bf16[16,2,128,128]{3,2,1,0:T(8,128)(2,1)} async-done(((bf16[16,2,128,128]{3,2,1,0:T(8,128)(2,1)}), bf16[16,2,128,128]{3,2,1,0:T(8,128)(2,1)}, u32[]{:S(2)}, u32[]{:S(2)}) %all-to-all-start.5) | async-done | bytes 1048608 | tf_op jit(solution)/shard_map/all_to_all | solution.py:360
  201.5 2.5 %last.1 = bf16[2048,128]{1,0:T(8,128)(2,1)} custom-call(s32[1024]{0:T(1024)S(1)} %get-tuple-element.19.table.table_in, bf16[15,128,128]{2,1,0:T(8,128)(2,1)S(1)} %get-tuple-element.20.blocks.rest_1_, bf16[32,128,128]{2,1,0:T(8,128)(2,1)} %bitcast.13.far, bf16[2048,128]{1,0:T(8,128)(2,1)S(1)} %under_second.5.part_in), custom_call_target="tpu_custom_call" | custom-call | flops 62914560 | bytes 2592768 | tf_op jit(solution)/shard_map/last/pallas_call | solution.py:34
  (14 shorter events, 0.0 us)
Async XLA Ops:
  0.6 10.7 %copy-start.5 = (s32[1,16,2]{1,2,0:T(2,128)S(1)}, s32[1,16,2]{1,2,0:T(2,128)}, u32[]{:S(2)}) copy-start(s32[1,16,2]{1,2,0:T(2,128)} %param.22) | copy-start | bytes 388
  0.6 10.7 %copy-start.6 = (s32[47]{0:T(128)S(1)}, s32[47]{0:T(128)}, u32[]{:S(2)}) copy-start(s32[47]{0:T(128)} %target.1) | copy-start | bytes 568
  0.7 10.7 %copy-start.7 = (s32[47]{0:T(128)S(1)}, s32[47]{0:T(128)}, u32[]{:S(2)}) copy-start(s32[47]{0:T(128)} %owner.1) | copy-start | bytes 568
  0.7 10.7 %copy-start.8 = (s32[47]{0:T(128)S(1)}, s32[47]{0:T(128)}, u32[]{:S(2)}) copy-start(s32[47]{0:T(128)} %slot.1) | copy-start | bytes 568
  0.7 10.7 %copy-start.9 = (s32[1,16]{1,0:T(1,128)S(1)}, s32[1,16]{1,0:T(1,128)}, u32[]{:S(2)}) copy-start(s32[1,16]{1,0:T(1,128)} %count.1) | copy-start | bytes 196
  4.6 9.8 %copy-start.2 = (bf16[3,256,256]{2,1,0:T(8,128)(2,1)S(1)}, bf16[3,256,256]{2,1,0:T(8,128)(2,1)}, u32[]{:S(2)}) copy-start(bf16[3,256,256]{2,1,0:T(8,128)(2,1)} %skip_all.5) | copy-start | bytes 1179652
  4.6 9.8 %copy-start.3 = (bf16[2048,128]{1,0:T(8,128)(2,1)S(1)}, bf16[2048,128]{1,0:T(8,128)(2,1)}, u32[]{:S(2)}) copy-start(bf16[2048,128]{1,0:T(8,128)(2,1)} %rest_0_.1) | copy-start | bytes 1572868
  4.6 31.7 %all-to-all-start = ((bf16[16,2,128,128]{3,2,1,0:T(8,128)(2,1)}), bf16[16,2,128,128]{3,2,1,0:T(8,128)(2,1)}, u32[]{:S(2)}, u32[]{:S(2)}) async-start(bf16[16,2,128,128]{3,2,1,0:T(8,128)(2,1)} %bitcast.19), calls=%async_computation | async-start | bytes 2097152 | tf_op jit(solution)/shard_map/all_to_all | solution.py:360
  38.9 29.9 %all-to-all-start.1 = ((bf16[16,2,128,128]{3,2,1,0:T(8,128)(2,1)}), bf16[16,2,128,128]{3,2,1,0:T(8,128)(2,1)}, u32[]{:S(2)}, u32[]{:S(2)}) async-start(bf16[16,2,128,128]{3,2,1,0:T(8,128)(2,1)} %bitcast.16), calls=%async_computation.1 | async-start | bytes 2097152 | tf_op jit(solution)/shard_map/all_to_all | solution.py:360
  43.9 25.0 %copy-start = (bf16[3,768,128]{2,1,0:T(8,128)(2,1)S(1)}, bf16[3,768,128]{2,1,0:T(8,128)(2,1)}, u32[]{:S(2)}) copy-start(bf16[3,768,128]{2,1,0:T(8,128)(2,1)} %mix_all.11) | copy-start | bytes 1769476
  43.9 24.9 %copy-start.4 = (f32[3,512]{1,0:T(4,128)S(1)}, f32[3,512]{1,0:T(4,128)}, u32[]{:S(2)}) copy-start(f32[3,512]{1,0:T(4,128)} %bias_all.5) | copy-start | bytes 18436
  72.6 29.9 %all-to-all-start.2 = ((bf16[16,2,128,128]{3,2,1,0:T(8,128)(2,1)}), bf16[16,2,128,128]{3,2,1,0:T(8,128)(2,1)}, u32[]{:S(2)}, u32[]{:S(2)}) async-start(bf16[16,2,128,128]{3,2,1,0:T(8,128)(2,1)} %bitcast.20), calls=%async_computation.2 | async-start | bytes 2097152 | tf_op jit(solution)/shard_map/all_to_all | solution.py:360
  105.1 29.9 %all-to-all-start.3 = ((bf16[16,2,128,128]{3,2,1,0:T(8,128)(2,1)}), bf16[16,2,128,128]{3,2,1,0:T(8,128)(2,1)}, u32[]{:S(2)}, u32[]{:S(2)}) async-start(bf16[16,2,128,128]{3,2,1,0:T(8,128)(2,1)} %bitcast.17), calls=%async_computation.3 | async-start | bytes 2097152 | tf_op jit(solution)/shard_map/all_to_all | solution.py:360
  110.1 25.0 %copy-start.1 = (bf16[3,768,128]{2,1,0:T(8,128)(2,1)S(1)}, bf16[3,768,128]{2,1,0:T(8,128)(2,1)}, u32[]{:S(2)}) copy-start(bf16[3,768,128]{2,1,0:T(8,128)(2,1)} %mix_all.11) | copy-start | bytes 1769476
  138.9 29.9 %all-to-all-start.4 = ((bf16[16,2,128,128]{3,2,1,0:T(8,128)(2,1)}), bf16[16,2,128,128]{3,2,1,0:T(8,128)(2,1)}, u32[]{:S(2)}, u32[]{:S(2)}) async-start(bf16[16,2,128,128]{3,2,1,0:T(8,128)(2,1)} %bitcast.21), calls=%async_computation.4 | async-start | bytes 2097152 | tf_op jit(solution)/shard_map/all_to_all | solution.py:360
  171.5 29.9 %all-to-all-start.5 = ((bf16[16,2,128,128]{3,2,1,0:T(8,128)(2,1)}), bf16[16,2,128,128]{3,2,1,0:T(8,128)(2,1)}, u32[]{:S(2)}, u32[]{:S(2)}) async-start(bf16[16,2,128,128]{3,2,1,0:T(8,128)(2,1)} %bitcast.18), calls=%async_computation.5 | async-start | bytes 2097152 | tf_op jit(solution)/shard_map/all_to_all | solution.py:360

commit v6 on v5

--- a/solution.py
+++ b/solution.py
@@ -14,7 +14,7 @@
 VMEM = pl.BlockSpec(memory_space=pltpu.VMEM)
 SMEM = pl.BlockSpec(memory_space=pltpu.SMEM)
 HBM = pl.BlockSpec(memory_space=pl.ANY)
-LIMITS = {"conv_first": 60}
+LIMITS = {"conv_first": 60, "hop": 50}
 PART = 512
 SECTION = 128
 TARGET, SOURCE, PLACE, ROUTE, OWN, OTHER, FROM, SPARE = (SECTION * i for i in range(8))
@@ -170,15 +170,15 @@
         copy.wait()
 
 
-def receive(table_in, far, part_in, table, part, total, near, sems, more=lambda: None):
-    index = start(table_in, table, sems.at[0])
-    tiles = start_parts(far, near, sems.at[2], 8)
-    sums = start_parts(part_in, part, sems.at[1], 2)
+def receive(table_in, part_in, table, part, total, sems, more=lambda: None, far=None, near=None):
+    waits = [start(table_in, table, sems.at[0])]
+    if near is not None:
+        waits.append(start_parts(far, near, sems.at[2], 8))
+    waits.append(start_parts(part_in, part, sems.at[1], 2))
     total[...] = jnp.zeros_like(total)
     result = more()
-    index.wait()
-    sums.wait()
-    tiles.wait()
+    for copy in waits:
+        copy.wait()
     return result
 
 
@@ -197,7 +197,7 @@
         loads.append(start_parts(past_all.at[layer], past, sems.at[4], 2))
         return loads
 
-    loads = receive(table_in, far, part_in, table, part, total, near, arrive, more)
+    loads = receive(table_in, part_in, table, part, total, arrive, more, far, near)
     add_arrived(table, blocks, near, total)
     state[...] = joined(part[...], total[...])
     for copy in loads:
@@ -210,10 +210,10 @@
 
 
 def hop_kernel(
-    table_in, blocks, far, part_in, send, field, table, part, total, near, arrive, send_sems
-):
-    receive(table_in, far, part_in, table, part, total, near, arrive)
-    add_arrived(table, blocks, near, total)
+    table_in, blocks, far, part_in, send, field, table, part, total, arrive, send_sems
+):
+    receive(table_in, part_in, table, part, total, arrive)
+    add_arrived(table, blocks, far, total)
     field[...] = joined(part[...], total[...])
     Sends(table, field, send, send_sems).wait()
 
@@ -221,7 +221,7 @@
 def last_kernel(
     table_in, blocks, far, part_in, state_out, state, table, part, total, near, arrive, sem
 ):
-    receive(table_in, far, part_in, table, part, total, near, arrive)
+    receive(table_in, part_in, table, part, total, arrive, far=far, near=near)
     add_arrived(table, blocks, near, total)
     state[...] = joined(part[...], total[...])
     start_parts(state, state_out, sem.at[0], 4).wait()
@@ -383,6 +383,7 @@
         return pltpu.SemaphoreType.DMA((n,))
 
     arrival = [index, thin_field, wide_field, pltpu.VMEM((slots, TILE, res), BF16), sems(3)]
+    direct_arrival = [index, thin_field, wide_field, sems(2)]
     weights = (conv_cache, conv_weight, conv_bias, mix_weight)
     state = hidden_state
     skip = None
@@ -444,10 +445,10 @@
             "hop",
             (table, remote_blocks, far, total),
             (shape((slots, TILE, res), BF16),),
-            [HBM, VMEM, HBM, HBM],
+            [HBM, VMEM, VMEM, HBM],
             [HBM],
             hop_flops,
-            [thin_field] + arrival + [sems(slots // GROUP)],
+            [thin_field] + direct_arrival + [sems(slots // GROUP)],
         )
         near_far, far = far, exchange(send)
         (total,) = call(

time: 205 us -> 203 us (level)
  waiting for transfers between devices: 116 us -> 113 us
  Pallas kernels: 55.9 us -> 53.7 us
  local copies, waits for them, and re-layouts: 0.05 us -> 2.14 us
    all_to_all x6, waiting for transfers between devices: 116 us -> 113 us  [exchange(): lax.all_to_all(send.reshape(peers, CAP, TILE, res), 'node', split_axis=0,...]
    pallas_call x14, Pallas kernels: 55.9 us -> 53.7 us  [call(): pl.pallas_call(kernel, name=name, out_shape=tuple(outs), in_specs=in_spec...]
    unnamed x20 -> x34, local copies, waits for them, and re-layouts: 0.05 us -> 2.14 us
where the time goes in v6:
time: 203 us; the launch traced here: 202 us
  waiting for transfers between devices  113 us (56%)
  Pallas kernels  53.7 us (26%)
  starting transfers between devices  31.6 us (16%)
  local copies, waits for them, and re-layouts  2.14 us (1%)
    all_to_all x6, waiting for transfers between devices, exchange(): lax.all_to_all(send.reshape(peers, CAP, TILE, res), 'node', split_axis=0,...  113 us
    pallas_call x14, Pallas kernels, call(): pl.pallas_call(kernel, name=name, out_shape=tuple(outs), in_specs=in_spec...  53.7 us
    all_to_all x6, starting transfers between devices, exchange(): lax.all_to_all(send.reshape(peers, CAP, TILE, res), 'node', split_axis=0,...  31.6 us
  transfers between devices with their start and end apart: 6, of which 6 were waited for; matrix products, arithmetic and copies ran while one was open for 0% of the time, Pallas kernels for 17%

profile of v6, /device:TPU:9, one launch (start us, length us, event | category | flops | bytes accessed | tf_op | source)
XLA Modules:
  0.0 201.7 jit_solution(2655679390795753429)
XLA Ops:
  0.7 3.9 %conv_first.1 = (bf16[2048,256]{1,0:T(8,128)(2,1)}, bf16[32,128,128]{2,1,0:T(8,128)(2,1)}) custom-call(s32[1,2,16]{2,1,0:T(2,128)} %bitcast.20, bf16[2048,128]{1,0:T(8,128)(2,1)} %rest_0_.1, bf16[3,2048,128]{2,1,0:T(8,128)(2,1)} %past_all.5, bf16[3,256,512]{2,1,0:T(8,128)(2,1)} %weight_all.5, f32[3,512]{1,0:T(4,128)} %bias_all.5, bf16[3,768,128]{2,1,0:T(8,128)(2,1)} %mix_all.11), custom_call_target="tpu_custom_call" | custom-call | flops 671088640 | bytes 5576832 | tf_op jit(solution)/shard_map/conv_first/pallas_call | solution.py:34
  4.6 0.0 copy-start.5
  4.6 0.0 copy-start.6
  4.6 6.8 %all-to-all-start = ((bf16[16,2,128,128]{3,2,1,0:T(8,128)(2,1)}), bf16[16,2,128,128]{3,2,1,0:T(8,128)(2,1)S(1)}, u32[]{:S(2)}, u32[]{:S(2)}) async-start(bf16[16,2,128,128]{3,2,1,0:T(8,128)(2,1)} %bitcast.22), calls=%async_computation | async-start | bytes 2097152 | tf_op jit(solution)/shard_map/all_to_all | solution.py:360
  11.4 3.0 %sort_blocks.1 = (s32[1024]{0:T(1024)S(1)}, bf16[15,128,128]{2,1,0:T(8,128)(2,1)S(1)}) custom-call(s32[1]{0:T(128)} %bitcast.place, s32[47]{0:T(128)S(1)} %copy-done.13, s32[47]{0:T(128)S(1)} %copy-done.14, s32[47]{0:T(128)S(1)} %copy-done.15, s32[1,2,16]{2,1,0:T(2,128)S(1)} %bitcast.21, s32[1,16]{1,0:T(1,128)S(1)} %copy-done.16, bf16[47,128,128]{2,1,0:T(8,128)(2,1)} %values.13), custom_call_target="tpu_custom_call" | custom-call | flops 47000 | bytes 2036472 | tf_op jit(solution)/shard_map/sort_blocks/pallas_call | solution.py:34
  14.4 6.2 %under_first.3 = (bf16[2048,128]{1,0:T(8,128)(2,1)S(1)}, f32[2048,128]{1,0:T(8,128)}, f32[2048,256]{1,0:T(8,128)}) custom-call(s32[1024]{0:T(1024)S(1)} %get-tuple-element.19.table.table_in, bf16[47,128,128]{2,1,0:T(8,128)(2,1)} %values.13, bf16[2048,256]{1,0:T(8,128)(2,1)} %get-tuple-element.22.gated, bf16[3,768,128]{2,1,0:T(8,128)(2,1)} %mix_all.11, ...), custom_call_target="tpu_custom_call" | custom-call | flops 805306368 | bytes 7770112 | tf_op jit(solution)/shard_map/under_first/pallas_call | solution.py:34
  20.6 0.0 copy-start.9
  20.6 15.6 %all-to-all-done = bf16[16,2,128,128]{3,2,1,0:T(8,128)(2,1)S(1)} async-done(((bf16[16,2,128,128]{3,2,1,0:T(8,128)(2,1)}), bf16[16,2,128,128]{3,2,1,0:T(8,128)(2,1)S(1)}, u32[]{:S(2)}, u32[]{:S(2)}) %all-to-all-start) | async-done | bytes 1048608 | tf_op jit(solution)/shard_map/all_to_all | solution.py:360
  36.2 1.9 hop.3
  38.1 5.0 %all-to-all-start.1 = ((bf16[16,2,128,128]{3,2,1,0:T(8,128)(2,1)}), bf16[16,2,128,128]{3,2,1,0:T(8,128)(2,1)}, u32[]{:S(2)}, u32[]{:S(2)}) async-start(bf16[16,2,128,128]{3,2,1,0:T(8,128)(2,1)} %bitcast.4), calls=%async_computation.1 | async-start | bytes 2097152 | tf_op jit(solution)/shard_map/all_to_all | solution.py:360
  43.1 1.0 copy-done.10
  44.2 3.7 %under_second.3.part_in.rest_3_ = bf16[2048,128]{1,0:T(8,128)(2,1)S(1)} custom-call(s32[1024]{0:T(1024)S(1)} %get-tuple-element.19.table.table_in, bf16[47,128,128]{2,1,0:T(8,128)(2,1)} %values.13, bf16[15,128,128]{2,1,0:T(8,128)(2,1)S(1)} %get-tuple-element.20.blocks.rest_1_, bf16[32,128,128]{2,1,0:T(8,128)(2,1)} %bitcast.15, ...), custom_call_target="tpu_custom_call" | custom-call | flops 197132288 | bytes 5181440 | tf_op jit(solution)/shard_map/under_second/pallas_call | solution.py:34
  47.8 20.2 %all-to-all-done.1 = bf16[16,2,128,128]{3,2,1,0:T(8,128)(2,1)} async-done(((bf16[16,2,128,128]{3,2,1,0:T(8,128)(2,1)}), bf16[16,2,128,128]{3,2,1,0:T(8,128)(2,1)}, u32[]{:S(2)}, u32[]{:S(2)}) %all-to-all-start.1) | async-done | bytes 1048608 | tf_op jit(solution)/shard_map/all_to_all | solution.py:360
  68.1 3.8 %conv_next.2 = (bf16[2048,256]{1,0:T(8,128)(2,1)}, bf16[32,128,128]{2,1,0:T(8,128)(2,1)}) custom-call(s32[1024]{0:T(1024)S(1)} %get-tuple-element.19.table.table_in, bf16[15,128,128]{2,1,0:T(8,128)(2,1)S(1)} %get-tuple-element.20.blocks.rest_1_, bf16[32,128,128]{2,1,0:T(8,128)(2,1)} %bitcast.5.far.rest_2_, ...), custom_call_target="tpu_custom_call" | custom-call | flops 734003200 | bytes 7120896 | tf_op jit(solution)/shard_map/conv_next/pallas_call | solution.py:34
  71.8 5.0 %all-to-all-start.2 = ((bf16[16,2,128,128]{3,2,1,0:T(8,128)(2,1)}), bf16[16,2,128,128]{3,2,1,0:T(8,128)(2,1)S(1)}, u32[]{:S(2)}, u32[]{:S(2)}) async-start(bf16[16,2,128,128]{3,2,1,0:T(8,128)(2,1)} %bitcast.23), calls=%async_computation.2 | async-start | bytes 2097152 | tf_op jit(solution)/shard_map/all_to_all | solution.py:360
  76.8 7.1 %under_first.4 = (bf16[2048,128]{1,0:T(8,128)(2,1)S(1)}, f32[2048,128]{1,0:T(8,128)}, f32[2048,256]{1,0:T(8,128)}) custom-call(s32[1024]{0:T(1024)S(1)} %get-tuple-element.19.table.table_in, bf16[47,128,128]{2,1,0:T(8,128)(2,1)} %values.13, bf16[2048,256]{1,0:T(8,128)(2,1)} %get-tuple-element.26.gated, bf16[3,768,128]{2,1,0:T(8,128)(2,1)} %mix_all.11, ...), custom_call_target="tpu_custom_call" | custom-call | flops 805306368 | bytes 11407360 | tf_op jit(solution)/shard_map/under_first/pallas_call | solution.py:34
  83.9 0.0 copy-start.7
  83.9 17.7 %all-to-all-done.2 = bf16[16,2,128,128]{3,2,1,0:T(8,128)(2,1)S(1)} async-done(((bf16[16,2,128,128]{3,2,1,0:T(8,128)(2,1)}), bf16[16,2,128,128]{3,2,1,0:T(8,128)(2,1)S(1)}, u32[]{:S(2)}, u32[]{:S(2)}) %all-to-all-start.2) | async-done | bytes 1048608 | tf_op jit(solution)/shard_map/all_to_all | solution.py:360
  101.7 1.9 hop.4
  103.6 5.0 %all-to-all-start.3 = ((bf16[16,2,128,128]{3,2,1,0:T(8,128)(2,1)}), bf16[16,2,128,128]{3,2,1,0:T(8,128)(2,1)}, u32[]{:S(2)}, u32[]{:S(2)}) async-start(bf16[16,2,128,128]{3,2,1,0:T(8,128)(2,1)} %bitcast.8), calls=%async_computation.3 | async-start | bytes 2097152 | tf_op jit(solution)/shard_map/all_to_all | solution.py:360
  108.6 1.0 copy-done.8
  109.6 3.7 %under_second.4.part_in.rest_3_ = bf16[2048,128]{1,0:T(8,128)(2,1)S(1)} custom-call(s32[1024]{0:T(1024)S(1)} %get-tuple-element.19.table.table_in, bf16[47,128,128]{2,1,0:T(8,128)(2,1)} %values.13, bf16[15,128,128]{2,1,0:T(8,128)(2,1)S(1)} %get-tuple-element.20.blocks.rest_1_, bf16[32,128,128]{2,1,0:T(8,128)(2,1)} %bitcast.17, ...), custom_call_target="tpu_custom_call" | custom-call | flops 197132288 | bytes 5181440 | tf_op jit(solution)/shard_map/under_second/pallas_call | solution.py:34
  113.3 20.2 %all-to-all-done.3 = bf16[16,2,128,128]{3,2,1,0:T(8,128)(2,1)} async-done(((bf16[16,2,128,128]{3,2,1,0:T(8,128)(2,1)}), bf16[16,2,128,128]{3,2,1,0:T(8,128)(2,1)}, u32[]{:S(2)}, u32[]{:S(2)}) %all-to-all-start.3) | async-done | bytes 1048608 | tf_op jit(solution)/shard_map/all_to_all | solution.py:360
  133.5 3.8 %conv_next.3 = (bf16[2048,256]{1,0:T(8,128)(2,1)}, bf16[32,128,128]{2,1,0:T(8,128)(2,1)}) custom-call(s32[1024]{0:T(1024)S(1)} %get-tuple-element.19.table.table_in, bf16[15,128,128]{2,1,0:T(8,128)(2,1)S(1)} %get-tuple-element.20.blocks.rest_1_, bf16[32,128,128]{2,1,0:T(8,128)(2,1)} %bitcast.9.far.rest_2_, ...), custom_call_target="tpu_custom_call" | custom-call | flops 734003200 | bytes 7120896 | tf_op jit(solution)/shard_map/conv_next/pallas_call | solution.py:34
  137.3 5.0 %all-to-all-start.4 = ((bf16[16,2,128,128]{3,2,1,0:T(8,128)(2,1)}), bf16[16,2,128,128]{3,2,1,0:T(8,128)(2,1)S(1)}, u32[]{:S(2)}, u32[]{:S(2)}) async-start(bf16[16,2,128,128]{3,2,1,0:T(8,128)(2,1)} %bitcast.24), calls=%async_computation.4 | async-start | bytes 2097152 | tf_op jit(solution)/shard_map/all_to_all | solution.py:360
  142.3 6.8 %under_first.5 = (bf16[2048,128]{1,0:T(8,128)(2,1)S(1)}, f32[2048,128]{1,0:T(8,128)}, bf16[2048,256]{1,0:T(8,128)(2,1)}) custom-call(s32[1024]{0:T(1024)S(1)} %get-tuple-element.19.table.table_in, bf16[47,128,128]{2,1,0:T(8,128)(2,1)} %values.13, bf16[2048,256]{1,0:T(8,128)(2,1)} %get-tuple-element.31.gated, bf16[3,768,128]{2,1,0:T(8,128)(2,1)} %mix_all.11, ...), custom_call_target="tpu_custom_call" | custom-call | flops 805306368 | bytes 10358784 | tf_op jit(solution)/shard_map/under_first/pallas_call | solution.py:34
  149.1 18.0 %all-to-all-done.4 = bf16[16,2,128,128]{3,2,1,0:T(8,128)(2,1)S(1)} async-done(((bf16[16,2,128,128]{3,2,1,0:T(8,128)(2,1)}), bf16[16,2,128,128]{3,2,1,0:T(8,128)(2,1)S(1)}, u32[]{:S(2)}, u32[]{:S(2)}) %all-to-all-start.4) | async-done | bytes 1048608 | tf_op jit(solution)/shard_map/all_to_all | solution.py:360
  167.2 1.9 hop.5
  169.1 5.0 %all-to-all-start.5 = ((bf16[16,2,128,128]{3,2,1,0:T(8,128)(2,1)}), bf16[16,2,128,128]{3,2,1,0:T(8,128)(2,1)}, u32[]{:S(2)}, u32[]{:S(2)}) async-start(bf16[16,2,128,128]{3,2,1,0:T(8,128)(2,1)} %bitcast.12), calls=%async_computation.5 | async-start | bytes 2097152 | tf_op jit(solution)/shard_map/all_to_all | solution.py:360
  174.1 3.6 %under_second.5.part_in = bf16[2048,128]{1,0:T(8,128)(2,1)S(1)} custom-call(s32[1024]{0:T(1024)S(1)} %get-tuple-element.19.table.table_in, bf16[47,128,128]{2,1,0:T(8,128)(2,1)} %values.13, bf16[15,128,128]{2,1,0:T(8,128)(2,1)S(1)} %get-tuple-element.20.blocks.rest_1_, bf16[32,128,128]{2,1,0:T(8,128)(2,1)} %bitcast.19, ...), custom_call_target="tpu_custom_call" | custom-call | flops 197132288 | bytes 5181440 | tf_op jit(solution)/shard_map/under_second/pallas_call | solution.py:34
  177.7 21.3 %all-to-all-done.5 = bf16[16,2,128,128]{3,2,1,0:T(8,128)(2,1)} async-done(((bf16[16,2,128,128]{3,2,1,0:T(8,128)(2,1)}), bf16[16,2,128,128]{3,2,1,0:T(8,128)(2,1)}, u32[]{:S(2)}, u32[]{:S(2)}) %all-to-all-start.5) | async-done | bytes 1048608 | tf_op jit(solution)/shard_map/all_to_all | solution.py:360
  199.0 2.5 %last.1 = bf16[2048,128]{1,0:T(8,128)(2,1)} custom-call(s32[1024]{0:T(1024)S(1)} %get-tuple-element.19.table.table_in, bf16[15,128,128]{2,1,0:T(8,128)(2,1)S(1)} %get-tuple-element.20.blocks.rest_1_, bf16[32,128,128]{2,1,0:T(8,128)(2,1)} %bitcast.13.far, bf16[2048,128]{1,0:T(8,128)(2,1)S(1)} %under_second.5.part_in), custom_call_target="tpu_custom_call" | custom-call | flops 62914560 | bytes 2592768 | tf_op jit(solution)/shard_map/last/pallas_call | solution.py:34
  (28 shorter events, 0.1 us)
Async XLA Ops:
  0.6 10.7 %copy-start.12 = (s32[1,16,2]{1,2,0:T(2,128)S(1)}, s32[1,16,2]{1,2,0:T(2,128)}, u32[]{:S(2)}) copy-start(s32[1,16,2]{1,2,0:T(2,128)} %param.22) | copy-start | bytes 388
  0.6 10.7 %copy-start.13 = (s32[47]{0:T(128)S(1)}, s32[47]{0:T(128)}, u32[]{:S(2)}) copy-start(s32[47]{0:T(128)} %target.1) | copy-start | bytes 568
  0.7 10.7 %copy-start.14 = (s32[47]{0:T(128)S(1)}, s32[47]{0:T(128)}, u32[]{:S(2)}) copy-start(s32[47]{0:T(128)} %owner.1) | copy-start | bytes 568
  0.7 10.7 %copy-start.15 = (s32[47]{0:T(128)S(1)}, s32[47]{0:T(128)}, u32[]{:S(2)}) copy-start(s32[47]{0:T(128)} %slot.1) | copy-start | bytes 568
  0.7 10.7 %copy-start.16 = (s32[1,16]{1,0:T(1,128)S(1)}, s32[1,16]{1,0:T(1,128)}, u32[]{:S(2)}) copy-start(s32[1,16]{1,0:T(1,128)} %count.1) | copy-start | bytes 196
  4.6 9.8 %copy-start.5 = (bf16[3,256,256]{2,1,0:T(8,128)(2,1)S(1)}, bf16[3,256,256]{2,1,0:T(8,128)(2,1)}, u32[]{:S(2)}) copy-start(bf16[3,256,256]{2,1,0:T(8,128)(2,1)} %skip_all.5) | copy-start | bytes 1179652
  4.6 9.8 %copy-start.6 = (bf16[2048,128]{1,0:T(8,128)(2,1)S(1)}, bf16[2048,128]{1,0:T(8,128)(2,1)}, u32[]{:S(2)}) copy-start(bf16[2048,128]{1,0:T(8,128)(2,1)} %rest_0_.1) | copy-start | bytes 1572868
  4.6 31.6 %all-to-all-start = ((bf16[16,2,128,128]{3,2,1,0:T(8,128)(2,1)}), bf16[16,2,128,128]{3,2,1,0:T(8,128)(2,1)S(1)}, u32[]{:S(2)}, u32[]{:S(2)}) async-start(bf16[16,2,128,128]{3,2,1,0:T(8,128)(2,1)} %bitcast.22), calls=%async_computation | async-start | bytes 2097152 | tf_op jit(solution)/shard_map/all_to_all | solution.py:360
  20.6 17.5 %copy-start.9 = (bf16[2048,128]{1,0:T(8,128)(2,1)}, bf16[2048,128]{1,0:T(8,128)(2,1)S(1)}, u32[]{:S(2)}) copy-start(bf16[2048,128]{1,0:T(8,128)(2,1)S(1)} %get-tuple-element.23.part_in) | copy-start | bytes 1572868
  36.2 1.9 copy-start.2
  38.1 29.9 %all-to-all-start.1 = ((bf16[16,2,128,128]{3,2,1,0:T(8,128)(2,1)}), bf16[16,2,128,128]{3,2,1,0:T(8,128)(2,1)}, u32[]{:S(2)}, u32[]{:S(2)}) async-start(bf16[16,2,128,128]{3,2,1,0:T(8,128)(2,1)} %bitcast.4), calls=%async_computation.1 | async-start | bytes 2097152 | tf_op jit(solution)/shard_map/all_to_all | solution.py:360
  43.1 1.0 copy-start.10
  44.2 23.9 %copy-start = (bf16[3,768,128]{2,1,0:T(8,128)(2,1)S(1)}, bf16[3,768,128]{2,1,0:T(8,128)(2,1)}, u32[]{:S(2)}) copy-start(bf16[3,768,128]{2,1,0:T(8,128)(2,1)} %mix_all.11) | copy-start | bytes 1769476
  44.2 23.9 %copy-start.11 = (f32[3,512]{1,0:T(4,128)S(1)}, f32[3,512]{1,0:T(4,128)}, u32[]{:S(2)}) copy-start(f32[3,512]{1,0:T(4,128)} %bias_all.5) | copy-start | bytes 18436
  71.8 29.8 %all-to-all-start.2 = ((bf16[16,2,128,128]{3,2,1,0:T(8,128)(2,1)}), bf16[16,2,128,128]{3,2,1,0:T(8,128)(2,1)S(1)}, u32[]{:S(2)}, u32[]{:S(2)}) async-start(bf16[16,2,128,128]{3,2,1,0:T(8,128)(2,1)} %bitcast.23), calls=%async_computation.2 | async-start | bytes 2097152 | tf_op jit(solution)/shard_map/all_to_all | solution.py:360
  83.9 19.7 %copy-start.7 = (bf16[2048,128]{1,0:T(8,128)(2,1)}, bf16[2048,128]{1,0:T(8,128)(2,1)S(1)}, u32[]{:S(2)}) copy-start(bf16[2048,128]{1,0:T(8,128)(2,1)S(1)} %get-tuple-element.28.part_in) | copy-start | bytes 1572868
  101.7 1.9 copy-start.3
  103.6 29.9 %all-to-all-start.3 = ((bf16[16,2,128,128]{3,2,1,0:T(8,128)(2,1)}), bf16[16,2,128,128]{3,2,1,0:T(8,128)(2,1)}, u32[]{:S(2)}, u32[]{:S(2)}) async-start(bf16[16,2,128,128]{3,2,1,0:T(8,128)(2,1)} %bitcast.8), calls=%async_computation.3 | async-start | bytes 2097152 | tf_op jit(solution)/shard_map/all_to_all | solution.py:360
  108.6 1.0 copy-start.8
  109.6 23.9 %copy-start.1 = (bf16[3,768,128]{2,1,0:T(8,128)(2,1)S(1)}, bf16[3,768,128]{2,1,0:T(8,128)(2,1)}, u32[]{:S(2)}) copy-start(bf16[3,768,128]{2,1,0:T(8,128)(2,1)} %mix_all.11) | copy-start | bytes 1769476
  137.3 29.8 %all-to-all-start.4 = ((bf16[16,2,128,128]{3,2,1,0:T(8,128)(2,1)}), bf16[16,2,128,128]{3,2,1,0:T(8,128)(2,1)S(1)}, u32[]{:S(2)}, u32[]{:S(2)}) async-start(bf16[16,2,128,128]{3,2,1,0:T(8,128)(2,1)} %bitcast.24), calls=%async_computation.4 | async-start | bytes 2097152 | tf_op jit(solution)/shard_map/all_to_all | solution.py:360
  167.2 1.9 copy-start.4
  169.1 29.9 %all-to-all-start.5 = ((bf16[16,2,128,128]{3,2,1,0:T(8,128)(2,1)}), bf16[16,2,128,128]{3,2,1,0:T(8,128)(2,1)}, u32[]{:S(2)}, u32[]{:S(2)}) async-start(bf16[16,2,128,128]{3,2,1,0:T(8,128)(2,1)} %bitcast.12), calls=%async_computation.5 | async-start | bytes 2097152 | tf_op jit(solution)/shard_map/all_to_all | solution.py:360

commit v7 on v6

--- a/solution.py
+++ b/solution.py
@@ -173,8 +173,8 @@
 def receive(table_in, part_in, table, part, total, sems, more=lambda: None, far=None, near=None):
     waits = [start(table_in, table, sems.at[0])]
     if near is not None:
-        waits.append(start_parts(far, near, sems.at[2], 8))
-    waits.append(start_parts(part_in, part, sems.at[1], 2))
+        waits.append(start_parts(far, near, sems.at[2], 4))
+    waits.append(start_parts(part_in, part, sems.at[1], 1))
     total[...] = jnp.zeros_like(total)
     result = more()
     for copy in waits:
@@ -194,7 +194,7 @@
 ):
     def more():
         loads = weight_loads(layer, weight_all, bias_all, mix_all, weight, bias, mix, sems)
-        loads.append(start_parts(past_all.at[layer], past, sems.at[4], 2))
+        loads.append(start_parts(past_all.at[layer], past, sems.at[4], 1))
         return loads
 
     loads = receive(table_in, part_in, table, part, total, arrive, more, far, near)
@@ -224,7 +224,7 @@
     receive(table_in, part_in, table, part, total, arrive, far=far, near=near)
     add_arrived(table, blocks, near, total)
     state[...] = joined(part[...], total[...])
-    start_parts(state, state_out, sem.at[0], 4).wait()
+    start_parts(state, state_out, sem.at[0], 2).wait()
 
 
 def build_kernel(place, target, owner, slot, tiles, count, values, table, remote_blocks):

time: 203 us -> 203 us (level)
  no operation moved by 1% of the time
where the time goes in v7:
time: 203 us; the launch traced here: 201 us
  waiting for transfers between devices  113 us (56%)
  Pallas kernels  53.3 us (26%)
  starting transfers between devices  31.8 us (16%)
  local copies, waits for them, and re-layouts  2.14 us (1%)
    all_to_all x6, waiting for transfers between devices, exchange(): lax.all_to_all(send.reshape(peers, CAP, TILE, res), 'node', split_axis=0,...  113 us
    pallas_call x14, Pallas kernels, call(): pl.pallas_call(kernel, name=name, out_shape=tuple(outs), in_specs=in_spec...  53.3 us
    all_to_all x6, starting transfers between devices, exchange(): lax.all_to_all(send.reshape(peers, CAP, TILE, res), 'node', split_axis=0,...  31.8 us
  transfers between devices with their start and end apart: 6, of which 6 were waited for; matrix products, arithmetic and copies ran while one was open for 0% of the time, Pallas kernels for 17%

profile of v7, /device:TPU:9, one launch (start us, length us, event | category | flops | bytes accessed | tf_op | source)
XLA Modules:
  0.0 201.4 jit_solution(7485675607488853293)
XLA Ops:
  0.7 3.9 %conv_first.1 = (bf16[2048,256]{1,0:T(8,128)(2,1)}, bf16[32,128,128]{2,1,0:T(8,128)(2,1)}) custom-call(s32[1,2,16]{2,1,0:T(2,128)} %bitcast.20, bf16[2048,128]{1,0:T(8,128)(2,1)} %rest_0_.1, bf16[3,2048,128]{2,1,0:T(8,128)(2,1)} %past_all.5, bf16[3,256,512]{2,1,0:T(8,128)(2,1)} %weight_all.5, f32[3,512]{1,0:T(4,128)} %bias_all.5, bf16[3,768,128]{2,1,0:T(8,128)(2,1)} %mix_all.11), custom_call_target="tpu_custom_call" | custom-call | flops 671088640 | bytes 5576832 | tf_op jit(solution)/shard_map/conv_first/pallas_call | solution.py:34
  4.6 0.0 copy-start.5
  4.6 0.0 copy-start.6
  4.6 6.8 %all-to-all-start = ((bf16[16,2,128,128]{3,2,1,0:T(8,128)(2,1)}), bf16[16,2,128,128]{3,2,1,0:T(8,128)(2,1)S(1)}, u32[]{:S(2)}, u32[]{:S(2)}) async-start(bf16[16,2,128,128]{3,2,1,0:T(8,128)(2,1)} %bitcast.22), calls=%async_computation | async-start | bytes 2097152 | tf_op jit(solution)/shard_map/all_to_all | solution.py:360
  11.4 3.0 %sort_blocks.1 = (s32[1024]{0:T(1024)S(1)}, bf16[15,128,128]{2,1,0:T(8,128)(2,1)S(1)}) custom-call(s32[1]{0:T(128)} %bitcast.place, s32[47]{0:T(128)S(1)} %copy-done.13, s32[47]{0:T(128)S(1)} %copy-done.14, s32[47]{0:T(128)S(1)} %copy-done.15, s32[1,2,16]{2,1,0:T(2,128)S(1)} %bitcast.21, s32[1,16]{1,0:T(1,128)S(1)} %copy-done.16, bf16[47,128,128]{2,1,0:T(8,128)(2,1)} %values.13), custom_call_target="tpu_custom_call" | custom-call | flops 47000 | bytes 2036472 | tf_op jit(solution)/shard_map/sort_blocks/pallas_call | solution.py:34
  14.4 6.2 %under_first.3 = (bf16[2048,128]{1,0:T(8,128)(2,1)S(1)}, f32[2048,128]{1,0:T(8,128)}, f32[2048,256]{1,0:T(8,128)}) custom-call(s32[1024]{0:T(1024)S(1)} %get-tuple-element.19.table.table_in, bf16[47,128,128]{2,1,0:T(8,128)(2,1)} %values.13, bf16[2048,256]{1,0:T(8,128)(2,1)} %get-tuple-element.22.gated, bf16[3,768,128]{2,1,0:T(8,128)(2,1)} %mix_all.11, ...), custom_call_target="tpu_custom_call" | custom-call | flops 805306368 | bytes 7770112 | tf_op jit(solution)/shard_map/under_first/pallas_call | solution.py:34
  20.6 0.0 copy-start.9
  20.6 15.6 %all-to-all-done = bf16[16,2,128,128]{3,2,1,0:T(8,128)(2,1)S(1)} async-done(((bf16[16,2,128,128]{3,2,1,0:T(8,128)(2,1)}), bf16[16,2,128,128]{3,2,1,0:T(8,128)(2,1)S(1)}, u32[]{:S(2)}, u32[]{:S(2)}) %all-to-all-start) | async-done | bytes 1048608 | tf_op jit(solution)/shard_map/all_to_all | solution.py:360
  36.2 1.9 hop.3
  38.1 5.0 %all-to-all-start.1 = ((bf16[16,2,128,128]{3,2,1,0:T(8,128)(2,1)}), bf16[16,2,128,128]{3,2,1,0:T(8,128)(2,1)}, u32[]{:S(2)}, u32[]{:S(2)}) async-start(bf16[16,2,128,128]{3,2,1,0:T(8,128)(2,1)} %bitcast.4), calls=%async_computation.1 | async-start | bytes 2097152 | tf_op jit(solution)/shard_map/all_to_all | solution.py:360
  43.1 1.0 copy-done.10
  44.1 3.7 %under_second.3.part_in.rest_3_ = bf16[2048,128]{1,0:T(8,128)(2,1)S(1)} custom-call(s32[1024]{0:T(1024)S(1)} %get-tuple-element.19.table.table_in, bf16[47,128,128]{2,1,0:T(8,128)(2,1)} %values.13, bf16[15,128,128]{2,1,0:T(8,128)(2,1)S(1)} %get-tuple-element.20.blocks.rest_1_, bf16[32,128,128]{2,1,0:T(8,128)(2,1)} %bitcast.15, ...), custom_call_target="tpu_custom_call" | custom-call | flops 197132288 | bytes 5181440 | tf_op jit(solution)/shard_map/under_second/pallas_call | solution.py:34
  47.8 20.2 %all-to-all-done.1 = bf16[16,2,128,128]{3,2,1,0:T(8,128)(2,1)} async-done(((bf16[16,2,128,128]{3,2,1,0:T(8,128)(2,1)}), bf16[16,2,128,128]{3,2,1,0:T(8,128)(2,1)}, u32[]{:S(2)}, u32[]{:S(2)}) %all-to-all-start.1) | async-done | bytes 1048608 | tf_op jit(solution)/shard_map/all_to_all | solution.py:360
  68.1 3.6 %conv_next.2 = (bf16[2048,256]{1,0:T(8,128)(2,1)}, bf16[32,128,128]{2,1,0:T(8,128)(2,1)}) custom-call(s32[1024]{0:T(1024)S(1)} %get-tuple-element.19.table.table_in, bf16[15,128,128]{2,1,0:T(8,128)(2,1)S(1)} %get-tuple-element.20.blocks.rest_1_, bf16[32,128,128]{2,1,0:T(8,128)(2,1)} %bitcast.5.far.rest_2_, ...), custom_call_target="tpu_custom_call" | custom-call | flops 734003200 | bytes 7120896 | tf_op jit(solution)/shard_map/conv_next/pallas_call | solution.py:34
  71.7 5.0 %all-to-all-start.2 = ((bf16[16,2,128,128]{3,2,1,0:T(8,128)(2,1)}), bf16[16,2,128,128]{3,2,1,0:T(8,128)(2,1)S(1)}, u32[]{:S(2)}, u32[]{:S(2)}) async-start(bf16[16,2,128,128]{3,2,1,0:T(8,128)(2,1)} %bitcast.23), calls=%async_computation.2 | async-start | bytes 2097152 | tf_op jit(solution)/shard_map/all_to_all | solution.py:360
  76.7 7.1 %under_first.4 = (bf16[2048,128]{1,0:T(8,128)(2,1)S(1)}, f32[2048,128]{1,0:T(8,128)}, f32[2048,256]{1,0:T(8,128)}) custom-call(s32[1024]{0:T(1024)S(1)} %get-tuple-element.19.table.table_in, bf16[47,128,128]{2,1,0:T(8,128)(2,1)} %values.13, bf16[2048,256]{1,0:T(8,128)(2,1)} %get-tuple-element.26.gated, bf16[3,768,128]{2,1,0:T(8,128)(2,1)} %mix_all.11, ...), custom_call_target="tpu_custom_call" | custom-call | flops 805306368 | bytes 11407360 | tf_op jit(solution)/shard_map/under_first/pallas_call | solution.py:34
  83.8 0.0 copy-start.7
  83.8 17.7 %all-to-all-done.2 = bf16[16,2,128,128]{3,2,1,0:T(8,128)(2,1)S(1)} async-done(((bf16[16,2,128,128]{3,2,1,0:T(8,128)(2,1)}), bf16[16,2,128,128]{3,2,1,0:T(8,128)(2,1)S(1)}, u32[]{:S(2)}, u32[]{:S(2)}) %all-to-all-start.2) | async-done | bytes 1048608 | tf_op jit(solution)/shard_map/all_to_all | solution.py:360
  101.5 1.9 hop.4
  103.4 5.0 %all-to-all-start.3 = ((bf16[16,2,128,128]{3,2,1,0:T(8,128)(2,1)}), bf16[16,2,128,128]{3,2,1,0:T(8,128)(2,1)}, u32[]{:S(2)}, u32[]{:S(2)}) async-start(bf16[16,2,128,128]{3,2,1,0:T(8,128)(2,1)} %bitcast.8), calls=%async_computation.3 | async-start | bytes 2097152 | tf_op jit(solution)/shard_map/all_to_all | solution.py:360
  108.4 1.0 copy-done.8
  109.5 3.7 %under_second.4.part_in.rest_3_ = bf16[2048,128]{1,0:T(8,128)(2,1)S(1)} custom-call(s32[1024]{0:T(1024)S(1)} %get-tuple-element.19.table.table_in, bf16[47,128,128]{2,1,0:T(8,128)(2,1)} %values.13, bf16[15,128,128]{2,1,0:T(8,128)(2,1)S(1)} %get-tuple-element.20.blocks.rest_1_, bf16[32,128,128]{2,1,0:T(8,128)(2,1)} %bitcast.17, ...), custom_call_target="tpu_custom_call" | custom-call | flops 197132288 | bytes 5181440 | tf_op jit(solution)/shard_map/under_second/pallas_call | solution.py:34
  113.1 20.2 %all-to-all-done.3 = bf16[16,2,128,128]{3,2,1,0:T(8,128)(2,1)} async-done(((bf16[16,2,128,128]{3,2,1,0:T(8,128)(2,1)}), bf16[16,2,128,128]{3,2,1,0:T(8,128)(2,1)}, u32[]{:S(2)}, u32[]{:S(2)}) %all-to-all-start.3) | async-done | bytes 1048608 | tf_op jit(solution)/shard_map/all_to_all | solution.py:360
  133.4 3.7 %conv_next.3 = (bf16[2048,256]{1,0:T(8,128)(2,1)}, bf16[32,128,128]{2,1,0:T(8,128)(2,1)}) custom-call(s32[1024]{0:T(1024)S(1)} %get-tuple-element.19.table.table_in, bf16[15,128,128]{2,1,0:T(8,128)(2,1)S(1)} %get-tuple-element.20.blocks.rest_1_, bf16[32,128,128]{2,1,0:T(8,128)(2,1)} %bitcast.9.far.rest_2_, ...), custom_call_target="tpu_custom_call" | custom-call | flops 734003200 | bytes 7120896 | tf_op jit(solution)/shard_map/conv_next/pallas_call | solution.py:34
  137.1 5.0 %all-to-all-start.4 = ((bf16[16,2,128,128]{3,2,1,0:T(8,128)(2,1)}), bf16[16,2,128,128]{3,2,1,0:T(8,128)(2,1)S(1)}, u32[]{:S(2)}, u32[]{:S(2)}) async-start(bf16[16,2,128,128]{3,2,1,0:T(8,128)(2,1)} %bitcast.24), calls=%async_computation.4 | async-start | bytes 2097152 | tf_op jit(solution)/shard_map/all_to_all | solution.py:360
  142.1 6.8 %under_first.5 = (bf16[2048,128]{1,0:T(8,128)(2,1)S(1)}, f32[2048,128]{1,0:T(8,128)}, bf16[2048,256]{1,0:T(8,128)(2,1)}) custom-call(s32[1024]{0:T(1024)S(1)} %get-tuple-element.19.table.table_in, bf16[47,128,128]{2,1,0:T(8,128)(2,1)} %values.13, bf16[2048,256]{1,0:T(8,128)(2,1)} %get-tuple-element.31.gated, bf16[3,768,128]{2,1,0:T(8,128)(2,1)} %mix_all.11, ...), custom_call_target="tpu_custom_call" | custom-call | flops 805306368 | bytes 10358784 | tf_op jit(solution)/shard_map/under_first/pallas_call | solution.py:34
  148.9 18.0 %all-to-all-done.4 = bf16[16,2,128,128]{3,2,1,0:T(8,128)(2,1)S(1)} async-done(((bf16[16,2,128,128]{3,2,1,0:T(8,128)(2,1)}), bf16[16,2,128,128]{3,2,1,0:T(8,128)(2,1)S(1)}, u32[]{:S(2)}, u32[]{:S(2)}) %all-to-all-start.4) | async-done | bytes 1048608 | tf_op jit(solution)/shard_map/all_to_all | solution.py:360
  166.9 1.9 hop.5
  168.8 5.0 %all-to-all-start.5 = ((bf16[16,2,128,128]{3,2,1,0:T(8,128)(2,1)}), bf16[16,2,128,128]{3,2,1,0:T(8,128)(2,1)}, u32[]{:S(2)}, u32[]{:S(2)}) async-start(bf16[16,2,128,128]{3,2,1,0:T(8,128)(2,1)} %bitcast.12), calls=%async_computation.5 | async-start | bytes 2097152 | tf_op jit(solution)/shard_map/all_to_all | solution.py:360
  173.8 3.6 %under_second.5.part_in = bf16[2048,128]{1,0:T(8,128)(2,1)S(1)} custom-call(s32[1024]{0:T(1024)S(1)} %get-tuple-element.19.table.table_in, bf16[47,128,128]{2,1,0:T(8,128)(2,1)} %values.13, bf16[15,128,128]{2,1,0:T(8,128)(2,1)S(1)} %get-tuple-element.20.blocks.rest_1_, bf16[32,128,128]{2,1,0:T(8,128)(2,1)} %bitcast.19, ...), custom_call_target="tpu_custom_call" | custom-call | flops 197132288 | bytes 5181440 | tf_op jit(solution)/shard_map/under_second/pallas_call | solution.py:34
  177.4 21.3 %all-to-all-done.5 = bf16[16,2,128,128]{3,2,1,0:T(8,128)(2,1)} async-done(((bf16[16,2,128,128]{3,2,1,0:T(8,128)(2,1)}), bf16[16,2,128,128]{3,2,1,0:T(8,128)(2,1)}, u32[]{:S(2)}, u32[]{:S(2)}) %all-to-all-start.5) | async-done | bytes 1048608 | tf_op jit(solution)/shard_map/all_to_all | solution.py:360
  198.8 2.5 %last.1 = bf16[2048,128]{1,0:T(8,128)(2,1)} custom-call(s32[1024]{0:T(1024)S(1)} %get-tuple-element.19.table.table_in, bf16[15,128,128]{2,1,0:T(8,128)(2,1)S(1)} %get-tuple-element.20.blocks.rest_1_, bf16[32,128,128]{2,1,0:T(8,128)(2,1)} %bitcast.13.far, bf16[2048,128]{1,0:T(8,128)(2,1)S(1)} %under_second.5.part_in), custom_call_target="tpu_custom_call" | custom-call | flops 62914560 | bytes 2592768 | tf_op jit(solution)/shard_map/last/pallas_call | solution.py:34
  (28 shorter events, 0.1 us)
Async XLA Ops:
  0.6 10.7 %copy-start.12 = (s32[1,16,2]{1,2,0:T(2,128)S(1)}, s32[1,16,2]{1,2,0:T(2,128)}, u32[]{:S(2)}) copy-start(s32[1,16,2]{1,2,0:T(2,128)} %param.22) | copy-start | bytes 388
  0.6 10.7 %copy-start.13 = (s32[47]{0:T(128)S(1)}, s32[47]{0:T(128)}, u32[]{:S(2)}) copy-start(s32[47]{0:T(128)} %target.1) | copy-start | bytes 568
  0.7 10.7 %copy-start.14 = (s32[47]{0:T(128)S(1)}, s32[47]{0:T(128)}, u32[]{:S(2)}) copy-start(s32[47]{0:T(128)} %owner.1) | copy-start | bytes 568
  0.7 10.7 %copy-start.15 = (s32[47]{0:T(128)S(1)}, s32[47]{0:T(128)}, u32[]{:S(2)}) copy-start(s32[47]{0:T(128)} %slot.1) | copy-start | bytes 568
  0.7 10.7 %copy-start.16 = (s32[1,16]{1,0:T(1,128)S(1)}, s32[1,16]{1,0:T(1,128)}, u32[]{:S(2)}) copy-start(s32[1,16]{1,0:T(1,128)} %count.1) | copy-start | bytes 196
  4.6 9.8 %copy-start.5 = (bf16[3,256,256]{2,1,0:T(8,128)(2,1)S(1)}, bf16[3,256,256]{2,1,0:T(8,128)(2,1)}, u32[]{:S(2)}) copy-start(bf16[3,256,256]{2,1,0:T(8,128)(2,1)} %skip_all.5) | copy-start | bytes 1179652
  4.6 9.8 %copy-start.6 = (bf16[2048,128]{1,0:T(8,128)(2,1)S(1)}, bf16[2048,128]{1,0:T(8,128)(2,1)}, u32[]{:S(2)}) copy-start(bf16[2048,128]{1,0:T(8,128)(2,1)} %rest_0_.1) | copy-start | bytes 1572868
  4.6 31.6 %all-to-all-start = ((bf16[16,2,128,128]{3,2,1,0:T(8,128)(2,1)}), bf16[16,2,128,128]{3,2,1,0:T(8,128)(2,1)S(1)}, u32[]{:S(2)}, u32[]{:S(2)}) async-start(bf16[16,2,128,128]{3,2,1,0:T(8,128)(2,1)} %bitcast.22), calls=%async_computation | async-start | bytes 2097152 | tf_op jit(solution)/shard_map/all_to_all | solution.py:360
  20.6 17.4 %copy-start.9 = (bf16[2048,128]{1,0:T(8,128)(2,1)}, bf16[2048,128]{1,0:T(8,128)(2,1)S(1)}, u32[]{:S(2)}) copy-start(bf16[2048,128]{1,0:T(8,128)(2,1)S(1)} %get-tuple-element.23.part_in) | copy-start | bytes 1572868
  36.2 1.9 copy-start.2
  38.1 30.0 %all-to-all-start.1 = ((bf16[16,2,128,128]{3,2,1,0:T(8,128)(2,1)}), bf16[16,2,128,128]{3,2,1,0:T(8,128)(2,1)}, u32[]{:S(2)}, u32[]{:S(2)}) async-start(bf16[16,2,128,128]{3,2,1,0:T(8,128)(2,1)} %bitcast.4), calls=%async_computation.1 | async-start | bytes 2097152 | tf_op jit(solution)/shard_map/all_to_all | solution.py:360
  43.1 1.0 copy-start.10
  44.1 23.9 %copy-start = (bf16[3,768,128]{2,1,0:T(8,128)(2,1)S(1)}, bf16[3,768,128]{2,1,0:T(8,128)(2,1)}, u32[]{:S(2)}) copy-start(bf16[3,768,128]{2,1,0:T(8,128)(2,1)} %mix_all.11) | copy-start | bytes 1769476
  44.1 23.9 %copy-start.11 = (f32[3,512]{1,0:T(4,128)S(1)}, f32[3,512]{1,0:T(4,128)}, u32[]{:S(2)}) copy-start(f32[3,512]{1,0:T(4,128)} %bias_all.5) | copy-start | bytes 18436
  71.7 29.9 %all-to-all-start.2 = ((bf16[16,2,128,128]{3,2,1,0:T(8,128)(2,1)}), bf16[16,2,128,128]{3,2,1,0:T(8,128)(2,1)S(1)}, u32[]{:S(2)}, u32[]{:S(2)}) async-start(bf16[16,2,128,128]{3,2,1,0:T(8,128)(2,1)} %bitcast.23), calls=%async_computation.2 | async-start | bytes 2097152 | tf_op jit(solution)/shard_map/all_to_all | solution.py:360
  83.8 19.6 %copy-start.7 = (bf16[2048,128]{1,0:T(8,128)(2,1)}, bf16[2048,128]{1,0:T(8,128)(2,1)S(1)}, u32[]{:S(2)}) copy-start(bf16[2048,128]{1,0:T(8,128)(2,1)S(1)} %get-tuple-element.28.part_in) | copy-start | bytes 1572868
  101.5 1.9 copy-start.3
  103.4 30.0 %all-to-all-start.3 = ((bf16[16,2,128,128]{3,2,1,0:T(8,128)(2,1)}), bf16[16,2,128,128]{3,2,1,0:T(8,128)(2,1)}, u32[]{:S(2)}, u32[]{:S(2)}) async-start(bf16[16,2,128,128]{3,2,1,0:T(8,128)(2,1)} %bitcast.8), calls=%async_computation.3 | async-start | bytes 2097152 | tf_op jit(solution)/shard_map/all_to_all | solution.py:360
  108.4 1.0 copy-start.8
  109.5 23.9 %copy-start.1 = (bf16[3,768,128]{2,1,0:T(8,128)(2,1)S(1)}, bf16[3,768,128]{2,1,0:T(8,128)(2,1)}, u32[]{:S(2)}) copy-start(bf16[3,768,128]{2,1,0:T(8,128)(2,1)} %mix_all.11) | copy-start | bytes 1769476
  137.1 29.8 %all-to-all-start.4 = ((bf16[16,2,128,128]{3,2,1,0:T(8,128)(2,1)}), bf16[16,2,128,128]{3,2,1,0:T(8,128)(2,1)S(1)}, u32[]{:S(2)}, u32[]{:S(2)}) async-start(bf16[16,2,128,128]{3,2,1,0:T(8,128)(2,1)} %bitcast.24), calls=%async_computation.4 | async-start | bytes 2097152 | tf_op jit(solution)/shard_map/all_to_all | solution.py:360
  166.9 1.9 copy-start.4
  168.8 30.0 %all-to-all-start.5 = ((bf16[16,2,128,128]{3,2,1,0:T(8,128)(2,1)}), bf16[16,2,128,128]{3,2,1,0:T(8,128)(2,1)}, u32[]{:S(2)}, u32[]{:S(2)}) async-start(bf16[16,2,128,128]{3,2,1,0:T(8,128)(2,1)} %bitcast.12), calls=%async_computation.5 | async-start | bytes 2097152 | tf_op jit(solution)/shard_map/all_to_all | solution.py:360

commit v8 on v7

--- a/solution.py
+++ b/solution.py
@@ -20,7 +20,7 @@
 TARGET, SOURCE, PLACE, ROUTE, OWN, OTHER, FROM, SPARE = (SECTION * i for i in range(8))
 TABLE = 8 * SECTION
 COUNT = TABLE - 1
-GROUP = 4
+GROUP = 8
 
 
 def dot(a, b):
@@ -174,7 +174,8 @@
     waits = [start(table_in, table, sems.at[0])]
     if near is not None:
         waits.append(start_parts(far, near, sems.at[2], 4))
-    waits.append(start_parts(part_in, part, sems.at[1], 1))
+    if part is not None:
+        waits.append(start_parts(part_in, part, sems.at[1], 1))
     total[...] = jnp.zeros_like(total)
     result = more()
     for copy in waits:
@@ -210,11 +211,11 @@
 
 
 def hop_kernel(
-    table_in, blocks, far, part_in, send, field, table, part, total, arrive, send_sems
-):
-    receive(table_in, part_in, table, part, total, arrive)
+    table_in, blocks, far, part_in, send, field, table, total, arrive, send_sems
+):
+    receive(table_in, part_in, table, None, total, arrive)
     add_arrived(table, blocks, far, total)
-    field[...] = joined(part[...], total[...])
+    field[...] = joined(part_in[...], total[...])
     Sends(table, field, send, send_sems).wait()
 
 
@@ -383,7 +384,7 @@
         return pltpu.SemaphoreType.DMA((n,))
 
     arrival = [index, thin_field, wide_field, pltpu.VMEM((slots, TILE, res), BF16), sems(3)]
-    direct_arrival = [index, thin_field, wide_field, sems(2)]
+    direct_arrival = [index, wide_field, sems(1)]
     weights = (conv_cache, conv_weight, conv_bias, mix_weight)
     state = hidden_state
     skip = None
@@ -445,7 +446,7 @@
             "hop",
             (table, remote_blocks, far, total),
             (shape((slots, TILE, res), BF16),),
-            [HBM, VMEM, VMEM, HBM],
+            [HBM, VMEM, VMEM, VMEM],
             [HBM],
             hop_flops,
             [thin_field] + direct_arrival + [sems(slots // GROUP)],

time: 203 us -> 203 us (level)
  no operation moved by 1% of the time
where the time goes in v8:
time: 203 us; the launch traced here: 201 us
  waiting for transfers between devices  113 us (56%)
  Pallas kernels  53.2 us (26%)
  starting transfers between devices  31.8 us (16%)
  local copies, waits for them, and re-layouts  2.14 us (1%)
    all_to_all x6, waiting for transfers between devices, exchange(): lax.all_to_all(send.reshape(peers, CAP, TILE, res), 'node', split_axis=0,...  113 us
    pallas_call x14, Pallas kernels, call(): pl.pallas_call(kernel, name=name, out_shape=tuple(outs), in_specs=in_spec...  53.2 us
    all_to_all x6, starting transfers between devices, exchange(): lax.all_to_all(send.reshape(peers, CAP, TILE, res), 'node', split_axis=0,...  31.8 us
  transfers between devices with their start and end apart: 6, of which 6 were waited for; matrix products, arithmetic and copies ran while one was open for 0% of the time, Pallas kernels for 17%

profile of v8, /device:TPU:9, one launch (start us, length us, event | category | flops | bytes accessed | tf_op | source)
XLA Modules:
  0.0 201.4 jit_solution(5443599904803680415)
XLA Ops:
  0.7 3.9 %conv_first.1 = (bf16[2048,256]{1,0:T(8,128)(2,1)}, bf16[32,128,128]{2,1,0:T(8,128)(2,1)}) custom-call(s32[1,2,16]{2,1,0:T(2,128)} %bitcast.20, bf16[2048,128]{1,0:T(8,128)(2,1)} %rest_0_.1, bf16[3,2048,128]{2,1,0:T(8,128)(2,1)} %past_all.5, bf16[3,256,512]{2,1,0:T(8,128)(2,1)} %weight_all.5, f32[3,512]{1,0:T(4,128)} %bias_all.5, bf16[3,768,128]{2,1,0:T(8,128)(2,1)} %mix_all.11), custom_call_target="tpu_custom_call" | custom-call | flops 671088640 | bytes 5576832 | tf_op jit(solution)/shard_map/conv_first/pallas_call | solution.py:34
  4.6 0.0 copy-start.5
  4.6 0.0 copy-start.6
  4.6 6.8 %all-to-all-start = ((bf16[16,2,128,128]{3,2,1,0:T(8,128)(2,1)}), bf16[16,2,128,128]{3,2,1,0:T(8,128)(2,1)S(1)}, u32[]{:S(2)}, u32[]{:S(2)}) async-start(bf16[16,2,128,128]{3,2,1,0:T(8,128)(2,1)} %bitcast.22), calls=%async_computation | async-start | bytes 2097152 | tf_op jit(solution)/shard_map/all_to_all | solution.py:361
  11.4 3.0 %sort_blocks.1 = (s32[1024]{0:T(1024)S(1)}, bf16[15,128,128]{2,1,0:T(8,128)(2,1)S(1)}) custom-call(s32[1]{0:T(128)} %bitcast.place, s32[47]{0:T(128)S(1)} %copy-done.13, s32[47]{0:T(128)S(1)} %copy-done.14, s32[47]{0:T(128)S(1)} %copy-done.15, s32[1,2,16]{2,1,0:T(2,128)S(1)} %bitcast.21, s32[1,16]{1,0:T(1,128)S(1)} %copy-done.16, bf16[47,128,128]{2,1,0:T(8,128)(2,1)} %values.13), custom_call_target="tpu_custom_call" | custom-call | flops 47000 | bytes 2036472 | tf_op jit(solution)/shard_map/sort_blocks/pallas_call | solution.py:34
  14.4 6.2 %under_first.3 = (bf16[2048,128]{1,0:T(8,128)(2,1)S(1)}, f32[2048,128]{1,0:T(8,128)}, f32[2048,256]{1,0:T(8,128)}) custom-call(s32[1024]{0:T(1024)S(1)} %get-tuple-element.19.table.table_in, bf16[47,128,128]{2,1,0:T(8,128)(2,1)} %values.13, bf16[2048,256]{1,0:T(8,128)(2,1)} %get-tuple-element.22.gated, bf16[3,768,128]{2,1,0:T(8,128)(2,1)} %mix_all.11, ...), custom_call_target="tpu_custom_call" | custom-call | flops 805306368 | bytes 7770112 | tf_op jit(solution)/shard_map/under_first/pallas_call | solution.py:34
  20.6 0.0 copy-start.9
  20.6 15.6 %all-to-all-done = bf16[16,2,128,128]{3,2,1,0:T(8,128)(2,1)S(1)} async-done(((bf16[16,2,128,128]{3,2,1,0:T(8,128)(2,1)}), bf16[16,2,128,128]{3,2,1,0:T(8,128)(2,1)S(1)}, u32[]{:S(2)}, u32[]{:S(2)}) %all-to-all-start) | async-done | bytes 1048608 | tf_op jit(solution)/shard_map/all_to_all | solution.py:361
  36.2 1.9 hop.3
  38.1 5.0 %all-to-all-start.1 = ((bf16[16,2,128,128]{3,2,1,0:T(8,128)(2,1)}), bf16[16,2,128,128]{3,2,1,0:T(8,128)(2,1)}, u32[]{:S(2)}, u32[]{:S(2)}) async-start(bf16[16,2,128,128]{3,2,1,0:T(8,128)(2,1)} %bitcast.4), calls=%async_computation.1 | async-start | bytes 2097152 | tf_op jit(solution)/shard_map/all_to_all | solution.py:361
  43.1 1.0 copy-done.10
  44.1 3.7 %under_second.3.part_in.rest_3_ = bf16[2048,128]{1,0:T(8,128)(2,1)S(1)} custom-call(s32[1024]{0:T(1024)S(1)} %get-tuple-element.19.table.table_in, bf16[47,128,128]{2,1,0:T(8,128)(2,1)} %values.13, bf16[15,128,128]{2,1,0:T(8,128)(2,1)S(1)} %get-tuple-element.20.blocks.rest_1_, bf16[32,128,128]{2,1,0:T(8,128)(2,1)} %bitcast.15, ...), custom_call_target="tpu_custom_call" | custom-call | flops 197132288 | bytes 5181440 | tf_op jit(solution)/shard_map/under_second/pallas_call | solution.py:34
  47.8 20.2 %all-to-all-done.1 = bf16[16,2,128,128]{3,2,1,0:T(8,128)(2,1)} async-done(((bf16[16,2,128,128]{3,2,1,0:T(8,128)(2,1)}), bf16[16,2,128,128]{3,2,1,0:T(8,128)(2,1)}, u32[]{:S(2)}, u32[]{:S(2)}) %all-to-all-start.1) | async-done | bytes 1048608 | tf_op jit(solution)/shard_map/all_to_all | solution.py:361
  68.0 3.6 %conv_next.2 = (bf16[2048,256]{1,0:T(8,128)(2,1)}, bf16[32,128,128]{2,1,0:T(8,128)(2,1)}) custom-call(s32[1024]{0:T(1024)S(1)} %get-tuple-element.19.table.table_in, bf16[15,128,128]{2,1,0:T(8,128)(2,1)S(1)} %get-tuple-element.20.blocks.rest_1_, bf16[32,128,128]{2,1,0:T(8,128)(2,1)} %bitcast.5.far.rest_2_, ...), custom_call_target="tpu_custom_call" | custom-call | flops 734003200 | bytes 7120896 | tf_op jit(solution)/shard_map/conv_next/pallas_call | solution.py:34
  71.7 5.0 %all-to-all-start.2 = ((bf16[16,2,128,128]{3,2,1,0:T(8,128)(2,1)}), bf16[16,2,128,128]{3,2,1,0:T(8,128)(2,1)S(1)}, u32[]{:S(2)}, u32[]{:S(2)}) async-start(bf16[16,2,128,128]{3,2,1,0:T(8,128)(2,1)} %bitcast.23), calls=%async_computation.2 | async-start | bytes 2097152 | tf_op jit(solution)/shard_map/all_to_all | solution.py:361
  76.7 7.1 %under_first.4 = (bf16[2048,128]{1,0:T(8,128)(2,1)S(1)}, f32[2048,128]{1,0:T(8,128)}, f32[2048,256]{1,0:T(8,128)}) custom-call(s32[1024]{0:T(1024)S(1)} %get-tuple-element.19.table.table_in, bf16[47,128,128]{2,1,0:T(8,128)(2,1)} %values.13, bf16[2048,256]{1,0:T(8,128)(2,1)} %get-tuple-element.26.gated, bf16[3,768,128]{2,1,0:T(8,128)(2,1)} %mix_all.11, ...), custom_call_target="tpu_custom_call" | custom-call | flops 805306368 | bytes 11407360 | tf_op jit(solution)/shard_map/under_first/pallas_call | solution.py:34
  83.8 0.0 copy-start.7
  83.8 17.7 %all-to-all-done.2 = bf16[16,2,128,128]{3,2,1,0:T(8,128)(2,1)S(1)} async-done(((bf16[16,2,128,128]{3,2,1,0:T(8,128)(2,1)}), bf16[16,2,128,128]{3,2,1,0:T(8,128)(2,1)S(1)}, u32[]{:S(2)}, u32[]{:S(2)}) %all-to-all-start.2) | async-done | bytes 1048608 | tf_op jit(solution)/shard_map/all_to_all | solution.py:361
  101.5 1.9 hop.4
  103.4 5.0 %all-to-all-start.3 = ((bf16[16,2,128,128]{3,2,1,0:T(8,128)(2,1)}), bf16[16,2,128,128]{3,2,1,0:T(8,128)(2,1)}, u32[]{:S(2)}, u32[]{:S(2)}) async-start(bf16[16,2,128,128]{3,2,1,0:T(8,128)(2,1)} %bitcast.8), calls=%async_computation.3 | async-start | bytes 2097152 | tf_op jit(solution)/shard_map/all_to_all | solution.py:361
  108.4 1.0 copy-done.8
  109.5 3.7 %under_second.4.part_in.rest_3_ = bf16[2048,128]{1,0:T(8,128)(2,1)S(1)} custom-call(s32[1024]{0:T(1024)S(1)} %get-tuple-element.19.table.table_in, bf16[47,128,128]{2,1,0:T(8,128)(2,1)} %values.13, bf16[15,128,128]{2,1,0:T(8,128)(2,1)S(1)} %get-tuple-element.20.blocks.rest_1_, bf16[32,128,128]{2,1,0:T(8,128)(2,1)} %bitcast.17, ...), custom_call_target="tpu_custom_call" | custom-call | flops 197132288 | bytes 5181440 | tf_op jit(solution)/shard_map/under_second/pallas_call | solution.py:34
  113.1 20.2 %all-to-all-done.3 = bf16[16,2,128,128]{3,2,1,0:T(8,128)(2,1)} async-done(((bf16[16,2,128,128]{3,2,1,0:T(8,128)(2,1)}), bf16[16,2,128,128]{3,2,1,0:T(8,128)(2,1)}, u32[]{:S(2)}, u32[]{:S(2)}) %all-to-all-start.3) | async-done | bytes 1048608 | tf_op jit(solution)/shard_map/all_to_all | solution.py:361
  133.4 3.7 %conv_next.3 = (bf16[2048,256]{1,0:T(8,128)(2,1)}, bf16[32,128,128]{2,1,0:T(8,128)(2,1)}) custom-call(s32[1024]{0:T(1024)S(1)} %get-tuple-element.19.table.table_in, bf16[15,128,128]{2,1,0:T(8,128)(2,1)S(1)} %get-tuple-element.20.blocks.rest_1_, bf16[32,128,128]{2,1,0:T(8,128)(2,1)} %bitcast.9.far.rest_2_, ...), custom_call_target="tpu_custom_call" | custom-call | flops 734003200 | bytes 7120896 | tf_op jit(solution)/shard_map/conv_next/pallas_call | solution.py:34
  137.0 5.0 %all-to-all-start.4 = ((bf16[16,2,128,128]{3,2,1,0:T(8,128)(2,1)}), bf16[16,2,128,128]{3,2,1,0:T(8,128)(2,1)S(1)}, u32[]{:S(2)}, u32[]{:S(2)}) async-start(bf16[16,2,128,128]{3,2,1,0:T(8,128)(2,1)} %bitcast.24), calls=%async_computation.4 | async-start | bytes 2097152 | tf_op jit(solution)/shard_map/all_to_all | solution.py:361
  142.1 6.8 %under_first.5 = (bf16[2048,128]{1,0:T(8,128)(2,1)S(1)}, f32[2048,128]{1,0:T(8,128)}, bf16[2048,256]{1,0:T(8,128)(2,1)}) custom-call(s32[1024]{0:T(1024)S(1)} %get-tuple-element.19.table.table_in, bf16[47,128,128]{2,1,0:T(8,128)(2,1)} %values.13, bf16[2048,256]{1,0:T(8,128)(2,1)} %get-tuple-element.31.gated, bf16[3,768,128]{2,1,0:T(8,128)(2,1)} %mix_all.11, ...), custom_call_target="tpu_custom_call" | custom-call | flops 805306368 | bytes 10358784 | tf_op jit(solution)/shard_map/under_first/pallas_call | solution.py:34
  148.9 18.0 %all-to-all-done.4 = bf16[16,2,128,128]{3,2,1,0:T(8,128)(2,1)S(1)} async-done(((bf16[16,2,128,128]{3,2,1,0:T(8,128)(2,1)}), bf16[16,2,128,128]{3,2,1,0:T(8,128)(2,1)S(1)}, u32[]{:S(2)}, u32[]{:S(2)}) %all-to-all-start.4) | async-done | bytes 1048608 | tf_op jit(solution)/shard_map/all_to_all | solution.py:361
  166.9 1.9 hop.5
  168.8 5.0 %all-to-all-start.5 = ((bf16[16,2,128,128]{3,2,1,0:T(8,128)(2,1)}), bf16[16,2,128,128]{3,2,1,0:T(8,128)(2,1)}, u32[]{:S(2)}, u32[]{:S(2)}) async-start(bf16[16,2,128,128]{3,2,1,0:T(8,128)(2,1)} %bitcast.12), calls=%async_computation.5 | async-start | bytes 2097152 | tf_op jit(solution)/shard_map/all_to_all | solution.py:361
  173.8 3.6 %under_second.5.part_in = bf16[2048,128]{1,0:T(8,128)(2,1)S(1)} custom-call(s32[1024]{0:T(1024)S(1)} %get-tuple-element.19.table.table_in, bf16[47,128,128]{2,1,0:T(8,128)(2,1)} %values.13, bf16[15,128,128]{2,1,0:T(8,128)(2,1)S(1)} %get-tuple-element.20.blocks.rest_1_, bf16[32,128,128]{2,1,0:T(8,128)(2,1)} %bitcast.19, ...), custom_call_target="tpu_custom_call" | custom-call | flops 197132288 | bytes 5181440 | tf_op jit(solution)/shard_map/under_second/pallas_call | solution.py:34
  177.4 21.3 %all-to-all-done.5 = bf16[16,2,128,128]{3,2,1,0:T(8,128)(2,1)} async-done(((bf16[16,2,128,128]{3,2,1,0:T(8,128)(2,1)}), bf16[16,2,128,128]{3,2,1,0:T(8,128)(2,1)}, u32[]{:S(2)}, u32[]{:S(2)}) %all-to-all-start.5) | async-done | bytes 1048608 | tf_op jit(solution)/shard_map/all_to_all | solution.py:361
  198.8 2.5 %last.1 = bf16[2048,128]{1,0:T(8,128)(2,1)} custom-call(s32[1024]{0:T(1024)S(1)} %get-tuple-element.19.table.table_in, bf16[15,128,128]{2,1,0:T(8,128)(2,1)S(1)} %get-tuple-element.20.blocks.rest_1_, bf16[32,128,128]{2,1,0:T(8,128)(2,1)} %bitcast.13.far, bf16[2048,128]{1,0:T(8,128)(2,1)S(1)} %under_second.5.part_in), custom_call_target="tpu_custom_call" | custom-call | flops 62914560 | bytes 2592768 | tf_op jit(solution)/shard_map/last/pallas_call | solution.py:34
  (28 shorter events, 0.1 us)
Async XLA Ops:
  0.6 10.7 %copy-start.12 = (s32[1,16,2]{1,2,0:T(2,128)S(1)}, s32[1,16,2]{1,2,0:T(2,128)}, u32[]{:S(2)}) copy-start(s32[1,16,2]{1,2,0:T(2,128)} %param.22) | copy-start | bytes 388
  0.6 10.7 %copy-start.13 = (s32[47]{0:T(128)S(1)}, s32[47]{0:T(128)}, u32[]{:S(2)}) copy-start(s32[47]{0:T(128)} %target.1) | copy-start | bytes 568
  0.7 10.7 %copy-start.14 = (s32[47]{0:T(128)S(1)}, s32[47]{0:T(128)}, u32[]{:S(2)}) copy-start(s32[47]{0:T(128)} %owner.1) | copy-start | bytes 568
  0.7 10.7 %copy-start.15 = (s32[47]{0:T(128)S(1)}, s32[47]{0:T(128)}, u32[]{:S(2)}) copy-start(s32[47]{0:T(128)} %slot.1) | copy-start | bytes 568
  0.7 10.7 %copy-start.16 = (s32[1,16]{1,0:T(1,128)S(1)}, s32[1,16]{1,0:T(1,128)}, u32[]{:S(2)}) copy-start(s32[1,16]{1,0:T(1,128)} %count.1) | copy-start | bytes 196
  4.6 9.8 %copy-start.5 = (bf16[3,256,256]{2,1,0:T(8,128)(2,1)S(1)}, bf16[3,256,256]{2,1,0:T(8,128)(2,1)}, u32[]{:S(2)}) copy-start(bf16[3,256,256]{2,1,0:T(8,128)(2,1)} %skip_all.5) | copy-start | bytes 1179652
  4.6 9.8 %copy-start.6 = (bf16[2048,128]{1,0:T(8,128)(2,1)S(1)}, bf16[2048,128]{1,0:T(8,128)(2,1)}, u32[]{:S(2)}) copy-start(bf16[2048,128]{1,0:T(8,128)(2,1)} %rest_0_.1) | copy-start | bytes 1572868
  4.6 31.6 %all-to-all-start = ((bf16[16,2,128,128]{3,2,1,0:T(8,128)(2,1)}), bf16[16,2,128,128]{3,2,1,0:T(8,128)(2,1)S(1)}, u32[]{:S(2)}, u32[]{:S(2)}) async-start(bf16[16,2,128,128]{3,2,1,0:T(8,128)(2,1)} %bitcast.22), calls=%async_computation | async-start | bytes 2097152 | tf_op jit(solution)/shard_map/all_to_all | solution.py:361
  20.6 17.4 %copy-start.9 = (bf16[2048,128]{1,0:T(8,128)(2,1)}, bf16[2048,128]{1,0:T(8,128)(2,1)S(1)}, u32[]{:S(2)}) copy-start(bf16[2048,128]{1,0:T(8,128)(2,1)S(1)} %get-tuple-element.23.part_in) | copy-start | bytes 1572868
  36.2 1.9 copy-start.2
  38.1 30.0 %all-to-all-start.1 = ((bf16[16,2,128,128]{3,2,1,0:T(8,128)(2,1)}), bf16[16,2,128,128]{3,2,1,0:T(8,128)(2,1)}, u32[]{:S(2)}, u32[]{:S(2)}) async-start(bf16[16,2,128,128]{3,2,1,0:T(8,128)(2,1)} %bitcast.4), calls=%async_computation.1 | async-start | bytes 2097152 | tf_op jit(solution)/shard_map/all_to_all | solution.py:361
  43.1 1.0 copy-start.10
  44.1 23.9 %copy-start = (bf16[3,768,128]{2,1,0:T(8,128)(2,1)S(1)}, bf16[3,768,128]{2,1,0:T(8,128)(2,1)}, u32[]{:S(2)}) copy-start(bf16[3,768,128]{2,1,0:T(8,128)(2,1)} %mix_all.11) | copy-start | bytes 1769476
  44.1 23.9 %copy-start.11 = (f32[3,512]{1,0:T(4,128)S(1)}, f32[3,512]{1,0:T(4,128)}, u32[]{:S(2)}) copy-start(f32[3,512]{1,0:T(4,128)} %bias_all.5) | copy-start | bytes 18436
  71.7 29.8 %all-to-all-start.2 = ((bf16[16,2,128,128]{3,2,1,0:T(8,128)(2,1)}), bf16[16,2,128,128]{3,2,1,0:T(8,128)(2,1)S(1)}, u32[]{:S(2)}, u32[]{:S(2)}) async-start(bf16[16,2,128,128]{3,2,1,0:T(8,128)(2,1)} %bitcast.23), calls=%async_computation.2 | async-start | bytes 2097152 | tf_op jit(solution)/shard_map/all_to_all | solution.py:361
  83.8 19.6 %copy-start.7 = (bf16[2048,128]{1,0:T(8,128)(2,1)}, bf16[2048,128]{1,0:T(8,128)(2,1)S(1)}, u32[]{:S(2)}) copy-start(bf16[2048,128]{1,0:T(8,128)(2,1)S(1)} %get-tuple-element.28.part_in) | copy-start | bytes 1572868
  101.5 1.9 copy-start.3
  103.4 30.0 %all-to-all-start.3 = ((bf16[16,2,128,128]{3,2,1,0:T(8,128)(2,1)}), bf16[16,2,128,128]{3,2,1,0:T(8,128)(2,1)}, u32[]{:S(2)}, u32[]{:S(2)}) async-start(bf16[16,2,128,128]{3,2,1,0:T(8,128)(2,1)} %bitcast.8), calls=%async_computation.3 | async-start | bytes 2097152 | tf_op jit(solution)/shard_map/all_to_all | solution.py:361
  108.4 1.0 copy-start.8
  109.4 23.9 %copy-start.1 = (bf16[3,768,128]{2,1,0:T(8,128)(2,1)S(1)}, bf16[3,768,128]{2,1,0:T(8,128)(2,1)}, u32[]{:S(2)}) copy-start(bf16[3,768,128]{2,1,0:T(8,128)(2,1)} %mix_all.11) | copy-start | bytes 1769476
  137.0 29.9 %all-to-all-start.4 = ((bf16[16,2,128,128]{3,2,1,0:T(8,128)(2,1)}), bf16[16,2,128,128]{3,2,1,0:T(8,128)(2,1)S(1)}, u32[]{:S(2)}, u32[]{:S(2)}) async-start(bf16[16,2,128,128]{3,2,1,0:T(8,128)(2,1)} %bitcast.24), calls=%async_computation.4 | async-start | bytes 2097152 | tf_op jit(solution)/shard_map/all_to_all | solution.py:361
  166.9 1.9 copy-start.4
  168.8 29.9 %all-to-all-start.5 = ((bf16[16,2,128,128]{3,2,1,0:T(8,128)(2,1)}), bf16[16,2,128,128]{3,2,1,0:T(8,128)(2,1)}, u32[]{:S(2)}, u32[]{:S(2)}) async-start(bf16[16,2,128,128]{3,2,1,0:T(8,128)(2,1)} %bitcast.12), calls=%async_computation.5 | async-start | bytes 2097152 | tf_op jit(solution)/shard_map/all_to_all | solution.py:361

commit v9 on v8

--- a/solution.py
+++ b/solution.py
@@ -153,12 +153,13 @@
 
     def ready(i):
         if i == 0:
-            for copy in loads:
+            for copy in loads[:2]:
                 copy.wait()
         for copy in pieces[i]:
             copy.wait()
 
     copies = [convolve(past, state, weight, bias, gated, gated_out, sems.at[3], ready)]
+    loads[2].wait()
     second[...] = dot(gated[...], mix[...]).astype(BF16)
     routes.wait()
     def tile_of(place):
@@ -201,9 +202,10 @@
     loads = receive(table_in, part_in, table, part, total, arrive, more, far, near)
     add_arrived(table, blocks, near, total)
     state[...] = joined(part[...], total[...])
-    for copy in loads:
+    for copy in loads[:2] + loads[3:]:
         copy.wait()
     copies = [convolve(past, state, weight, bias, gated, gated_out, sems.at[3])]
+    loads[2].wait()
     second[...] = dot(gated[...], mix[...]).astype(BF16)
     copies.append(Sends(table, second, send, send_sems))
     for copy in copies:

time: 203 us -> 203 us (level)
  no operation moved by 1% of the time
where the time goes in v9:
time: 203 us; the launch traced here: 202 us
  waiting for transfers between devices  113 us (56%)
  Pallas kernels  53.5 us (26%)
  starting transfers between devices  31.6 us (16%)
  local copies, waits for them, and re-layouts  2.14 us (1%)
    all_to_all x6, waiting for transfers between devices, exchange(): lax.all_to_all(send.reshape(peers, CAP, TILE, res), 'node', split_axis=0,...  113 us
    pallas_call x14, Pallas kernels, call(): pl.pallas_call(kernel, name=name, out_shape=tuple(outs), in_specs=in_spec...  53.5 us
    all_to_all x6, starting transfers between devices, exchange(): lax.all_to_all(send.reshape(peers, CAP, TILE, res), 'node', split_axis=0,...  31.6 us
  transfers between devices with their start and end apart: 6, of which 6 were waited for; matrix products, arithmetic and copies ran while one was open for 0% of the time, Pallas kernels for 17%

profile of v9, /device:TPU:9, one launch (start us, length us, event | category | flops | bytes accessed | tf_op | source)
XLA Modules:
  0.0 201.5 jit_solution(1261361821136875390)
XLA Ops:
  0.7 4.0 %conv_first.1 = (bf16[2048,256]{1,0:T(8,128)(2,1)}, bf16[32,128,128]{2,1,0:T(8,128)(2,1)}) custom-call(s32[1,2,16]{2,1,0:T(2,128)} %bitcast.20, bf16[2048,128]{1,0:T(8,128)(2,1)} %rest_0_.1, bf16[3,2048,128]{2,1,0:T(8,128)(2,1)} %past_all.5, bf16[3,256,512]{2,1,0:T(8,128)(2,1)} %weight_all.5, f32[3,512]{1,0:T(4,128)} %bias_all.5, bf16[3,768,128]{2,1,0:T(8,128)(2,1)} %mix_all.11), custom_call_target="tpu_custom_call" | custom-call | flops 671088640 | bytes 5576832 | tf_op jit(solution)/shard_map/conv_first/pallas_call | solution.py:34
  4.7 0.0 copy-start.5
  4.7 0.0 copy-start.6
  4.7 6.8 %all-to-all-start = ((bf16[16,2,128,128]{3,2,1,0:T(8,128)(2,1)}), bf16[16,2,128,128]{3,2,1,0:T(8,128)(2,1)S(1)}, u32[]{:S(2)}, u32[]{:S(2)}) async-start(bf16[16,2,128,128]{3,2,1,0:T(8,128)(2,1)} %bitcast.22), calls=%async_computation | async-start | bytes 2097152 | tf_op jit(solution)/shard_map/all_to_all | solution.py:363
  11.5 3.0 %sort_blocks.1 = (s32[1024]{0:T(1024)S(1)}, bf16[15,128,128]{2,1,0:T(8,128)(2,1)S(1)}) custom-call(s32[1]{0:T(128)} %bitcast.place, s32[47]{0:T(128)S(1)} %copy-done.13, s32[47]{0:T(128)S(1)} %copy-done.14, s32[47]{0:T(128)S(1)} %copy-done.15, s32[1,2,16]{2,1,0:T(2,128)S(1)} %bitcast.21, s32[1,16]{1,0:T(1,128)S(1)} %copy-done.16, bf16[47,128,128]{2,1,0:T(8,128)(2,1)} %values.13), custom_call_target="tpu_custom_call" | custom-call | flops 47000 | bytes 2036472 | tf_op jit(solution)/shard_map/sort_blocks/pallas_call | solution.py:34
  14.5 6.2 %under_first.3 = (bf16[2048,128]{1,0:T(8,128)(2,1)S(1)}, f32[2048,128]{1,0:T(8,128)}, f32[2048,256]{1,0:T(8,128)}) custom-call(s32[1024]{0:T(1024)S(1)} %get-tuple-element.19.table.table_in, bf16[47,128,128]{2,1,0:T(8,128)(2,1)} %values.13, bf16[2048,256]{1,0:T(8,128)(2,1)} %get-tuple-element.22.gated, bf16[3,768,128]{2,1,0:T(8,128)(2,1)} %mix_all.11, ...), custom_call_target="tpu_custom_call" | custom-call | flops 805306368 | bytes 7770112 | tf_op jit(solution)/shard_map/under_first/pallas_call | solution.py:34
  20.7 0.0 copy-start.9
  20.8 15.6 %all-to-all-done = bf16[16,2,128,128]{3,2,1,0:T(8,128)(2,1)S(1)} async-done(((bf16[16,2,128,128]{3,2,1,0:T(8,128)(2,1)}), bf16[16,2,128,128]{3,2,1,0:T(8,128)(2,1)S(1)}, u32[]{:S(2)}, u32[]{:S(2)}) %all-to-all-start) | async-done | bytes 1048608 | tf_op jit(solution)/shard_map/all_to_all | solution.py:363
  36.3 1.9 hop.3
  38.2 5.0 %all-to-all-start.1 = ((bf16[16,2,128,128]{3,2,1,0:T(8,128)(2,1)}), bf16[16,2,128,128]{3,2,1,0:T(8,128)(2,1)}, u32[]{:S(2)}, u32[]{:S(2)}) async-start(bf16[16,2,128,128]{3,2,1,0:T(8,128)(2,1)} %bitcast.4), calls=%async_computation.1 | async-start | bytes 2097152 | tf_op jit(solution)/shard_map/all_to_all | solution.py:363
  43.2 1.0 copy-done.10
  44.2 3.7 %under_second.3.part_in.rest_3_ = bf16[2048,128]{1,0:T(8,128)(2,1)S(1)} custom-call(s32[1024]{0:T(1024)S(1)} %get-tuple-element.19.table.table_in, bf16[47,128,128]{2,1,0:T(8,128)(2,1)} %values.13, bf16[15,128,128]{2,1,0:T(8,128)(2,1)S(1)} %get-tuple-element.20.blocks.rest_1_, bf16[32,128,128]{2,1,0:T(8,128)(2,1)} %bitcast.15, ...), custom_call_target="tpu_custom_call" | custom-call | flops 197132288 | bytes 5181440 | tf_op jit(solution)/shard_map/under_second/pallas_call | solution.py:34
  47.9 20.2 %all-to-all-done.1 = bf16[16,2,128,128]{3,2,1,0:T(8,128)(2,1)} async-done(((bf16[16,2,128,128]{3,2,1,0:T(8,128)(2,1)}), bf16[16,2,128,128]{3,2,1,0:T(8,128)(2,1)}, u32[]{:S(2)}, u32[]{:S(2)}) %all-to-all-start.1) | async-done | bytes 1048608 | tf_op jit(solution)/shard_map/all_to_all | solution.py:363
  68.1 3.7 %conv_next.2 = (bf16[2048,256]{1,0:T(8,128)(2,1)}, bf16[32,128,128]{2,1,0:T(8,128)(2,1)}) custom-call(s32[1024]{0:T(1024)S(1)} %get-tuple-element.19.table.table_in, bf16[15,128,128]{2,1,0:T(8,128)(2,1)S(1)} %get-tuple-element.20.blocks.rest_1_, bf16[32,128,128]{2,1,0:T(8,128)(2,1)} %bitcast.5.far.rest_2_, ...), custom_call_target="tpu_custom_call" | custom-call | flops 734003200 | bytes 7120896 | tf_op jit(solution)/shard_map/conv_next/pallas_call | solution.py:34
  71.9 5.0 %all-to-all-start.2 = ((bf16[16,2,128,128]{3,2,1,0:T(8,128)(2,1)}), bf16[16,2,128,128]{3,2,1,0:T(8,128)(2,1)S(1)}, u32[]{:S(2)}, u32[]{:S(2)}) async-start(bf16[16,2,128,128]{3,2,1,0:T(8,128)(2,1)} %bitcast.23), calls=%async_computation.2 | async-start | bytes 2097152 | tf_op jit(solution)/shard_map/all_to_all | solution.py:363
  76.9 7.1 %under_first.4 = (bf16[2048,128]{1,0:T(8,128)(2,1)S(1)}, f32[2048,128]{1,0:T(8,128)}, f32[2048,256]{1,0:T(8,128)}) custom-call(s32[1024]{0:T(1024)S(1)} %get-tuple-element.19.table.table_in, bf16[47,128,128]{2,1,0:T(8,128)(2,1)} %values.13, bf16[2048,256]{1,0:T(8,128)(2,1)} %get-tuple-element.26.gated, bf16[3,768,128]{2,1,0:T(8,128)(2,1)} %mix_all.11, ...), custom_call_target="tpu_custom_call" | custom-call | flops 805306368 | bytes 11407360 | tf_op jit(solution)/shard_map/under_first/pallas_call | solution.py:34
  84.0 0.0 copy-start.7
  84.0 17.7 %all-to-all-done.2 = bf16[16,2,128,128]{3,2,1,0:T(8,128)(2,1)S(1)} async-done(((bf16[16,2,128,128]{3,2,1,0:T(8,128)(2,1)}), bf16[16,2,128,128]{3,2,1,0:T(8,128)(2,1)S(1)}, u32[]{:S(2)}, u32[]{:S(2)}) %all-to-all-start.2) | async-done | bytes 1048608 | tf_op jit(solution)/shard_map/all_to_all | solution.py:363
  101.7 1.9 hop.4
  103.6 5.0 %all-to-all-start.3 = ((bf16[16,2,128,128]{3,2,1,0:T(8,128)(2,1)}), bf16[16,2,128,128]{3,2,1,0:T(8,128)(2,1)}, u32[]{:S(2)}, u32[]{:S(2)}) async-start(bf16[16,2,128,128]{3,2,1,0:T(8,128)(2,1)} %bitcast.8), calls=%async_computation.3 | async-start | bytes 2097152 | tf_op jit(solution)/shard_map/all_to_all | solution.py:363
  108.6 1.0 copy-done.8
  109.6 3.7 %under_second.4.part_in.rest_3_ = bf16[2048,128]{1,0:T(8,128)(2,1)S(1)} custom-call(s32[1024]{0:T(1024)S(1)} %get-tuple-element.19.table.table_in, bf16[47,128,128]{2,1,0:T(8,128)(2,1)} %values.13, bf16[15,128,128]{2,1,0:T(8,128)(2,1)S(1)} %get-tuple-element.20.blocks.rest_1_, bf16[32,128,128]{2,1,0:T(8,128)(2,1)} %bitcast.17, ...), custom_call_target="tpu_custom_call" | custom-call | flops 197132288 | bytes 5181440 | tf_op jit(solution)/shard_map/under_second/pallas_call | solution.py:34
  113.3 20.2 %all-to-all-done.3 = bf16[16,2,128,128]{3,2,1,0:T(8,128)(2,1)} async-done(((bf16[16,2,128,128]{3,2,1,0:T(8,128)(2,1)}), bf16[16,2,128,128]{3,2,1,0:T(8,128)(2,1)}, u32[]{:S(2)}, u32[]{:S(2)}) %all-to-all-start.3) | async-done | bytes 1048608 | tf_op jit(solution)/shard_map/all_to_all | solution.py:363
  133.5 3.8 %conv_next.3 = (bf16[2048,256]{1,0:T(8,128)(2,1)}, bf16[32,128,128]{2,1,0:T(8,128)(2,1)}) custom-call(s32[1024]{0:T(1024)S(1)} %get-tuple-element.19.table.table_in, bf16[15,128,128]{2,1,0:T(8,128)(2,1)S(1)} %get-tuple-element.20.blocks.rest_1_, bf16[32,128,128]{2,1,0:T(8,128)(2,1)} %bitcast.9.far.rest_2_, ...), custom_call_target="tpu_custom_call" | custom-call | flops 734003200 | bytes 7120896 | tf_op jit(solution)/shard_map/conv_next/pallas_call | solution.py:34
  137.3 5.0 %all-to-all-start.4 = ((bf16[16,2,128,128]{3,2,1,0:T(8,128)(2,1)}), bf16[16,2,128,128]{3,2,1,0:T(8,128)(2,1)S(1)}, u32[]{:S(2)}, u32[]{:S(2)}) async-start(bf16[16,2,128,128]{3,2,1,0:T(8,128)(2,1)} %bitcast.24), calls=%async_computation.4 | async-start | bytes 2097152 | tf_op jit(solution)/shard_map/all_to_all | solution.py:363
  142.3 6.8 %under_first.5 = (bf16[2048,128]{1,0:T(8,128)(2,1)S(1)}, f32[2048,128]{1,0:T(8,128)}, bf16[2048,256]{1,0:T(8,128)(2,1)}) custom-call(s32[1024]{0:T(1024)S(1)} %get-tuple-element.19.table.table_in, bf16[47,128,128]{2,1,0:T(8,128)(2,1)} %values.13, bf16[2048,256]{1,0:T(8,128)(2,1)} %get-tuple-element.31.gated, bf16[3,768,128]{2,1,0:T(8,128)(2,1)} %mix_all.11, ...), custom_call_target="tpu_custom_call" | custom-call | flops 805306368 | bytes 10358784 | tf_op jit(solution)/shard_map/under_first/pallas_call | solution.py:34
  149.1 18.0 %all-to-all-done.4 = bf16[16,2,128,128]{3,2,1,0:T(8,128)(2,1)S(1)} async-done(((bf16[16,2,128,128]{3,2,1,0:T(8,128)(2,1)}), bf16[16,2,128,128]{3,2,1,0:T(8,128)(2,1)S(1)}, u32[]{:S(2)}, u32[]{:S(2)}) %all-to-all-start.4) | async-done | bytes 1048608 | tf_op jit(solution)/shard_map/all_to_all | solution.py:363
  167.1 1.9 hop.5
  169.0 5.0 %all-to-all-start.5 = ((bf16[16,2,128,128]{3,2,1,0:T(8,128)(2,1)}), bf16[16,2,128,128]{3,2,1,0:T(8,128)(2,1)}, u32[]{:S(2)}, u32[]{:S(2)}) async-start(bf16[16,2,128,128]{3,2,1,0:T(8,128)(2,1)} %bitcast.12), calls=%async_computation.5 | async-start | bytes 2097152 | tf_op jit(solution)/shard_map/all_to_all | solution.py:363
  174.0 3.6 %under_second.5.part_in = bf16[2048,128]{1,0:T(8,128)(2,1)S(1)} custom-call(s32[1024]{0:T(1024)S(1)} %get-tuple-element.19.table.table_in, bf16[47,128,128]{2,1,0:T(8,128)(2,1)} %values.13, bf16[15,128,128]{2,1,0:T(8,128)(2,1)S(1)} %get-tuple-element.20.blocks.rest_1_, bf16[32,128,128]{2,1,0:T(8,128)(2,1)} %bitcast.19, ...), custom_call_target="tpu_custom_call" | custom-call | flops 197132288 | bytes 5181440 | tf_op jit(solution)/shard_map/under_second/pallas_call | solution.py:34
  177.6 21.3 %all-to-all-done.5 = bf16[16,2,128,128]{3,2,1,0:T(8,128)(2,1)} async-done(((bf16[16,2,128,128]{3,2,1,0:T(8,128)(2,1)}), bf16[16,2,128,128]{3,2,1,0:T(8,128)(2,1)}, u32[]{:S(2)}, u32[]{:S(2)}) %all-to-all-start.5) | async-done | bytes 1048608 | tf_op jit(solution)/shard_map/all_to_all | solution.py:363
  198.9 2.5 %last.1 = bf16[2048,128]{1,0:T(8,128)(2,1)} custom-call(s32[1024]{0:T(1024)S(1)} %get-tuple-element.19.table.table_in, bf16[15,128,128]{2,1,0:T(8,128)(2,1)S(1)} %get-tuple-element.20.blocks.rest_1_, bf16[32,128,128]{2,1,0:T(8,128)(2,1)} %bitcast.13.far, bf16[2048,128]{1,0:T(8,128)(2,1)S(1)} %under_second.5.part_in), custom_call_target="tpu_custom_call" | custom-call | flops 62914560 | bytes 2592768 | tf_op jit(solution)/shard_map/last/pallas_call | solution.py:34
  (28 shorter events, 0.1 us)
Async XLA Ops:
  0.6 10.8 %copy-start.12 = (s32[1,16,2]{1,2,0:T(2,128)S(1)}, s32[1,16,2]{1,2,0:T(2,128)}, u32[]{:S(2)}) copy-start(s32[1,16,2]{1,2,0:T(2,128)} %param.22) | copy-start | bytes 388
  0.6 10.8 %copy-start.13 = (s32[47]{0:T(128)S(1)}, s32[47]{0:T(128)}, u32[]{:S(2)}) copy-start(s32[47]{0:T(128)} %target.1) | copy-start | bytes 568
  0.7 10.8 %copy-start.14 = (s32[47]{0:T(128)S(1)}, s32[47]{0:T(128)}, u32[]{:S(2)}) copy-start(s32[47]{0:T(128)} %owner.1) | copy-start | bytes 568
  0.7 10.8 %copy-start.15 = (s32[47]{0:T(128)S(1)}, s32[47]{0:T(128)}, u32[]{:S(2)}) copy-start(s32[47]{0:T(128)} %slot.1) | copy-start | bytes 568
  0.7 10.8 %copy-start.16 = (s32[1,16]{1,0:T(1,128)S(1)}, s32[1,16]{1,0:T(1,128)}, u32[]{:S(2)}) copy-start(s32[1,16]{1,0:T(1,128)} %count.1) | copy-start | bytes 196
  4.7 9.8 %copy-start.5 = (bf16[3,256,256]{2,1,0:T(8,128)(2,1)S(1)}, bf16[3,256,256]{2,1,0:T(8,128)(2,1)}, u32[]{:S(2)}) copy-start(bf16[3,256,256]{2,1,0:T(8,128)(2,1)} %skip_all.5) | copy-start | bytes 1179652
  4.7 9.8 %copy-start.6 = (bf16[2048,128]{1,0:T(8,128)(2,1)S(1)}, bf16[2048,128]{1,0:T(8,128)(2,1)}, u32[]{:S(2)}) copy-start(bf16[2048,128]{1,0:T(8,128)(2,1)} %rest_0_.1) | copy-start | bytes 1572868
  4.7 31.6 %all-to-all-start = ((bf16[16,2,128,128]{3,2,1,0:T(8,128)(2,1)}), bf16[16,2,128,128]{3,2,1,0:T(8,128)(2,1)S(1)}, u32[]{:S(2)}, u32[]{:S(2)}) async-start(bf16[16,2,128,128]{3,2,1,0:T(8,128)(2,1)} %bitcast.22), calls=%async_computation | async-start | bytes 2097152 | tf_op jit(solution)/shard_map/all_to_all | solution.py:363
  20.7 17.4 %copy-start.9 = (bf16[2048,128]{1,0:T(8,128)(2,1)}, bf16[2048,128]{1,0:T(8,128)(2,1)S(1)}, u32[]{:S(2)}) copy-start(bf16[2048,128]{1,0:T(8,128)(2,1)S(1)} %get-tuple-element.23.part_in) | copy-start | bytes 1572868
  36.3 1.9 copy-start.2
  38.2 29.9 %all-to-all-start.1 = ((bf16[16,2,128,128]{3,2,1,0:T(8,128)(2,1)}), bf16[16,2,128,128]{3,2,1,0:T(8,128)(2,1)}, u32[]{:S(2)}, u32[]{:S(2)}) async-start(bf16[16,2,128,128]{3,2,1,0:T(8,128)(2,1)} %bitcast.4), calls=%async_computation.1 | async-start | bytes 2097152 | tf_op jit(solution)/shard_map/all_to_all | solution.py:363
  43.2 1.0 copy-start.10
  44.2 23.9 %copy-start = (bf16[3,768,128]{2,1,0:T(8,128)(2,1)S(1)}, bf16[3,768,128]{2,1,0:T(8,128)(2,1)}, u32[]{:S(2)}) copy-start(bf16[3,768,128]{2,1,0:T(8,128)(2,1)} %mix_all.11) | copy-start | bytes 1769476
  44.2 23.9 %copy-start.11 = (f32[3,512]{1,0:T(4,128)S(1)}, f32[3,512]{1,0:T(4,128)}, u32[]{:S(2)}) copy-start(f32[3,512]{1,0:T(4,128)} %bias_all.5) | copy-start | bytes 18436
  71.9 29.8 %all-to-all-start.2 = ((bf16[16,2,128,128]{3,2,1,0:T(8,128)(2,1)}), bf16[16,2,128,128]{3,2,1,0:T(8,128)(2,1)S(1)}, u32[]{:S(2)}, u32[]{:S(2)}) async-start(bf16[16,2,128,128]{3,2,1,0:T(8,128)(2,1)} %bitcast.23), calls=%async_computation.2 | async-start | bytes 2097152 | tf_op jit(solution)/shard_map/all_to_all | solution.py:363
  84.0 19.6 %copy-start.7 = (bf16[2048,128]{1,0:T(8,128)(2,1)}, bf16[2048,128]{1,0:T(8,128)(2,1)S(1)}, u32[]{:S(2)}) copy-start(bf16[2048,128]{1,0:T(8,128)(2,1)S(1)} %get-tuple-element.28.part_in) | copy-start | bytes 1572868
  101.7 1.9 copy-start.3
  103.6 29.9 %all-to-all-start.3 = ((bf16[16,2,128,128]{3,2,1,0:T(8,128)(2,1)}), bf16[16,2,128,128]{3,2,1,0:T(8,128)(2,1)}, u32[]{:S(2)}, u32[]{:S(2)}) async-start(bf16[16,2,128,128]{3,2,1,0:T(8,128)(2,1)} %bitcast.8), calls=%async_computation.3 | async-start | bytes 2097152 | tf_op jit(solution)/shard_map/all_to_all | solution.py:363
  108.6 1.0 copy-start.8
  109.6 23.9 %copy-start.1 = (bf16[3,768,128]{2,1,0:T(8,128)(2,1)S(1)}, bf16[3,768,128]{2,1,0:T(8,128)(2,1)}, u32[]{:S(2)}) copy-start(bf16[3,768,128]{2,1,0:T(8,128)(2,1)} %mix_all.11) | copy-start | bytes 1769476
  137.3 29.8 %all-to-all-start.4 = ((bf16[16,2,128,128]{3,2,1,0:T(8,128)(2,1)}), bf16[16,2,128,128]{3,2,1,0:T(8,128)(2,1)S(1)}, u32[]{:S(2)}, u32[]{:S(2)}) async-start(bf16[16,2,128,128]{3,2,1,0:T(8,128)(2,1)} %bitcast.24), calls=%async_computation.4 | async-start | bytes 2097152 | tf_op jit(solution)/shard_map/all_to_all | solution.py:363
  167.1 1.9 copy-start.4
  169.0 29.9 %all-to-all-start.5 = ((bf16[16,2,128,128]{3,2,1,0:T(8,128)(2,1)}), bf16[16,2,128,128]{3,2,1,0:T(8,128)(2,1)}, u32[]{:S(2)}, u32[]{:S(2)}) async-start(bf16[16,2,128,128]{3,2,1,0:T(8,128)(2,1)} %bitcast.12), calls=%async_computation.5 | async-start | bytes 2097152 | tf_op jit(solution)/shard_map/all_to_all | solution.py:363
